TPU v7x, 32 devices: a whole 2x2x4 slice. The times are simulated.
32 devices in a mesh: gx: 4 (over z), gy: 4 (over y, core), gz: 2 (over x).
Axes of the slice: x: 2, y: 2, z: 4, core: 2. Of those that a mesh axis runs over, the one named last changes fastest.
Arguments:
- populations: float32 [19, 16, 32, 256], P(None, 'gx', 'gy', 'gz'), may hold values from 0.015 to 0.49, as said below
- grain_velocity: float32 [3, 1024, 128], P(None, ('gx', 'gy', 'gz')), may hold values from -1.2 to 1.2
- grain_volume: float32 [1024, 128], P(('gx', 'gy', 'gz')), may hold values from 0.05 to 0.4
- slots: int32 [1024, 128], P(('gx', 'gy', 'gz')), may hold values 0 or 1
- contacts: int32 [1024, 32], P(('gx', 'gy', 'gz')), may hold values 0 or 1
- bin_cell: int32 [1024], P(('gx', 'gy', 'gz')), may hold values from 0 to 1023
Outputs:
- fluid: float32 [19, 16, 32, 256], P(None, 'gx', 'gy', 'gz')
- grains: float32 [3, 1024, 128], P(None, ('gx', 'gy', 'gz'))
Inputs may be any that keep to these rules, and one draw needn't show every extreme that they name: `populations`: each part of the grid of one device holds distributions near w_i times a factor of order one. A bin's column lies in the cells of the same index of gz as the device that holds the bin. Of the 32 bins that one device holds, at most 8 have columns in the cells of any one device, and in every draw every holder reaches 8 for some device.
All inputs are finite; a program needn't handle non-finite values. No bound on the sum of `slots` or of `contacts` on one device may be relied on, other than what follows from the above.
Results may differ from a plain program's by a relative error of at most 0.0001.
Values sent between devices are 32-bit elements; how exact they have to be, the bound alone decides.
No kernel may reach another device: no remote copies, remote signals or barrier semaphores. Data moves between devices by JAX's collectives and lax.ppermute only.
A program may use at most 64 MiB of HBM per device.

v0:
```python
import jax
import jax.numpy as jnp
import numpy as np
from jax import lax
from jax.sharding import PartitionSpec as P

SUBSTEPS = 4


VELOCITIES = np.array(
    [
        [0, 0, 0],
        [1, 0, 0],
        [-1, 0, 0],
        [0, 1, 0],
        [0, -1, 0],
        [0, 0, 1],
        [0, 0, -1],
        [1, 1, 0],
        [-1, -1, 0],
        [1, -1, 0],
        [-1, 1, 0],
        [1, 0, 1],
        [-1, 0, -1],
        [1, 0, -1],
        [-1, 0, 1],
        [0, 1, 1],
        [0, -1, -1],
        [0, 1, -1],
        [0, -1, 1],
    ]
)
WEIGHTS = np.array([1.0 / 3.0] + [1.0 / 18.0] * 6 + [1.0 / 36.0] * 12)
OPPOSITE = [0, 2, 1, 4, 3, 6, 5, 8, 7, 10, 9, 12, 11, 14, 13, 16, 15, 18, 17]
relax_time = 0.8
contact_stiffness = 0.1
drag_factor = 2.0
gravity = 0.01


def passed_along(x, axis, by):
    length = lax.axis_size(axis)
    return lax.ppermute(x, axis, [(i, (i + by) % length) for i in range(length)])


def passed_along_2(value, axis, steps):
    count = lax.axis_size(axis)
    leading, last = (max(0, -steps), min(count, count - steps))
    return lax.ppermute(value, axis, [(source, source + steps) for source in range(leading, last)])


def moments(popul):
    density = jnp.sum(popul, axis=0)
    speed = []
    for axis in range(3):
        rising = np.array([i for i in range(19) if VELOCITIES[i, axis] == 1])
        falling = np.array([i for i in range(19) if VELOCITIES[i, axis] == -1])
        momentum = jnp.sum(popul[rising], axis=0) - jnp.sum(popul[falling], axis=0)
        speed.append(momentum / density)
    return (density, speed)


def grain_step(block, velocity, live, volume, links):
    grains = velocity.shape[2]
    bins = links.shape[1]
    groups = velocity.shape[1] // bins
    rate = drag_factor * volume * live
    drag = rate[None] * (block[:3] - velocity)
    moving = (velocity * live[None]).reshape(3, groups, bins, grains)
    pairs = links.reshape(groups, bins, bins)
    near = jnp.einsum("gkj,cgjs->cgks", pairs, moving, precision=lax.Precision.HIGHEST).reshape(
        3, -1, grains
    )
    count = jnp.einsum(
        "gkj,gjs->gks", pairs, live.reshape(groups, bins, grains), precision=lax.Precision.HIGHEST
    ).reshape(-1, grains)
    push = contact_stiffness * live[None] * (near - count[None] * velocity)
    fall = jnp.asarray([0.0, 0.0, gravity], jnp.float32).reshape(3, 1, 1) * live[None]
    updated = velocity + drag + push - fall
    forces = jnp.concatenate([-drag, (volume * live)[None]], axis=0)
    return (updated, forces)


def collide(popul, density, speed, field):
    scale = 1.0 / (1.0 + field[3])
    target = [scale * (speed[a] + relax_time * field[a] / density) for a in range(3)]
    square = target[0] * target[0] + target[1] * target[1] + target[2] * target[2]
    rows = []
    for i in range(19):
        along = jnp.zeros_like(density)
        for a in range(3):
            if VELOCITIES[i, a] != 0:
                along = along + float(VELOCITIES[i, a]) * target[a]
        equil = (
            float(WEIGHTS[i]) * density * (1.0 + 3.0 * along + 4.5 * along * along - 1.5 * square)
        )
        rows.append(popul[i] - (popul[i] - equil) / relax_time)
    return jnp.stack(rows)


def walls(moved, post):
    depth = post.shape[3]
    zpos = jnp.arange(depth)
    bottom = (zpos == 0) & (lax.axis_index("gz") == 0)
    top = (zpos == depth - 1) & (lax.axis_index("gz") == lax.axis_size("gz") - 1)
    rows = []
    for i in range(19):
        layer = moved[i]
        if VELOCITIES[i, 2] == 1:
            layer = jnp.where(bottom, post[OPPOSITE[i]], layer)
        elif VELOCITIES[i, 2] == -1:
            layer = jnp.where(top, post[OPPOSITE[i]], layer)
        rows.append(layer)
    return jnp.stack(rows)


def leaving(axis):
    rising = np.array([i for i in range(19) if VELOCITIES[i, axis] == 1])
    falling = np.array([i for i in range(19) if VELOCITIES[i, axis] == -1])
    return (rising, falling)


def stream(post):
    moved = post
    rising, falling = leaving(0)
    upper = moved[rising]
    lower = moved[falling]
    edge_up = passed_along(upper[:, -1:], "gx", 1)
    edge_down = passed_along(lower[:, :1], "gx", -1)
    moved = moved.at[rising].set(jnp.concatenate([edge_up, upper[:, :-1]], axis=1))
    moved = moved.at[falling].set(jnp.concatenate([lower[:, 1:], edge_down], axis=1))
    rising, falling = leaving(1)
    upper = moved[rising]
    lower = moved[falling]
    edge_up = passed_along(upper[:, :, -1:], "gy", 1)
    edge_down = passed_along(lower[:, :, :1], "gy", -1)
    moved = moved.at[rising].set(jnp.concatenate([edge_up, upper[:, :, :-1]], axis=2))
    moved = moved.at[falling].set(jnp.concatenate([lower[:, :, 1:], edge_down], axis=2))
    rising, falling = leaving(2)
    upper = moved[rising]
    lower = moved[falling]
    edge_up = passed_along_2(upper[:, :, :, -1:], "gz", 1)
    edge_down = passed_along_2(lower[:, :, :, :1], "gz", -1)
    moved = moved.at[rising].set(jnp.concatenate([edge_up, upper[:, :, :, :-1]], axis=3))
    moved = moved.at[falling].set(jnp.concatenate([lower[:, :, :, 1:], edge_down], axis=3))
    return walls(moved, post)


def carry_flow(outgoing):
    result = lax.all_to_all(outgoing, ("gx", "gy"), split_axis=1, concat_axis=1, tiled=True)
    return result


def carry_force(outgoing):
    result = lax.all_to_all(outgoing, ("gx", "gy"), split_axis=1, concat_axis=1, tiled=True)
    return result


def rank_within(source):
    count = source.shape[-1]
    before = jnp.arange(count)[None, :] < jnp.arange(count)[:, None]
    same = source[..., :, None] == source[..., None, :]
    return jnp.sum((same & before).astype(jnp.int32), axis=-1)


def body(populations, grain_velocity, grain_volume, slots, contacts, bin_cell):
    n_gx = lax.axis_size("gx")
    n_gy = lax.axis_size("gy")
    n_gz = lax.axis_size("gz")
    sources = n_gx * n_gy
    bins = contacts.shape[1]
    grains = grain_velocity.shape[2]
    depth_x, depth_y, depth_z = (populations.shape[1], populations.shape[2], populations.shape[3])
    zblocks = depth_z // grains
    capacity = max(2, 4 * bins // sources)
    width_y = depth_y * n_gy
    column_blocks = depth_z * n_gz // grains

    def locate(cells):
        xcell = cells // (width_y * column_blocks)
        ycell = cells // column_blocks % width_y
        zblock = cells % column_blocks
        source = xcell // depth_x * n_gy + ycell // depth_y
        local = (xcell % depth_x * depth_y + ycell % depth_y) * zblocks + zblock % zblocks
        return (source, local)

    own_source, own_local = locate(bin_cell)
    own_row = own_source * capacity + rank_within(own_source)
    every = lax.all_gather(bin_cell, ("gx", "gy"), axis=0, tiled=True).reshape(sources, bins)
    all_source, all_local = locate(every)
    all_rank = rank_within(all_source)
    here = lax.axis_index("gx") * n_gy + lax.axis_index("gy")
    slot_ids = jnp.arange(capacity, dtype=jnp.int32)
    picked = (all_source == here)[:, None, :] & (all_rank[:, None, :] == slot_ids[None, :, None])
    send_column = jnp.sum(jnp.where(picked, all_local[:, None, :], 0), axis=2).reshape(-1)
    send_mask = jnp.any(picked, axis=2).reshape(-1).astype(jnp.float32)
    live = slots.astype(jnp.float32)
    links = contacts.astype(jnp.float32)
    fluid = populations
    velocity = grain_velocity
    for step in range(SUBSTEPS):
        density, speed = moments(fluid)
        flow = jnp.stack(speed + [density]).reshape(4, -1, grains)
        outgoing = jnp.take(flow, send_column, axis=1) * send_mask[None, :, None]
        incoming = carry_flow(outgoing)
        block = jnp.take(incoming, own_row, axis=1)
        velocity, forces = grain_step(block, velocity, live, grain_volume, links)
        back = jnp.zeros((4, sources * capacity, grains), jnp.float32).at[:, own_row].set(forces)
        returned = carry_force(back)
        field = jnp.zeros_like(flow).at[:, send_column].add(returned * send_mask[None, :, None])
        field = field.reshape(4, depth_x, depth_y, depth_z)
        post = collide(fluid, density, speed, field)
        fluid = stream(post)
    return (fluid, velocity)


def solution(mesh):
    placed = (
        P(None, "gx", "gy", "gz"),
        P(None, ("gx", "gy", "gz"), None),
        P(("gx", "gy", "gz"), None),
        P(("gx", "gy", "gz"), None),
        P(("gx", "gy", "gz"), None),
        P(("gx", "gy", "gz")),
    )
    return jax.shard_map(
        body,
        mesh=mesh,
        in_specs=placed,
        out_specs=(P(None, "gx", "gy", "gz"), P(None, ("gx", "gy", "gz"), None)),
        check_vma=False,
    )
```

profile of v0, /device:TPU:0, one launch (start us, length us, event | category | flops | bytes accessed | tf_op | source)
XLA Modules:
  0.0 286.1 jit_solution(9873769758458916731)
XLA Ops:
  2.5 0.9 dynamic-update-slice
  3.4 13.8 %all-reduce = s32[512]{0:T(512)S(1)} all-reduce(s32[512]{0:T(512)S(1)} %dynamic-update-slice), channel_id=1, replica_groups=mesh['gx'=4,'gy'=4,'gz'=2] {'gx','gy'}, use_global_device_ids=true, to_apply=%add | all-reduce | flops 512 | bytes 4096
  18.6 1.0 reduce_sum.52978
  23.6 0.7 gather_fusion.48
  24.4 1.0 bitcast_multiply_fusion.3
  25.4 3.7 %all-to-all-start = ((f32[4,128,128]{2,0,1:T(4,128)}), f32[4,128,128]{2,0,1:T(4,128)S(1)}, u32[]{:S(2)}, u32[]{:S(2)}) async-start(f32[4,128,128]{2,0,1:T(4,128)} %bitcast_multiply_fusion.3), calls=%async_computation | async-start | bytes 524288 | tf_op jit(solution)/shard_map/all_to_all | solution.py:150
  29.4 9.7 %all-to-all-done = f32[4,128,128]{2,0,1:T(4,128)S(1)} async-done(((f32[4,128,128]{2,0,1:T(4,128)}), f32[4,128,128]{2,0,1:T(4,128)S(1)}, u32[]{:S(2)}, u32[]{:S(2)}) %all-to-all-start) | async-done | bytes 262176 | tf_op jit(solution)/shard_map/all_to_all | solution.py:150
  41.3 3.7 %scatter_fusion = f32[4,128,128]{2,0,1:T(4,128)} fusion(f32[4,128,128]{2,0,1:T(4,128)} %broadcast.681055.clone, s32[32]{0:T(128)S(1)} %get-tuple-element.171, f32[32,4,128]{2,1,0:T(4,128)S(1)} %copy.157), kind=kCustom, calls=%fused_computation.56 | custom fusion | bytes 196736 | tf_op jit(solution)/shard_map/scatter | solution.py:208
  45.1 3.5 %all-to-all-start.1 = ((f32[4,128,128]{2,0,1:T(4,128)}), f32[4,128,128]{2,0,1:T(4,128)S(1)}, u32[]{:S(2)}, u32[]{:S(2)}) async-start(f32[4,128,128]{2,0,1:T(4,128)} %scatter_fusion), calls=%async_computation.1 | async-start | bytes 524288 | tf_op jit(solution)/shard_map/all_to_all | solution.py:155
  48.7 9.9 %all-to-all-done.1 = f32[4,128,128]{2,0,1:T(4,128)S(1)} async-done(((f32[4,128,128]{2,0,1:T(4,128)}), f32[4,128,128]{2,0,1:T(4,128)S(1)}, u32[]{:S(2)}, u32[]{:S(2)}) %all-to-all-start.1) | async-done | bytes 262176 | tf_op jit(solution)/shard_map/all_to_all | solution.py:155
  58.8 5.2 %scatter_fusion.1 = f32[4,32,128]{2,0,1:T(4,128)S(1)} fusion(f32[4,32,128]{2,0,1:T(4,128)S(1)} %broadcast.681051.clone, s32[128]{0:T(128)S(1)} %fusion.467, f32[128,4,128]{2,1,0:T(4,128)S(1)} %multiply_bitcast_fusion.3), kind=kCustom, calls=%fused_computation.57 | custom fusion | flops 65536 | bytes 786944 | tf_op jit(solution)/shard_map/scatter-add | solution.py:210
  66.4 3.8 %collective-permute-start.1 = (f32[5,1,8,128]{3,2,1,0:T(8,128)S(1)}, f32[5,1,8,128]{3,2,1,0:T(8,128)S(1)}, u32[]{:S(2)}, u32[]{:S(2)}) collective-permute-start(f32[5,1,8,128]{3,2,1,0:T(8,128)S(1)} %slice.812), channel_id=1, source_target_pairs={{0,24},{8,0},{16,8},{24,16},{1,25},{9,1},{17,9},{25,17},{2,26},{10... | collective-permute-start | bytes 61448 | tf_op jit(solution)/shard_map/ppermute | solution.py:43
  73.7 1.8 collective-permute-start.3
  78.3 3.4 %collective-permute-start.4 = (f32[5,4,8,1]{3,2,1,0:T(8,128)S(1)}, f32[5,4,8,1]{3,2,1,0:T(8,128)S(1)}, u32[]{:S(2)}, u32[]{:S(2)}) collective-permute-start(f32[5,4,8,1]{3,2,1,0:T(8,128)S(1)} %slice.817), channel_id=1, source_target_pairs={{0,1},{2,3},{4,5},{6,7},{8,9},{10,11},{12,13},{14,15},{16,17},{18,... | collective-permute-start | bytes 1928 | tf_op jit(solution)/shard_map/ppermute | solution.py:49
  82.4 1.3 collective-permute-start.5
  84.5 4.2 %collective-permute-done.5 = f32[5,4,8,1]{3,2,1,0:T(8,128)S(1)} collective-permute-done((f32[5,4,8,1]{3,2,1,0:T(8,128)S(1)}, f32[5,4,8,1]{3,2,1,0:T(8,128)S(1)}, u32[]{:S(2)}, u32[]{:S(2)}) %collective-permute-start.5) | collective-permute-done | bytes 672 | tf_op jit(solution)/shard_map/ppermute | solution.py:49
  93.3 0.7 gather_fusion.50
  94.1 1.0 bitcast_multiply_fusion.2
  95.1 5.5 %all-to-all-start.2 = ((f32[4,128,128]{2,0,1:T(4,128)}), f32[4,128,128]{2,0,1:T(4,128)S(1)}, u32[]{:S(2)}, u32[]{:S(2)}) async-start(f32[4,128,128]{2,0,1:T(4,128)} %bitcast_multiply_fusion.2), calls=%async_computation.2 | async-start | bytes 524288 | tf_op jit(solution)/shard_map/all_to_all | solution.py:150
  101.4 9.2 %all-to-all-done.2 = f32[4,128,128]{2,0,1:T(4,128)S(1)} async-done(((f32[4,128,128]{2,0,1:T(4,128)}), f32[4,128,128]{2,0,1:T(4,128)S(1)}, u32[]{:S(2)}, u32[]{:S(2)}) %all-to-all-start.2) | async-done | bytes 262176 | tf_op jit(solution)/shard_map/all_to_all | solution.py:150
  112.3 1.5 scatter_fusion.8
  113.8 12.7 %all_to_all.40 = f32[4,128,128]{2,0,1:T(4,128)S(1)} all-to-all(f32[4,128,128]{2,0,1:T(4,128)S(1)} %scatter_fusion.8), channel_id=1, replica_groups=mesh['gx'=4,'gy'=4,'gz'=2] {'gx','gy'}, dimensions={1} | all-to-all | bytes 524288 | tf_op jit(solution)/shard_map/all_to_all | solution.py:155
  126.7 5.2 %scatter_fusion.9 = f32[4,32,128]{2,0,1:T(4,128)S(1)} fusion(f32[4,32,128]{2,0,1:T(4,128)S(1)} %broadcast.681051.clone.1, s32[128]{0:T(128)S(1)} %fusion.467, f32[128,4,128]{2,1,0:T(4,128)S(1)} %multiply_bitcast_fusion.2), kind=kCustom, calls=%fused_computation.65 | custom fusion | flops 65536 | bytes 786944 | tf_op jit(solution)/shard_map/scatter-add | solution.py:210
  134.2 3.9 %collective-permute-start.7 = (f32[5,1,8,128]{3,2,1,0:T(8,128)S(1)}, f32[5,1,8,128]{3,2,1,0:T(8,128)S(1)}, u32[]{:S(2)}, u32[]{:S(2)}) collective-permute-start(f32[5,1,8,128]{3,2,1,0:T(8,128)S(1)} %slice.850), channel_id=1, source_target_pairs={{0,24},{8,0},{16,8},{24,16},{1,25},{9,1},{17,9},{25,17},{2,26},{10... | collective-permute-start | bytes 61448 | tf_op jit(solution)/shard_map/ppermute | solution.py:43
  141.6 1.8 collective-permute-start.9
  146.2 1.6 collective-permute-start.10
  148.4 1.5 collective-permute-start.11
  150.7 4.0 %collective-permute-done.11 = f32[5,4,8,1]{3,2,1,0:T(8,128)S(1)} collective-permute-done((f32[5,4,8,1]{3,2,1,0:T(8,128)S(1)}, f32[5,4,8,1]{3,2,1,0:T(8,128)S(1)}, u32[]{:S(2)}, u32[]{:S(2)}) %collective-permute-start.11) | collective-permute-done | bytes 672 | tf_op jit(solution)/shard_map/ppermute | solution.py:49
  159.4 0.7 gather_fusion.52
  160.4 15.3 %all_to_all.41 = f32[4,128,128]{2,0,1:T(4,128)S(1)} all-to-all(f32[4,128,128]{2,0,1:T(4,128)S(1)} %bitcast_multiply_fusion.1), channel_id=1, replica_groups=mesh['gx'=4,'gy'=4,'gz'=2] {'gx','gy'}, dimensions={1} | all-to-all | bytes 524288 | tf_op jit(solution)/shard_map/all_to_all | solution.py:150
  176.7 1.5 scatter_fusion.16
  178.2 12.7 %all_to_all.42 = f32[4,128,128]{2,0,1:T(4,128)S(1)} all-to-all(f32[4,128,128]{2,0,1:T(4,128)S(1)} %scatter_fusion.16), channel_id=1, replica_groups=mesh['gx'=4,'gy'=4,'gz'=2] {'gx','gy'}, dimensions={1} | all-to-all | bytes 524288 | tf_op jit(solution)/shard_map/all_to_all | solution.py:155
  191.1 5.2 %scatter_fusion.17 = f32[4,32,128]{2,0,1:T(4,128)S(1)} fusion(f32[4,32,128]{2,0,1:T(4,128)S(1)} %broadcast.681051.clone.2, s32[128]{0:T(128)S(1)} %fusion.467, f32[128,4,128]{2,1,0:T(4,128)S(1)} %multiply_bitcast_fusion.1), kind=kCustom, calls=%fused_computation.73 | custom fusion | flops 65536 | bytes 786944 | tf_op jit(solution)/shard_map/scatter-add | solution.py:210
  198.7 3.8 %collective-permute-start.13 = (f32[5,1,8,128]{3,2,1,0:T(8,128)S(1)}, f32[5,1,8,128]{3,2,1,0:T(8,128)S(1)}, u32[]{:S(2)}, u32[]{:S(2)}) collective-permute-start(f32[5,1,8,128]{3,2,1,0:T(8,128)S(1)} %slice.888), channel_id=1, source_target_pairs={{0,24},{8,0},{16,8},{24,16},{1,25},{9,1},{17,9},{25,17},{2,26},{10... | collective-permute-start | bytes 61448 | tf_op jit(solution)/shard_map/ppermute | solution.py:43
  206.0 1.8 collective-permute-start.15
  210.6 1.6 collective-permute-start.16
  212.8 1.3 collective-permute-start.17
  215.0 4.1 %collective-permute-done.17 = f32[5,4,8,1]{3,2,1,0:T(8,128)S(1)} collective-permute-done((f32[5,4,8,1]{3,2,1,0:T(8,128)S(1)}, f32[5,4,8,1]{3,2,1,0:T(8,128)S(1)}, u32[]{:S(2)}, u32[]{:S(2)}) %collective-permute-start.17) | collective-permute-done | bytes 672 | tf_op jit(solution)/shard_map/ppermute | solution.py:49
  224.9 15.3 %all_to_all.43 = f32[4,128,128]{2,0,1:T(4,128)S(1)} all-to-all(f32[4,128,128]{2,0,1:T(4,128)S(1)} %bitcast_multiply_fusion), channel_id=1, replica_groups=mesh['gx'=4,'gy'=4,'gz'=2] {'gx','gy'}, dimensions={1} | all-to-all | bytes 524288 | tf_op jit(solution)/shard_map/all_to_all | solution.py:150
  241.2 1.5 scatter_fusion.24
  242.7 12.7 %all_to_all.44 = f32[4,128,128]{2,0,1:T(4,128)S(1)} all-to-all(f32[4,128,128]{2,0,1:T(4,128)S(1)} %scatter_fusion.24), channel_id=1, replica_groups=mesh['gx'=4,'gy'=4,'gz'=2] {'gx','gy'}, dimensions={1} | all-to-all | bytes 524288 | tf_op jit(solution)/shard_map/all_to_all | solution.py:155
  255.6 5.2 %scatter_fusion.25 = f32[4,32,128]{2,0,1:T(4,128)S(1)} fusion(f32[4,32,128]{2,0,1:T(4,128)S(1)} %broadcast.681051, s32[128]{0:T(128)S(1)} %fusion.467, f32[128,4,128]{2,1,0:T(4,128)S(1)} %multiply_bitcast_fusion), kind=kCustom, calls=%fused_computation.81 | custom fusion | flops 65536 | bytes 786944 | tf_op jit(solution)/shard_map/scatter-add | solution.py:210
  263.2 3.8 %collective-permute-start.19 = (f32[5,1,8,128]{3,2,1,0:T(8,128)S(1)}, f32[5,1,8,128]{3,2,1,0:T(8,128)S(1)}, u32[]{:S(2)}, u32[]{:S(2)}) collective-permute-start(f32[5,1,8,128]{3,2,1,0:T(8,128)S(1)} %slice.926), channel_id=1, source_target_pairs={{0,24},{8,0},{16,8},{24,16},{1,25},{9,1},{17,9},{25,17},{2,26},{10... | collective-permute-start | bytes 61448 | tf_op jit(solution)/shard_map/ppermute | solution.py:43
  270.4 1.8 collective-permute-start.21
  275.1 1.6 collective-permute-start.22
  276.6 0.8 fusion.3
  278.1 1.3 collective-permute-start.23
  280.2 4.2 %collective-permute-done.23 = f32[5,4,8,1]{3,2,1,0:T(8,128)S(1)} collective-permute-done((f32[5,4,8,1]{3,2,1,0:T(8,128)S(1)}, f32[5,4,8,1]{3,2,1,0:T(8,128)S(1)}, u32[]{:S(2)}, u32[]{:S(2)}) %collective-permute-start.23) | collective-permute-done | bytes 672 | tf_op jit(solution)/shard_map/ppermute | solution.py:49
  (432 shorter events, 69.8 us)
Async XLA Ops:
  0.6 0.7 copy-start.18
  0.6 19.0 %copy-start = (f32[19,4,8,128]{3,2,1,0:T(8,128)S(1)}, f32[19,4,8,128]{3,2,1,0:T(8,128)}, u32[]{:S(2)}) copy-start(f32[19,4,8,128]{3,2,1,0:T(8,128)} %param.134) | copy-start | bytes 933892
  18.6 1.0 copy-start.14
  18.6 1.0 copy-start.15
  20.2 0.7 copy-start.10
  20.2 0.7 copy-start.11
  21.5 0.7 copy-start.12
  21.5 0.7 copy-start.13
  25.4 3.7 %copy-start.17 = (s32[32]{0:T(128)S(1)}, s32[32]{0:T(128)}, u32[]{:S(2)}) copy-start(s32[32]{0:T(128)} %param.139) | copy-start | bytes 388
  25.4 3.9 %copy-start.7 = (s32[32,128]{1,0:T(8,128)S(1)}, s32[32,128]{1,0:T(8,128)}, u32[]{:S(2)}) copy-start(s32[32,128]{1,0:T(8,128)} %param.137) | copy-start | bytes 49156
  25.4 4.0 %copy-start.9 = (f32[32,128]{1,0:T(8,128)S(1)}, f32[32,128]{1,0:T(8,128)}, u32[]{:S(2)}) copy-start(f32[32,128]{1,0:T(8,128)} %param.136) | copy-start | bytes 49156
  25.4 13.7 %all-to-all-start = ((f32[4,128,128]{2,0,1:T(4,128)}), f32[4,128,128]{2,0,1:T(4,128)S(1)}, u32[]{:S(2)}, u32[]{:S(2)}) async-start(f32[4,128,128]{2,0,1:T(4,128)} %bitcast_multiply_fusion.3), calls=%async_computation | async-start | bytes 524288 | tf_op jit(solution)/shard_map/all_to_all | solution.py:150
  39.7 0.8 copy-start.6
  45.1 13.5 %all-to-all-start.1 = ((f32[4,128,128]{2,0,1:T(4,128)}), f32[4,128,128]{2,0,1:T(4,128)S(1)}, u32[]{:S(2)}, u32[]{:S(2)}) async-start(f32[4,128,128]{2,0,1:T(4,128)} %scatter_fusion), calls=%async_computation.1 | async-start | bytes 524288 | tf_op jit(solution)/shard_map/all_to_all | solution.py:155
  65.1 5.7 %collective-permute-start = (f32[5,1,8,128]{3,2,1,0:T(8,128)S(1)}, f32[5,1,8,128]{3,2,1,0:T(8,128)S(1)}, u32[]{:S(2)}, u32[]{:S(2)}) collective-permute-start(f32[5,1,8,128]{3,2,1,0:T(8,128)S(1)} %slice.809), channel_id=1, source_target_pairs={{0,8},{8,16},{16,24},{24,0},{1,9},{9,17},{17,25},{25,1},{2,10},{10... | collective-permute-start | bytes 61448 | tf_op jit(solution)/shard_map/ppermute | solution.py:43
  65.7 0.6 copy-start.3
  66.4 5.3 %collective-permute-start.1 = (f32[5,1,8,128]{3,2,1,0:T(8,128)S(1)}, f32[5,1,8,128]{3,2,1,0:T(8,128)S(1)}, u32[]{:S(2)}, u32[]{:S(2)}) collective-permute-start(f32[5,1,8,128]{3,2,1,0:T(8,128)S(1)} %slice.812), channel_id=1, source_target_pairs={{0,24},{8,0},{16,8},{24,16},{1,25},{9,1},{17,9},{25,17},{2,26},{10... | collective-permute-start | bytes 61448 | tf_op jit(solution)/shard_map/ppermute | solution.py:43
  70.9 0.8 slice-start.1
  73.0 3.2 %collective-permute-start.2 = (f32[5,4,1,128]{3,2,1,0:T(1,128)S(1)}, f32[5,4,1,128]{3,2,1,0:T(1,128)S(1)}, u32[]{:S(2)}, u32[]{:S(2)}) collective-permute-start(f32[5,4,1,128]{3,2,1,0:T(1,128)S(1)} %slice.813), channel_id=1, source_target_pairs={{0,2},{2,4},{4,6},{6,0},{1,3},{3,5},{5,7},{7,1},{8,10},{10,12},{12... | collective-permute-start | bytes 30728 | tf_op jit(solution)/shard_map/ppermute | solution.py:43
  73.7 3.2 %collective-permute-start.3 = (f32[5,4,1,128]{3,2,1,0:T(1,128)S(1)}, f32[5,4,1,128]{3,2,1,0:T(1,128)S(1)}, u32[]{:S(2)}, u32[]{:S(2)}) collective-permute-start(f32[5,4,1,128]{3,2,1,0:T(1,128)S(1)} %slice.816), channel_id=1, source_target_pairs={{0,6},{2,0},{4,2},{6,4},{1,7},{3,1},{5,3},{7,5},{8,14},{10,8},{12,... | collective-permute-start | bytes 30728 | tf_op jit(solution)/shard_map/ppermute | solution.py:43
  78.3 5.4 %collective-permute-start.4 = (f32[5,4,8,1]{3,2,1,0:T(8,128)S(1)}, f32[5,4,8,1]{3,2,1,0:T(8,128)S(1)}, u32[]{:S(2)}, u32[]{:S(2)}) collective-permute-start(f32[5,4,8,1]{3,2,1,0:T(8,128)S(1)} %slice.817), channel_id=1, source_target_pairs={{0,1},{2,3},{4,5},{6,7},{8,9},{10,11},{12,13},{14,15},{16,17},{18,... | collective-permute-start | bytes 1928 | tf_op jit(solution)/shard_map/ppermute | solution.py:49
  82.4 6.3 %collective-permute-start.5 = (f32[5,4,8,1]{3,2,1,0:T(8,128)S(1)}, f32[5,4,8,1]{3,2,1,0:T(8,128)S(1)}, u32[]{:S(2)}, u32[]{:S(2)}) collective-permute-start(f32[5,4,8,1]{3,2,1,0:T(8,128)S(1)} %bitcast.389), channel_id=1, source_target_pairs={{1,0},{3,2},{5,4},{7,6},{9,8},{11,10},{13,12},{15,14},{17,16},{19,... | collective-permute-start | bytes 1928 | tf_op jit(solution)/shard_map/ppermute | solution.py:49
  95.1 15.5 %all-to-all-start.2 = ((f32[4,128,128]{2,0,1:T(4,128)}), f32[4,128,128]{2,0,1:T(4,128)S(1)}, u32[]{:S(2)}, u32[]{:S(2)}) async-start(f32[4,128,128]{2,0,1:T(4,128)} %bitcast_multiply_fusion.2), calls=%async_computation.2 | async-start | bytes 524288 | tf_op jit(solution)/shard_map/all_to_all | solution.py:150
  100.6 0.7 copy-start.1
  111.3 0.7 copy-start.16
  133.0 5.7 %collective-permute-start.6 = (f32[5,1,8,128]{3,2,1,0:T(8,128)S(1)}, f32[5,1,8,128]{3,2,1,0:T(8,128)S(1)}, u32[]{:S(2)}, u32[]{:S(2)}) collective-permute-start(f32[5,1,8,128]{3,2,1,0:T(8,128)S(1)} %slice.847), channel_id=1, source_target_pairs={{0,8},{8,16},{16,24},{24,0},{1,9},{9,17},{17,25},{25,1},{2,10},{10... | collective-permute-start | bytes 61448 | tf_op jit(solution)/shard_map/ppermute | solution.py:43
  133.6 0.6 copy-start.4
  134.2 5.3 %collective-permute-start.7 = (f32[5,1,8,128]{3,2,1,0:T(8,128)S(1)}, f32[5,1,8,128]{3,2,1,0:T(8,128)S(1)}, u32[]{:S(2)}, u32[]{:S(2)}) collective-permute-start(f32[5,1,8,128]{3,2,1,0:T(8,128)S(1)} %slice.850), channel_id=1, source_target_pairs={{0,24},{8,0},{16,8},{24,16},{1,25},{9,1},{17,9},{25,17},{2,26},{10... | collective-permute-start | bytes 61448 | tf_op jit(solution)/shard_map/ppermute | solution.py:43
  138.6 1.0 slice-start.2
  140.9 3.2 %collective-permute-start.8 = (f32[5,4,1,128]{3,2,1,0:T(1,128)S(1)}, f32[5,4,1,128]{3,2,1,0:T(1,128)S(1)}, u32[]{:S(2)}, u32[]{:S(2)}) collective-permute-start(f32[5,4,1,128]{3,2,1,0:T(1,128)S(1)} %slice.851), channel_id=1, source_target_pairs={{0,2},{2,4},{4,6},{6,0},{1,3},{3,5},{5,7},{7,1},{8,10},{10,12},{12... | collective-permute-start | bytes 30728 | tf_op jit(solution)/shard_map/ppermute | solution.py:43
  141.6 3.2 %collective-permute-start.9 = (f32[5,4,1,128]{3,2,1,0:T(1,128)S(1)}, f32[5,4,1,128]{3,2,1,0:T(1,128)S(1)}, u32[]{:S(2)}, u32[]{:S(2)}) collective-permute-start(f32[5,4,1,128]{3,2,1,0:T(1,128)S(1)} %slice.854), channel_id=1, source_target_pairs={{0,6},{2,0},{4,2},{6,4},{1,7},{3,1},{5,3},{7,5},{8,14},{10,8},{12,... | collective-permute-start | bytes 30728 | tf_op jit(solution)/shard_map/ppermute | solution.py:43
  146.2 3.7 %collective-permute-start.10 = (f32[5,4,8,1]{3,2,1,0:T(8,128)S(1)}, f32[5,4,8,1]{3,2,1,0:T(8,128)S(1)}, u32[]{:S(2)}, u32[]{:S(2)}) collective-permute-start(f32[5,4,8,1]{3,2,1,0:T(8,128)S(1)} %slice.855), channel_id=1, source_target_pairs={{0,1},{2,3},{4,5},{6,7},{8,9},{10,11},{12,13},{14,15},{16,17},{18,... | collective-permute-start | bytes 1928 | tf_op jit(solution)/shard_map/ppermute | solution.py:49
  148.4 6.3 %collective-permute-start.11 = (f32[5,4,8,1]{3,2,1,0:T(8,128)S(1)}, f32[5,4,8,1]{3,2,1,0:T(8,128)S(1)}, u32[]{:S(2)}, u32[]{:S(2)}) collective-permute-start(f32[5,4,8,1]{3,2,1,0:T(8,128)S(1)} %bitcast.390), channel_id=1, source_target_pairs={{1,0},{3,2},{5,4},{7,6},{9,8},{11,10},{13,12},{15,14},{17,16},{19,... | collective-permute-start | bytes 1928 | tf_op jit(solution)/shard_map/ppermute | solution.py:49
  197.5 5.7 %collective-permute-start.12 = (f32[5,1,8,128]{3,2,1,0:T(8,128)S(1)}, f32[5,1,8,128]{3,2,1,0:T(8,128)S(1)}, u32[]{:S(2)}, u32[]{:S(2)}) collective-permute-start(f32[5,1,8,128]{3,2,1,0:T(8,128)S(1)} %slice.885), channel_id=1, source_target_pairs={{0,8},{8,16},{16,24},{24,0},{1,9},{9,17},{17,25},{25,1},{2,10},{10... | collective-permute-start | bytes 61448 | tf_op jit(solution)/shard_map/ppermute | solution.py:43
  198.7 5.3 %collective-permute-start.13 = (f32[5,1,8,128]{3,2,1,0:T(8,128)S(1)}, f32[5,1,8,128]{3,2,1,0:T(8,128)S(1)}, u32[]{:S(2)}, u32[]{:S(2)}) collective-permute-start(f32[5,1,8,128]{3,2,1,0:T(8,128)S(1)} %slice.888), channel_id=1, source_target_pairs={{0,24},{8,0},{16,8},{24,16},{1,25},{9,1},{17,9},{25,17},{2,26},{10... | collective-permute-start | bytes 61448 | tf_op jit(solution)/shard_map/ppermute | solution.py:43
  203.2 0.8 slice-start.3
  205.3 3.2 %collective-permute-start.14 = (f32[5,4,1,128]{3,2,1,0:T(1,128)S(1)}, f32[5,4,1,128]{3,2,1,0:T(1,128)S(1)}, u32[]{:S(2)}, u32[]{:S(2)}) collective-permute-start(f32[5,4,1,128]{3,2,1,0:T(1,128)S(1)} %slice.889), channel_id=1, source_target_pairs={{0,2},{2,4},{4,6},{6,0},{1,3},{3,5},{5,7},{7,1},{8,10},{10,12},{12... | collective-permute-start | bytes 30728 | tf_op jit(solution)/shard_map/ppermute | solution.py:43
  206.0 3.2 %collective-permute-start.15 = (f32[5,4,1,128]{3,2,1,0:T(1,128)S(1)}, f32[5,4,1,128]{3,2,1,0:T(1,128)S(1)}, u32[]{:S(2)}, u32[]{:S(2)}) collective-permute-start(f32[5,4,1,128]{3,2,1,0:T(1,128)S(1)} %slice.892), channel_id=1, source_target_pairs={{0,6},{2,0},{4,2},{6,4},{1,7},{3,1},{5,3},{7,5},{8,14},{10,8},{12,... | collective-permute-start | bytes 30728 | tf_op jit(solution)/shard_map/ppermute | solution.py:43
  210.6 3.6 %collective-permute-start.16 = (f32[5,4,8,1]{3,2,1,0:T(8,128)S(1)}, f32[5,4,8,1]{3,2,1,0:T(8,128)S(1)}, u32[]{:S(2)}, u32[]{:S(2)}) collective-permute-start(f32[5,4,8,1]{3,2,1,0:T(8,128)S(1)} %slice.893), channel_id=1, source_target_pairs={{0,1},{2,3},{4,5},{6,7},{8,9},{10,11},{12,13},{14,15},{16,17},{18,... | collective-permute-start | bytes 1928 | tf_op jit(solution)/shard_map/ppermute | solution.py:49
  212.8 6.3 %collective-permute-start.17 = (f32[5,4,8,1]{3,2,1,0:T(8,128)S(1)}, f32[5,4,8,1]{3,2,1,0:T(8,128)S(1)}, u32[]{:S(2)}, u32[]{:S(2)}) collective-permute-start(f32[5,4,8,1]{3,2,1,0:T(8,128)S(1)} %bitcast.391), channel_id=1, source_target_pairs={{1,0},{3,2},{5,4},{7,6},{9,8},{11,10},{13,12},{15,14},{17,16},{19,... | collective-permute-start | bytes 1928 | tf_op jit(solution)/shard_map/ppermute | solution.py:49
  261.9 5.7 %collective-permute-start.18 = (f32[5,1,8,128]{3,2,1,0:T(8,128)S(1)}, f32[5,1,8,128]{3,2,1,0:T(8,128)S(1)}, u32[]{:S(2)}, u32[]{:S(2)}) collective-permute-start(f32[5,1,8,128]{3,2,1,0:T(8,128)S(1)} %slice.923), channel_id=1, source_target_pairs={{0,8},{8,16},{16,24},{24,0},{1,9},{9,17},{17,25},{25,1},{2,10},{10... | collective-permute-start | bytes 61448 | tf_op jit(solution)/shard_map/ppermute | solution.py:43
  263.2 5.3 %collective-permute-start.19 = (f32[5,1,8,128]{3,2,1,0:T(8,128)S(1)}, f32[5,1,8,128]{3,2,1,0:T(8,128)S(1)}, u32[]{:S(2)}, u32[]{:S(2)}) collective-permute-start(f32[5,1,8,128]{3,2,1,0:T(8,128)S(1)} %slice.926), channel_id=1, source_target_pairs={{0,24},{8,0},{16,8},{24,16},{1,25},{9,1},{17,9},{25,17},{2,26},{10... | collective-permute-start | bytes 61448 | tf_op jit(solution)/shard_map/ppermute | solution.py:43
  267.6 0.8 slice-start
  269.8 3.2 %collective-permute-start.20 = (f32[5,4,1,128]{3,2,1,0:T(1,128)S(1)}, f32[5,4,1,128]{3,2,1,0:T(1,128)S(1)}, u32[]{:S(2)}, u32[]{:S(2)}) collective-permute-start(f32[5,4,1,128]{3,2,1,0:T(1,128)S(1)} %slice.927), channel_id=1, source_target_pairs={{0,2},{2,4},{4,6},{6,0},{1,3},{3,5},{5,7},{7,1},{8,10},{10,12},{12... | collective-permute-start | bytes 30728 | tf_op jit(solution)/shard_map/ppermute | solution.py:43
  270.4 3.2 %collective-permute-start.21 = (f32[5,4,1,128]{3,2,1,0:T(1,128)S(1)}, f32[5,4,1,128]{3,2,1,0:T(1,128)S(1)}, u32[]{:S(2)}, u32[]{:S(2)}) collective-permute-start(f32[5,4,1,128]{3,2,1,0:T(1,128)S(1)} %slice.930), channel_id=1, source_target_pairs={{0,6},{2,0},{4,2},{6,4},{1,7},{3,1},{5,3},{7,5},{8,14},{10,8},{12,... | collective-permute-start | bytes 30728 | tf_op jit(solution)/shard_map/ppermute | solution.py:43
  275.1 4.3 %collective-permute-start.22 = (f32[5,4,8,1]{3,2,1,0:T(8,128)S(1)}, f32[5,4,8,1]{3,2,1,0:T(8,128)S(1)}, u32[]{:S(2)}, u32[]{:S(2)}) collective-permute-start(f32[5,4,8,1]{3,2,1,0:T(8,128)S(1)} %slice.931), channel_id=1, source_target_pairs={{0,1},{2,3},{4,5},{6,7},{8,9},{10,11},{12,13},{14,15},{16,17},{18,... | collective-permute-start | bytes 1928 | tf_op jit(solution)/shard_map/ppermute | solution.py:49
  278.1 6.3 %collective-permute-start.23 = (f32[5,4,8,1]{3,2,1,0:T(8,128)S(1)}, f32[5,4,8,1]{3,2,1,0:T(8,128)S(1)}, u32[]{:S(2)}, u32[]{:S(2)}) collective-permute-start(f32[5,4,8,1]{3,2,1,0:T(8,128)S(1)} %bitcast.388), channel_id=1, source_target_pairs={{1,0},{3,2},{5,4},{7,6},{9,8},{11,10},{13,12},{15,14},{17,16},{19,... | collective-permute-start | bytes 1928 | tf_op jit(solution)/shard_map/ppermute | solution.py:49
  285.4 0.7 copy-start.8
  (2 other events, 1.3 us)
where the time goes:
time: 287 us; the launch traced here: 286 us
  blocking collectives  82.4 us (29%)
  local copies, waits for them, and re-layouts  67 us (23%)
  waiting for transfers between devices  51.2 us (18%)
  starting transfers between devices  49 us (17%)
  other arithmetic  30.8 us (11%)
  between operations  4.16 us (1%)
    all_to_all x3, blocking collectives, carry_force(): lax.all_to_all(outgoing, ('gx', 'gy'), split_axis=1, concat_axis=1, tiled...  38.1 us
    all_to_all x2, blocking collectives, carry_flow(): lax.all_to_all(outgoing, ('gx', 'gy'), split_axis=1, concat_axis=1, tiled...  30.6 us
    ppermute x16, starting transfers between devices, passed_along(): lax.ppermute(x, axis, [(i, (i + by) % length) for i in range(length)])  22.9 us
    scatter-add x4, other arithmetic, body(): jnp.zeros_like(flow).at[:, send_column]  20.8 us
    all_to_all x2, waiting for transfers between devices, carry_flow(): lax.all_to_all(outgoing, ('gx', 'gy'), split_axis=1, concat_axis=1, tiled...  18.8 us
    ppermute x8, waiting for transfers between devices, passed_along_2(): lax.ppermute(value, axis, [(source, source + steps) for source in range(l...  16.7 us
    unnamed x1, blocking collectives  13.8 us
    ppermute x8, starting transfers between devices, passed_along_2(): lax.ppermute(value, axis, [(source, source + steps) for source in range(l...  13.4 us
  transfers between devices with their start and end apart: 27, of which 21 were waited for; matrix products, arithmetic and copies ran while one was open for 6% of the time, Pallas kernels for 0%

commit v1 on v0

--- a/solution.py
+++ b/solution.py
@@ -2,6 +2,8 @@
 import jax.numpy as jnp
 import numpy as np
 from jax import lax
+from jax.experimental import pallas as pl
+from jax.experimental.pallas import tpu as pltpu
 from jax.sharding import PartitionSpec as P
 
 SUBSTEPS = 4
@@ -163,7 +165,7 @@
     return jnp.sum((same & before).astype(jnp.int32), axis=-1)
 
 
-def body(populations, grain_velocity, grain_volume, slots, contacts, bin_cell):
+def columns_body(populations, grain_velocity, grain_volume, slots, contacts, bin_cell):
     n_gx = lax.axis_size("gx")
     n_gy = lax.axis_size("gy")
     n_gz = lax.axis_size("gz")
@@ -214,6 +216,406 @@
     return (fluid, velocity)
 
 
+LANES = 128
+SUBLANES = 8
+VMEM = pl.BlockSpec(memory_space=pltpu.VMEM)
+SMEM = pl.BlockSpec(memory_space=pltpu.SMEM)
+
+
+class Plan:
+    def __init__(self, n_gx, n_gy, n_gz, populations, contacts, grains):
+        self.n_gx, self.n_gy, self.n_gz = n_gx, n_gy, n_gz
+        self.dx, self.dy, self.depth = populations.shape[1:]
+        self.grains = grains
+        self.bins = contacts.shape[1]
+        self.sources = n_gx * n_gy
+        self.group = self.dx * self.dy
+        self.halo = SUBSTEPS
+        self.own = self.depth // self.sources
+        self.rows = self.own + 2 * self.halo
+        self.columns = self.sources * self.group
+        self.per_tile = max(1, LANES // self.group)
+        self.fields = 24
+        self.tiles = self.fields // self.per_tile
+        self.width = self.fields * self.group
+
+    def fits(self):
+        group = self.group
+        return (
+            self.sources > 1
+            and self.depth == LANES
+            and self.grains == LANES
+            and self.depth % self.sources == 0
+            and self.own % SUBLANES == 0
+            and self.rows == 2 * SUBLANES
+            and group == self.bins
+            and group * group == SUBLANES * LANES
+            and self.sources % self.per_tile == 0
+        )
+
+
+def swap_groups(parts, group):
+    parts = list(parts)
+    lane = lax.broadcasted_iota(jnp.int32, parts[0].shape, 1)
+    step = len(parts) // 2
+    while step:
+        low = lane // (group * step) % 2 == 0
+        for a in range(len(parts)):
+            if a // step % 2 == 0:
+                first, second = parts[a], parts[a + step]
+                shift = group * step
+                parts[a] = jnp.where(low, first, pltpu.roll(second, shift, 1))
+                parts[a + step] = jnp.where(low, pltpu.roll(first, LANES - shift, 1), second)
+        step //= 2
+    return parts
+
+
+def prepare_kernel(plan, pop_ref, vel_ref, vol_ref, slot_ref, cell_ref, link_ref, turned_ref, edge_ref):
+    group, bins = plan.group, plan.bins
+    rate = vol_ref[...] * slot_ref[...].astype(jnp.float32)
+    whole = 19 * group // LANES
+    for t in range(whole):
+        turned_ref[:, t * LANES : (t + 1) * LANES] = pop_ref[t * LANES : (t + 1) * LANES, :].T
+    tail = jnp.concatenate(
+        [pop_ref[whole * LANES :, :], vel_ref[...], rate, jnp.zeros((bins, LANES), jnp.float32)], axis=0
+    )
+    for t in range(whole, plan.tiles):
+        part = tail[(t - whole) * LANES : (t - whole + 1) * LANES, :].T
+        if t == plan.tiles - 1:
+            lane = lax.broadcasted_iota(jnp.int32, part.shape, 1)
+            part = jnp.where(lane >= LANES - bins, cell_ref[...], part)
+        turned_ref[:, t * LANES : (t + 1) * LANES] = part
+    halo = plan.halo
+    edge_ref[0:halo, : plan.width] = turned_ref[plan.depth - halo :, :]
+    edge_ref[halo:, : plan.width] = turned_ref[0:halo, :]
+    edge_ref[:, plan.width :] = link_ref[...]
+
+
+def windows_kernel(plan, turned_ref, lower_ref, upper_ref, link_ref, out_ref, whole_ref):
+    halo, own, rows, width = plan.halo, plan.own, plan.rows, plan.width
+    whole_ref[0:halo, :] = lower_ref[0:halo, :width]
+    whole_ref[halo : halo + plan.depth, :] = turned_ref[...]
+    whole_ref[halo + plan.depth :, :] = upper_ref[halo:, :width]
+    for p in range(plan.sources):
+        out_ref[p, :, :width] = whole_ref[p * own : p * own + rows, :]
+        out_ref[p, :SUBLANES, width:] = link_ref[...]
+        if p == 0:
+            other = lower_ref[:, width:]
+        elif p == plan.sources - 1:
+            other = upper_ref[:, width:]
+        else:
+            other = link_ref[...]
+        out_ref[p, SUBLANES:, width:] = other
+
+
+def three_parts(x):
+    high = x.astype(jnp.bfloat16)
+    rest = x - high.astype(jnp.float32)
+    middle = rest.astype(jnp.bfloat16)
+    low = (rest - middle.astype(jnp.float32)).astype(jnp.bfloat16)
+    return high, middle, low
+
+
+def exact_dot(parts, matrix, contract):
+    stacked = jnp.concatenate([piece for x in parts for piece in three_parts(x)], axis=0)
+    out = lax.dot_general(
+        stacked, matrix, (((1,), (contract,)), ((), ())), preferred_element_type=jnp.float32
+    )
+    rows = parts[0].shape[0]
+    result = []
+    for i in range(len(parts)):
+        at = 3 * i * rows
+        result.append(
+            (out[at + 2 * rows : at + 3 * rows] + out[at + rows : at + 2 * rows]) + out[at : at + rows]
+        )
+    return result
+
+
+def shifted(plan, x, axis, by):
+    size = plan.columns
+    lane = lax.broadcasted_iota(jnp.int32, x.shape, 1)
+    group, dx, dy = plan.group, plan.dx, plan.dy
+
+    def back(amount):
+        return pltpu.roll(x, (by * amount) % size, 1) if amount % size else x
+
+    if axis == 0:
+        place = lane % group // dy
+        edge = place == (0 if by == 1 else dx - 1)
+        return jnp.where(edge, back(plan.n_gy * group - (dx - 1) * dy), back(dy))
+    place = lane % dy
+    holder = lane // group % plan.n_gy
+    edge = place == (0 if by == 1 else dy - 1)
+    last = holder == (0 if by == 1 else plan.n_gy - 1)
+    across = jnp.where(last, back(-((plan.n_gy - 1) * group + dy - 1)), back(group - dy + 1))
+    return jnp.where(edge, across, back(1))
+
+
+def substeps_kernel(plan, where_ref, in_ref, out_ref, f_ref, post_ref, u_ref, force_ref, v_ref, aux_ref,
+                    column_ref, link_ref):
+    rows, columns, group, per = plan.rows, plan.columns, plan.group, plan.per_tile
+    halo, own = plan.halo, plan.own
+    quads = plan.sources // per
+    first, last = where_ref[0] == 1, where_ref[1] == 1
+    ground, ceiling = where_ref[2] == 1, where_ref[3] == 1
+
+    for t in range(plan.tiles):
+        for q in range(quads):
+            lanes = slice(q * LANES, (q + 1) * LANES)
+            parts = [in_ref[q * per + s, :, t * LANES : (t + 1) * LANES] for s in range(per)]
+            for j, part in enumerate(swap_groups(parts, group)):
+                field = t * per + j
+                if field < 19:
+                    f_ref[field, :, lanes] = part
+                elif field < 22:
+                    v_ref[field - 19, :, lanes] = part
+                else:
+                    aux_ref[field - 22, :, lanes] = part
+
+    rate = aux_ref[0]
+    live = (rate > 0.0).astype(jnp.float32)
+    cells = aux_ref[1]
+    other_cells = jnp.where(first, cells[0:1, :], cells[rows - 1 : rows, :])
+    which = lax.broadcasted_iota(jnp.int32, (columns, columns), 0).astype(jnp.float32)
+    for k, chosen in enumerate((cells[halo : halo + 1, :], other_cells)):
+        column_ref[k] = (which == chosen).astype(jnp.float32).astype(jnp.bfloat16)
+    lane = lax.broadcasted_iota(jnp.int32, (SUBLANES, LANES), 1)
+    for k in range(2):
+        for s in range(plan.sources):
+            packed = in_ref[s, k * SUBLANES : (k + 1) * SUBLANES, plan.width :]
+            place = s % per
+            pieces = []
+            for g in range(per):
+                moved = packed if g == place else pltpu.roll(packed, (place - g) * group % LANES, 1)
+                pieces.append(jnp.where(lane // group == place, moved, 0.0))
+            link_ref[k, s * group : (s + 1) * group, :] = jnp.concatenate(pieces, axis=0).astype(jnp.bfloat16)
+
+    row = lax.broadcasted_iota(jnp.int32, (rows, columns), 0)
+    foreign = (first & (row < halo)) | (last & (row >= halo + own))
+
+    def choose(mine, others):
+        return [jnp.where(foreign, b, a) for a, b in zip(mine, others)]
+
+    def on_columns(parts, contract):
+        return choose(
+            exact_dot(parts, column_ref[0], contract), exact_dot(parts, column_ref[1], contract)
+        )
+
+    def near(parts):
+        both = []
+        for k in range(2):
+            blocks = [
+                exact_dot(
+                    [x[:, q * LANES : (q + 1) * LANES] for x in parts],
+                    link_ref[k, q * LANES : (q + 1) * LANES, :],
+                    1,
+                )
+                for q in range(quads)
+            ]
+            both.append([jnp.concatenate([b[i] for b in blocks], axis=1) for i in range(len(parts))])
+        return choose(*both)
+
+    force_ref[3] = on_columns([rate], 1)[0]
+    count = near([live])[0]
+    aux_ref[1] = count
+
+    def step(_, carry):
+        for q in range(quads):
+            lanes = slice(q * LANES, (q + 1) * LANES)
+            popul = [f_ref[i, :, lanes] for i in range(19)]
+            density = popul[0]
+            for i in range(1, 19):
+                density = density + popul[i]
+            u_ref[3, :, lanes] = density
+            for a in range(3):
+                rising = [popul[i] for i in range(19) if VELOCITIES[i, a] == 1]
+                falling = [popul[i] for i in range(19) if VELOCITIES[i, a] == -1]
+                u_ref[a, :, lanes] = (sum(rising[1:], rising[0]) - sum(falling[1:], falling[0])) / density
+        rate = aux_ref[0]
+        count = aux_ref[1]
+        live = (rate > 0.0).astype(jnp.float32)
+        speed = on_columns([u_ref[a] for a in range(3)], 0)
+        velocity = [v_ref[a] for a in range(3)]
+        touching = near([velocity[a] * live for a in range(3)])
+        drags = [drag_factor * rate * (speed[a] - velocity[a]) for a in range(3)]
+        for a, force in enumerate(on_columns([-d for d in drags], 1)):
+            force_ref[a] = force
+        for a in range(3):
+            push = contact_stiffness * live * (touching[a] - count * velocity[a])
+            updated = velocity[a] + drags[a] + push
+            if a == 2:
+                updated = updated - gravity * live
+            v_ref[a] = updated
+        for q in range(quads):
+            lanes = slice(q * LANES, (q + 1) * LANES)
+            density = u_ref[3, :, lanes]
+            scale = 1.0 / (1.0 + force_ref[3, :, lanes])
+            target = [
+                scale * (u_ref[a, :, lanes] + relax_time * force_ref[a, :, lanes] / density)
+                for a in range(3)
+            ]
+            square = target[0] * target[0] + target[1] * target[1] + target[2] * target[2]
+            base = 1.0 - 1.5 * square
+            for i in range(19):
+                along = None
+                for a in range(3):
+                    if VELOCITIES[i, a] != 0:
+                        term = target[a] if VELOCITIES[i, a] == 1 else -target[a]
+                        along = term if along is None else along + term
+                shape = base if along is None else base + along * (3.0 + 4.5 * along)
+                equil = (float(WEIGHTS[i]) * density) * shape
+                popul = f_ref[i, :, lanes]
+                post_ref[i, :, lanes] = popul - (popul - equil) * (1.0 / relax_time)
+        bottom = ground & (row == halo)
+        top = ceiling & (row == halo + own - 1)
+        for i in range(19):
+            moved = post_ref[i]
+            for axis in range(2):
+                if VELOCITIES[i, axis] != 0:
+                    moved = shifted(plan, moved, axis, int(VELOCITIES[i, axis]))
+            if VELOCITIES[i, 2] == 1:
+                moved = jnp.where(bottom, post_ref[OPPOSITE[i]], pltpu.roll(moved, 1, 0))
+            elif VELOCITIES[i, 2] == -1:
+                moved = jnp.where(top, post_ref[OPPOSITE[i]], pltpu.roll(moved, rows - 1, 0))
+            f_ref[i] = moved
+        return carry
+
+    lax.fori_loop(0, SUBSTEPS, step, 0)
+
+    for t in range(plan.tiles):
+        for q in range(quads):
+            lanes = slice(q * LANES, (q + 1) * LANES)
+            parts = []
+            for j in range(per):
+                field = t * per + j
+                if field < 19:
+                    part = f_ref[field, halo : halo + own, lanes]
+                elif field < 22:
+                    part = v_ref[field - 19, halo : halo + own, lanes]
+                else:
+                    part = jnp.zeros((own, LANES), jnp.float32)
+                parts.append(part)
+            for s, part in enumerate(swap_groups(parts, group)):
+                out_ref[q * per + s, :, t * LANES : (t + 1) * LANES] = part
+
+
+def finish_kernel(plan, in_ref, pop_ref, vel_ref):
+    group = plan.group
+    whole = 19 * group // LANES
+    rest = 19 * group - whole * LANES
+    tail = []
+    for t in range(plan.tiles):
+        part = in_ref[:, t * LANES : (t + 1) * LANES].T
+        if t < whole:
+            pop_ref[t * LANES : (t + 1) * LANES, :] = part
+        else:
+            tail.append(part)
+    tail = jnp.concatenate(tail, axis=0)
+    pop_ref[whole * LANES :, :] = tail[:rest, :]
+    vel_ref[...] = tail[rest : rest + 3 * plan.bins, :]
+
+
+def windows_body(plan, populations, grain_velocity, grain_volume, slots, contacts, bin_cell):
+    group, bins, sources = plan.group, plan.bins, plan.sources
+    n_gx, n_gy, n_gz = plan.n_gx, plan.n_gy, plan.n_gz
+    wide = plan.width + LANES
+    column_blocks = n_gz
+    width_y = plan.dy * n_gy
+    xcell = bin_cell // (width_y * column_blocks)
+    ycell = bin_cell // column_blocks % width_y
+    source = xcell // plan.dx * n_gy + ycell // plan.dy
+    place = source * group + xcell % plan.dx * plan.dy + ycell % plan.dy
+    cell_row = jnp.pad(place.astype(jnp.float32), (LANES - bins, 0)).reshape(1, LANES)
+    links = contacts.reshape(-1, SUBLANES, bins).transpose(1, 0, 2).reshape(SUBLANES, LANES)
+    links = links.astype(jnp.float32)
+    f32 = jnp.float32
+
+    def call(kernel, shapes, inputs, scratch=(), specs=None):
+        return pl.pallas_call(
+            lambda *refs: kernel(plan, *refs),
+            out_shape=shapes,
+            in_specs=specs or [VMEM] * len(inputs),
+            out_specs=jax.tree.map(lambda _: VMEM, shapes),
+            scratch_shapes=list(scratch),
+        )(*inputs)
+
+    turned, edge = call(
+        prepare_kernel,
+        (
+            jax.ShapeDtypeStruct((plan.depth, plan.width), f32),
+            jax.ShapeDtypeStruct((2 * plan.halo, wide), f32),
+        ),
+        (
+            populations.reshape(19 * group, LANES),
+            grain_velocity.reshape(3 * bins, LANES),
+            grain_volume,
+            slots,
+            cell_row,
+            links,
+        ),
+    )
+    if n_gz == 1:
+        lower = upper = edge
+    elif n_gz == 2:
+        lower = upper = lax.ppermute(edge, "gz", [(0, 1), (1, 0)])
+    else:
+        lower = passed_along(edge, "gz", 1)
+        upper = passed_along(edge, "gz", -1)
+    outgoing = call(
+        windows_kernel,
+        jax.ShapeDtypeStruct((sources, plan.rows, wide), f32),
+        (turned, lower, upper, links),
+        (pltpu.VMEM((plan.depth + 2 * plan.halo, plan.width), f32),),
+    )
+    incoming = lax.all_to_all(outgoing, ("gx", "gy"), split_axis=0, concat_axis=0, tiled=True)
+    here = lax.axis_index("gx") * n_gy + lax.axis_index("gy")
+    layer = lax.axis_index("gz")
+    first, last = here == 0, here == sources - 1
+    place = jnp.stack([first, last, first & (layer == 0), last & (layer == n_gz - 1)]).astype(jnp.int32)
+    rows, columns = plan.rows, plan.columns
+    back = call(
+        substeps_kernel,
+        jax.ShapeDtypeStruct((sources, plan.own, plan.width), f32),
+        (place, incoming),
+        (
+            pltpu.VMEM((19, rows, columns), f32),
+            pltpu.VMEM((19, rows, columns), f32),
+            pltpu.VMEM((4, rows, columns), f32),
+            pltpu.VMEM((4, rows, columns), f32),
+            pltpu.VMEM((3, rows, columns), f32),
+            pltpu.VMEM((2, rows, columns), f32),
+            pltpu.VMEM((2, columns, columns), jnp.bfloat16),
+            pltpu.VMEM((2, columns, LANES), jnp.bfloat16),
+        ),
+        [SMEM, VMEM],
+    )
+    result = lax.all_to_all(back, ("gx", "gy"), split_axis=0, concat_axis=0, tiled=True)
+    fluid, velocity = call(
+        finish_kernel,
+        (
+            jax.ShapeDtypeStruct((19 * group, LANES), f32),
+            jax.ShapeDtypeStruct((3 * bins, LANES), f32),
+        ),
+        (result.reshape(plan.depth, plan.width),),
+    )
+    return (fluid.reshape(populations.shape), velocity.reshape(grain_velocity.shape))
+
+
+def body(populations, grain_velocity, grain_volume, slots, contacts, bin_cell):
+    plan = Plan(
+        lax.axis_size("gx"),
+        lax.axis_size("gy"),
+        lax.axis_size("gz"),
+        populations,
+        contacts,
+        grain_velocity.shape[2],
+    )
+    arrays = (populations, grain_velocity, grain_volume, slots, contacts, bin_cell)
+    if plan.fits() and contacts.shape[0] == contacts.shape[1]:
+        return windows_body(plan, *arrays)
+    return columns_body(*arrays)
+
+
 def solution(mesh):
     placed = (
         P(None, "gx", "gy", "gz"),

time: 287 us -> 71.8 us (0.25)
  local copies, waits for them, and re-layouts: 67 us -> 2.91 us
  blocking collectives: 82.4 us -> 18.4 us
  starting transfers between devices: 49 us -> 9.44 us
  waiting for transfers between devices: 51.2 us -> 22.2 us
  other arithmetic: 30.8 us -> 2.06 us
  Pallas kernels: 0 us -> 15.8 us
  between operations: 4.16 us -> 0.66 us
    all_to_all x5 -> x1, blocking collectives: 68.7 us -> 18.4 us  [windows_body(): lax.all_to_all(back, ('gx', 'gy'), split_axis=0, concat_axis=0, tiled=True)]
    ppermute x24 -> x1, starting transfers between devices: 36.3 us -> 2.97 us  [windows_body(): lower = upper = lax.ppermute(edge, 'gz', [(0, 1), (1, 0)])]
    gather x56 -> x0, local copies, waits for them, and re-layouts: 32 us -> none  [the longest x24 13.3 us: moments(): momentum = jnp.sum(popul[rising], axis=0) - jnp.sum(popul[falling], axis=0)]
    scatter x28 -> x0, local copies, waits for them, and re-layouts: 25.2 us -> none  [the longest x4 8.21 us: body(): jnp.zeros((4, sources * capacity, grains), jnp.float32).at[:, own_row]]
    scatter-add x4 -> x0, other arithmetic: 20.8 us -> none  [body(): jnp.zeros_like(flow).at[:, send_column]]
    ppermute x24 -> x1, waiting for transfers between devices: 22.5 us -> 2.06 us  [windows_body(): lower = upper = lax.ppermute(edge, 'gz', [(0, 1), (1, 0)])]
    pallas_call x0 -> x4, Pallas kernels: none -> 15.8 us  [call(): pl.pallas_call(lambda *refs: kernel(plan, *refs), out_shape=shapes, in_sp...]
    unnamed x1 -> x0, blocking collectives: 13.8 us -> none
  transfers between devices with their start and end apart: 27 -> 2, of which waited for: 21 -> 2; matrix products, arithmetic and copies ran while one was open for 6% -> 1% of each run, Pallas kernels for 0% -> 0%
where the time goes in v1:
time: 71.8 us; the launch traced here: 71.3 us
  waiting for transfers between devices  22.2 us (31%)
  blocking collectives  18.4 us (26%)
  Pallas kernels  15.8 us (22%)
  starting transfers between devices  9.44 us (13%)
  local copies, waits for them, and re-layouts  2.91 us (4%)
  other arithmetic  2.06 us (3%)
    all_to_all x1, waiting for transfers between devices, windows_body(): lax.all_to_all(outgoing, ('gx', 'gy'), split_axis=0, concat_axis=0, tiled...  20.1 us
    all_to_all x1, blocking collectives, windows_body(): lax.all_to_all(back, ('gx', 'gy'), split_axis=0, concat_axis=0, tiled=True)  18.4 us
    pallas_call x4, Pallas kernels, call(): pl.pallas_call(lambda *refs: kernel(plan, *refs), out_shape=shapes, in_sp...  15.8 us
    all_to_all x1, starting transfers between devices, windows_body(): lax.all_to_all(outgoing, ('gx', 'gy'), split_axis=0, concat_axis=0, tiled...  6.47 us
    ppermute x1, starting transfers between devices, windows_body(): lower = upper = lax.ppermute(edge, 'gz', [(0, 1), (1, 0)])  2.97 us
    ppermute x1, waiting for transfers between devices, windows_body(): lower = upper = lax.ppermute(edge, 'gz', [(0, 1), (1, 0)])  2.06 us
    unnamed x4, local copies, waits for them, and re-layouts  1.56 us
  transfers between devices with their start and end apart: 2, of which 2 were waited for; matrix products, arithmetic and copies ran while one was open for 1% of the time, Pallas kernels for 0%

profile of v1, /device:TPU:0, one launch (start us, length us, event | category | flops | bytes accessed | tf_op | source)
XLA Modules:
  0.0 71.3 jit_solution(1770687289014140514)
XLA Ops:
  0.6 0.7 fusion.4
  1.3 0.7 pad_bitcast_fusion.refs_4_
  2.0 0.7 %convert_bitcast_fusion = f32[4,8,32]{2,1,0:T(8,128)S(1)} fusion(s32[32,32]{1,0:T(8,128)} %param.10), kind=kLoop, calls=%fused_computation.1 | loop fusion | flops 1024 | bytes 8192 | tf_op jit(solution)/shard_map/convert_element_type | solution.py:530
  2.7 0.7 convert_element_type.22.refs_5_.refs_3_
  3.4 1.9 %shard_map.77 = (f32[128,768]{1,0:T(8,128)}, f32[8,896]{1,0:T(8,128)}) custom-call(f32[608,128]{1,0:T(8,128)} %bitcast.17, f32[96,128]{1,0:T(8,128)} %bitcast.19, f32[32,128]{1,0:T(8,128)} %refs_2_.1, s32[32,128]{1,0:T(8,128)} %refs_3_.1, f32[1,128]{1,0:T(1,128)} %pad_bitcast_fusion.refs_4_, f32[8,128]{1,0:T(8,128)} %convert_element_type.22.refs_5_.refs_3_), custom_call_target="tpu_custom_call" | custom-call | tf_op jit(solution)/shard_map/pallas_call | solution.py:534
  5.3 3.0 %collective-permute-start = (f32[8,896]{1,0:T(8,128)}, f32[8,896]{1,0:T(8,128)S(1)}, u32[]{:S(2)}, u32[]{:S(2)}) collective-permute-start(f32[8,896]{1,0:T(8,128)} %get-tuple-element.7), channel_id=1, source_target_pairs={{0,1},{1,0},{2,3},{3,2},{4,5},{5,4},{6,7},{7,6},{8,9},{9,8},{10,11... | collective-permute-start | bytes 86024 | tf_op jit(solution)/shard_map/ppermute | solution.py:560
  8.3 2.1 %collective-permute-done.refs_1_.refs_2_ = f32[8,896]{1,0:T(8,128)S(1)} collective-permute-done((f32[8,896]{1,0:T(8,128)}, f32[8,896]{1,0:T(8,128)S(1)}, u32[]{:S(2)}, u32[]{:S(2)}) %collective-permute-start) | collective-permute-done | bytes 28704 | tf_op jit(solution)/shard_map/ppermute | solution.py:560
  10.4 0.0 copy-start.1
  10.4 0.6 copy-done.1
  11.0 2.0 %shard_map.78 = f32[16,16,896]{2,1,0:T(8,128)} custom-call(f32[128,768]{1,0:T(8,128)} %get-tuple-element.6.refs_0_, f32[8,896]{1,0:T(8,128)} %copy-done.1, f32[8,896]{1,0:T(8,128)} %copy-done.1, f32[8,128]{1,0:T(8,128)} %convert_element_type.22.refs_5_.refs_3_), custom_call_target="tpu_custom_call" | custom-call | tf_op jit(solution)/shard_map/pallas_call | solution.py:534
  13.0 6.5 %all-to-all-start = ((f32[16,16,896]{2,1,0:T(8,128)}), f32[16,16,896]{2,1,0:T(8,128)S(1)}, u32[]{:S(2)}, u32[]{:S(2)}) async-start(f32[16,16,896]{2,1,0:T(8,128)} %shard_map.78), calls=%async_computation | async-start | bytes 1835008 | tf_op jit(solution)/shard_map/all_to_all | solution.py:570
  19.5 0.7 add_convert_fusion.refs_0_
  20.2 20.1 %all-to-all-done.refs_1_ = f32[16,16,896]{2,1,0:T(8,128)S(1)} async-done(((f32[16,16,896]{2,1,0:T(8,128)}), f32[16,16,896]{2,1,0:T(8,128)S(1)}, u32[]{:S(2)}, u32[]{:S(2)}) %all-to-all-start) | async-done | bytes 917536 | tf_op jit(solution)/shard_map/all_to_all | solution.py:570
  40.3 0.0 copy-start
  40.3 1.0 %copy-done = f32[16,16,896]{2,1,0:T(8,128)} copy-done((f32[16,16,896]{2,1,0:T(8,128)}, f32[16,16,896]{2,1,0:T(8,128)S(1)}, u32[]{:S(2)}) %copy-start) | copy-done | bytes 917528
  41.2 9.9 %shard_map.79 = f32[16,8,768]{2,1,0:T(8,128)} custom-call(s32[4]{0:T(128)} %add_convert_fusion.refs_0_, f32[16,16,896]{2,1,0:T(8,128)} %copy-done), custom_call_target="tpu_custom_call" | custom-call | tf_op jit(solution)/shard_map/pallas_call | solution.py:534
  51.1 18.4 %all_to_all.10 = f32[16,8,768]{2,1,0:T(8,128)} all-to-all(f32[16,8,768]{2,1,0:T(8,128)} %shard_map.79), channel_id=1, replica_groups=mesh['gx'=4,'gy'=4,'gz'=2] {'gx','gy'}, dimensions={0} | all-to-all | bytes 786432 | tf_op jit(solution)/shard_map/all_to_all | solution.py:592
  69.5 1.9 %shard_map.80 = (f32[608,128]{1,0:T(8,128)}, f32[96,128]{1,0:T(8,128)}) custom-call(f32[128,768]{1,0:T(8,128)} %bitcast.16), custom_call_target="tpu_custom_call" | custom-call | tf_op jit(solution)/shard_map/pallas_call | solution.py:534
  (1 shorter events, 0.0 us)
Async XLA Ops:
  5.3 5.0 %collective-permute-start = (f32[8,896]{1,0:T(8,128)}, f32[8,896]{1,0:T(8,128)S(1)}, u32[]{:S(2)}, u32[]{:S(2)}) collective-permute-start(f32[8,896]{1,0:T(8,128)} %get-tuple-element.7), channel_id=1, source_target_pairs={{0,1},{1,0},{2,3},{3,2},{4,5},{5,4},{6,7},{7,6},{8,9},{9,8},{10,11... | collective-permute-start | bytes 86024 | tf_op jit(solution)/shard_map/ppermute | solution.py:560
  10.4 0.6 copy-start.1
  13.0 27.3 %all-to-all-start = ((f32[16,16,896]{2,1,0:T(8,128)}), f32[16,16,896]{2,1,0:T(8,128)S(1)}, u32[]{:S(2)}, u32[]{:S(2)}) async-start(f32[16,16,896]{2,1,0:T(8,128)} %shard_map.78), calls=%async_computation | async-start | bytes 1835008 | tf_op jit(solution)/shard_map/all_to_all | solution.py:570
  40.3 1.0 %copy-start = (f32[16,16,896]{2,1,0:T(8,128)}, f32[16,16,896]{2,1,0:T(8,128)S(1)}, u32[]{:S(2)}) copy-start(f32[16,16,896]{2,1,0:T(8,128)S(1)} %all-to-all-done.refs_1_) | copy-start | bytes 2752516

commit v2 on v0

--- a/solution.py
+++ b/solution.py
@@ -2,6 +2,8 @@
 import jax.numpy as jnp
 import numpy as np
 from jax import lax
+from jax.experimental import pallas as pl
+from jax.experimental.pallas import tpu as pltpu
 from jax.sharding import PartitionSpec as P
 
 SUBSTEPS = 4
@@ -163,7 +165,7 @@
     return jnp.sum((same & before).astype(jnp.int32), axis=-1)
 
 
-def body(populations, grain_velocity, grain_volume, slots, contacts, bin_cell):
+def columns_body(populations, grain_velocity, grain_volume, slots, contacts, bin_cell):
     n_gx = lax.axis_size("gx")
     n_gy = lax.axis_size("gy")
     n_gz = lax.axis_size("gz")
@@ -214,6 +216,440 @@
     return (fluid, velocity)
 
 
+LANES = 128
+SUBLANES = 8
+VMEM_LIMIT = 24 * 1024 * 1024
+VMEM = pl.BlockSpec(memory_space=pltpu.VMEM)
+FIELD_V = (19, 21, 22)
+FIELD_CELL = 20
+FIELD_RATE = 23
+
+
+class Plan:
+    def __init__(self, n_gx, n_gy, n_gz, populations, contacts, grains):
+        self.n_gx, self.n_gy, self.n_gz = n_gx, n_gy, n_gz
+        self.dx, self.dy, self.depth = populations.shape[1:]
+        self.grains = grains
+        self.bins = contacts.shape[1]
+        self.sources = n_gx * n_gy
+        self.group = self.dx * self.dy
+        self.halo = SUBSTEPS
+        self.own = self.depth // self.sources
+        self.rows = self.own + 2 * self.halo
+        self.columns = self.sources * self.group
+        self.per_tile = max(1, LANES // self.group)
+        self.fields = 24
+        self.tiles = self.fields // self.per_tile
+        self.width = self.fields * self.group
+        self.wide = self.width + LANES
+
+    def fits(self):
+        group = self.group
+        return (
+            self.sources % 2 == 0
+            and self.depth == LANES
+            and self.grains == LANES
+            and self.own * self.sources == LANES
+            and self.own == SUBLANES
+            and self.rows == 2 * SUBLANES
+            and group == self.bins
+            and group * group == SUBLANES * LANES
+            and self.per_tile == self.n_gy
+        )
+
+    def device(self, window):
+        layer, place = divmod(window, self.sources)
+        if layer % 2:
+            place = self.sources - 1 - place
+        return place * self.n_gz + layer
+
+    def swaps(self, start):
+        count = self.n_gz * self.sources
+        paired = []
+        for a in range(start, count - 1, 2):
+            paired += [(a, a + 1), (a + 1, a)]
+        if start:
+            paired += [(0, 0), (count - 1, count - 1)]
+        return [(self.device(a), self.device(b)) for a, b in paired]
+
+    def place(self):
+        layer = lax.axis_index("gz")
+        here = lax.axis_index("gx") * self.n_gy + lax.axis_index("gy")
+        return jnp.where(lax.rem(layer, 2) == 1, self.sources - 1 - here, here), layer
+
+    def holder(self, window):
+        layer = lax.axis_index("gz")
+        return jnp.where(lax.rem(layer, 2) == 1, self.sources - 1 - window, window)
+
+
+def swap_groups(parts, group):
+    parts = list(parts)
+    lane = lax.broadcasted_iota(jnp.int32, parts[0].shape, 1)
+    step = len(parts) // 2
+    while step:
+        low = lane // (group * step) % 2 == 0
+        for a in range(len(parts)):
+            if a // step % 2 == 0:
+                first, second = parts[a], parts[a + step]
+                shift = group * step
+                parts[a] = jnp.where(low, first, pltpu.roll(second, shift, 1))
+                parts[a + step] = jnp.where(low, pltpu.roll(first, LANES - shift, 1), second)
+        step //= 2
+    return parts
+
+
+def prepare_kernel(plan, pop_ref, vel_ref, vol_ref, slot_ref, link_ref, cell_ref, out_ref):
+    group, bins, own = plan.group, plan.bins, plan.own
+    whole = 19 * group // LANES
+    cell = cell_ref[...]
+    width_y = plan.dy * plan.n_gy
+    xcell = lax.div(cell, width_y * plan.n_gz)
+    ycell = lax.rem(lax.div(cell, plan.n_gz), width_y)
+    source = lax.div(xcell, plan.dx) * plan.n_gy + lax.div(ycell, plan.dy)
+    cell = source * group + lax.rem(xcell, plan.dx) * plan.dy + lax.rem(ycell, plan.dy)
+    cell = jnp.concatenate([cell.astype(jnp.float32), jnp.zeros((1, LANES - bins), jnp.float32)], axis=1)
+    packed = jnp.concatenate(
+        [link_ref[g * SUBLANES : (g + 1) * SUBLANES, :].astype(jnp.float32) for g in range(bins // SUBLANES)],
+        axis=1,
+    )
+    holders = [plan.holder(q) for q in range(plan.sources)]
+    for t in range(plan.tiles):
+        if t < whole:
+            block = pop_ref[t * LANES : (t + 1) * LANES, :]
+        elif t == whole:
+            block = jnp.concatenate([pop_ref[whole * LANES :, :], vel_ref[:bins, :]], axis=0)
+        else:
+            rate = vol_ref[...] * slot_ref[...].astype(jnp.float32)
+            block = jnp.concatenate([rate, vel_ref[bins:, :], rate], axis=0)
+        block = block.T
+        if t == plan.tiles - 1:
+            lane = lax.broadcasted_iota(jnp.int32, block.shape, 1)
+            block = jnp.where(lane < bins, cell, block)
+        for q in range(plan.sources):
+            out_ref[holders[q], :, t * LANES : (t + 1) * LANES] = block[q * own : (q + 1) * own, :]
+    for q in range(plan.sources):
+        out_ref[q, :, plan.width :] = packed
+
+
+def edges_kernel(plan, in_ref, inner_ref, outer_ref):
+    window, _ = plan.place()
+    even = lax.rem(window, 2) == 0
+    halo = plan.halo
+    low_rows = lax.broadcasted_iota(jnp.int32, (SUBLANES, LANES), 0) < halo
+    for h in range(plan.sources // 2):
+        for t in range(plan.tiles):
+            lanes = slice(t * LANES, (t + 1) * LANES)
+            a, b = in_ref[2 * h, :, lanes], in_ref[2 * h + 1, :, lanes]
+            low = jnp.where(low_rows, a, pltpu.roll(b, halo, 0))
+            high = jnp.where(low_rows, pltpu.roll(a, halo, 0), b)
+            inner_ref[h, :, lanes] = jnp.where(even, high, low)
+            outer_ref[h, :, lanes] = jnp.where(even, low, high)
+        for k in range(2):
+            start = plan.width + k * LANES
+            outer_ref[h, :, start : start + LANES] = in_ref[2 * h + k, :, plan.width :]
+
+
+def two_part_dot(parts, matrix, contract):
+    whole = jnp.concatenate(parts, axis=0)
+    rest = whole - whole.astype(jnp.bfloat16).astype(jnp.float32)
+    stacked = jnp.concatenate([whole, rest], axis=0).astype(jnp.bfloat16)
+    out = lax.dot_general(
+        stacked, matrix, (((1,), (contract,)), ((), ())), preferred_element_type=jnp.float32
+    )
+    rows = parts[0].shape[0]
+    half = rows * len(parts)
+    return [
+        out[i * rows : (i + 1) * rows] + out[half + i * rows : half + (i + 1) * rows]
+        for i in range(len(parts))
+    ]
+
+
+def substeps_kernel(plan, in_ref, inner_ref, outer_ref, out_ref, f_ref, post_ref, u_ref, force_ref, v_ref,
+                    aux_ref, column_ref, link_ref):
+    rows, columns, group, per = plan.rows, plan.columns, plan.group, plan.per_tile
+    halo, own, dx, dy = plan.halo, plan.own, plan.dx, plan.dy
+    quads = plan.sources // per
+    window, layer = plan.place()
+    even = lax.rem(window, 2) == 0
+    first, last = window == 0, window == plan.sources - 1
+    ground, ceiling = first & (layer == 0), last & (layer == plan.n_gz - 1)
+    tile_row = lax.broadcasted_iota(jnp.int32, (SUBLANES, LANES), 0)
+
+    def store(field, lanes, part):
+        if field < 19:
+            f_ref[field, :, lanes] = part
+        elif field in FIELD_V:
+            v_ref[FIELD_V.index(field), :, lanes] = part
+        else:
+            aux_ref[0 if field == FIELD_RATE else 1, :, lanes] = part
+
+    for t in range(plan.tiles):
+        at = slice(t * LANES, (t + 1) * LANES)
+        for q in range(quads):
+            parts = []
+            for s in range(q * per, (q + 1) * per):
+                inner, outer = inner_ref[s // 2, :, at], outer_ref[s // 2, :, at]
+                below = jnp.where(even, outer, inner)
+                above = jnp.where(even, inner, outer)
+                if s % 2:
+                    below = pltpu.roll(below, halo, 0)
+                else:
+                    above = pltpu.roll(above, halo, 0)
+                turned = pltpu.roll(in_ref[s, :, at], halo, 0)
+                parts.append(
+                    jnp.concatenate(
+                        [jnp.where(tile_row < halo, below, turned), jnp.where(tile_row < halo, turned, above)],
+                        axis=0,
+                    )
+                )
+            lanes = slice(q * LANES, (q + 1) * LANES)
+            for j, part in enumerate(swap_groups(parts, group)):
+                store(t * per + j, lanes, part)
+
+    rate = aux_ref[0]
+    live = (rate > 0.0).astype(jnp.float32)
+    cells = aux_ref[1]
+    other_cells = jnp.where(first, cells[0:1, :], cells[rows - 1 : rows, :])
+    which = lax.broadcasted_iota(jnp.int32, (columns, columns), 0).astype(jnp.float32)
+    for k, chosen in enumerate((cells[halo : halo + 1, :], other_cells)):
+        column_ref[k] = (which == chosen).astype(jnp.float32).astype(jnp.bfloat16)
+    lane = lax.broadcasted_iota(jnp.int32, (SUBLANES, LANES), 1)
+    for k in range(2):
+        for s in range(plan.sources):
+            if k == 0:
+                packed = in_ref[s, :, plan.width :]
+            else:
+                start = plan.width + s % 2 * LANES
+                packed = outer_ref[s // 2, :, start : start + LANES]
+            place = s % per
+            pieces = []
+            for g in range(per):
+                moved = packed if g == place else pltpu.roll(packed, (place - g) * group % LANES, 1)
+                pieces.append(jnp.where(lane // group == place, moved, 0.0))
+            link_ref[k, s * group : (s + 1) * group, :] = jnp.concatenate(pieces, axis=0).astype(jnp.bfloat16)
+
+    row = lax.broadcasted_iota(jnp.int32, (rows, columns), 0)
+    tile_rows = lax.broadcasted_iota(jnp.int32, (SUBLANES, columns), 0)
+    below_foreign = first & (tile_rows < halo)
+    above_foreign = last & (tile_rows >= halo)
+
+    def both_layers(parts, product):
+        mine = product(parts, 0)
+        others = product([jnp.where(first, x[:SUBLANES], x[SUBLANES:]) for x in parts], 1)
+        return [
+            jnp.concatenate(
+                [jnp.where(below_foreign, b, a[:SUBLANES]), jnp.where(above_foreign, b, a[SUBLANES:])], axis=0
+            )
+            for a, b in zip(mine, others)
+        ]
+
+    def to_bins(parts, k):
+        return two_part_dot(parts, column_ref[k], 0)
+
+    def to_columns(parts, k):
+        return two_part_dot(parts, column_ref[k], 1)
+
+    def near(parts, k):
+        blocks = [
+            two_part_dot(
+                [x[:, q * LANES : (q + 1) * LANES] for x in parts], link_ref[k, q * LANES : (q + 1) * LANES, :], 1
+            )
+            for q in range(quads)
+        ]
+        return [jnp.concatenate([b[i] for b in blocks], axis=1) for i in range(len(parts))]
+
+    force_ref[3] = both_layers([rate], to_columns)[0]
+    aux_ref[1] = both_layers([live], near)[0]
+
+    wide_lane = lax.broadcasted_iota(jnp.int32, (rows, LANES), 1)
+    lane_y = lax.div(wide_lane, group) * dy + lax.rem(wide_lane, dy)
+    lane_x = lax.rem(lax.div(wide_lane, dy), dx)
+
+    def source_lanes(cx, cy):
+        y = lax.rem(lane_y - cy + plan.n_gy * dy, plan.n_gy * dy)
+        x = lax.rem(lane_x - cx + dx, dx)
+        return lax.div(y, dy) * group + x * dy + lax.rem(y, dy)
+
+    def step(_, carry):
+        for q in range(quads):
+            lanes = slice(q * LANES, (q + 1) * LANES)
+            popul = [f_ref[i, :, lanes] for i in range(19)]
+            density = popul[0]
+            for i in range(1, 19):
+                density = density + popul[i]
+            u_ref[3, :, lanes] = density
+            for a in range(3):
+                rising = [popul[i] for i in range(19) if VELOCITIES[i, a] == 1]
+                falling = [popul[i] for i in range(19) if VELOCITIES[i, a] == -1]
+                u_ref[a, :, lanes] = (sum(rising[1:], rising[0]) - sum(falling[1:], falling[0])) / density
+        rate = aux_ref[0]
+        count = aux_ref[1]
+        live = (rate > 0.0).astype(jnp.float32)
+        velocity = [v_ref[a] for a in range(3)]
+        speed = both_layers([u_ref[a] for a in range(3)], to_bins)
+        drags = [drag_factor * rate * (speed[a] - velocity[a]) for a in range(3)]
+        for a, force in enumerate(both_layers([-d for d in drags], to_columns)):
+            force_ref[a] = force
+        touching = both_layers([velocity[a] * live for a in range(3)], near)
+        for a in range(3):
+            push = contact_stiffness * live * (touching[a] - count * velocity[a])
+            updated = velocity[a] + drags[a] + push
+            if a == 2:
+                updated = updated - gravity * live
+            v_ref[a] = updated
+        for q in range(quads):
+            lanes = slice(q * LANES, (q + 1) * LANES)
+            density = u_ref[3, :, lanes]
+            scale = 1.0 / (1.0 + force_ref[3, :, lanes])
+            target = [
+                scale * (u_ref[a, :, lanes] + relax_time * force_ref[a, :, lanes] / density)
+                for a in range(3)
+            ]
+            square = target[0] * target[0] + target[1] * target[1] + target[2] * target[2]
+            base = 1.0 - 1.5 * square
+            for i in range(19):
+                along = None
+                for a in range(3):
+                    if VELOCITIES[i, a] != 0:
+                        term = target[a] if VELOCITIES[i, a] == 1 else -target[a]
+                        along = term if along is None else along + term
+                shape = base if along is None else base + along * (3.0 + 4.5 * along)
+                equil = (float(WEIGHTS[i]) * density) * shape
+                popul = f_ref[i, :, lanes]
+                post_ref[i, :, lanes] = popul - (popul - equil) * (1.0 / relax_time)
+        small_row = lax.broadcasted_iota(jnp.int32, (rows, LANES), 0)
+        bottom = ground & (small_row == halo)
+        top = ceiling & (small_row == halo + own - 1)
+        for i in range(19):
+            cx, cy, cz = (int(c) for c in VELOCITIES[i])
+            moved = [post_ref[i, :, q * LANES : (q + 1) * LANES] for q in range(quads)]
+            if cx or cy:
+                from_lane = source_lanes(cx, cy)
+                moved = [jnp.take_along_axis(x, from_lane, axis=1, mode="promise_in_bounds") for x in moved]
+            if cx:
+                edge = lane_x == (0 if cx == 1 else dx - 1)
+                moved = [jnp.where(edge, moved[(q - cx) % quads], moved[q]) for q in range(quads)]
+            for q in range(quads):
+                lanes = slice(q * LANES, (q + 1) * LANES)
+                x = moved[q]
+                if cz:
+                    x = pltpu.roll(x, cz % rows, 0)
+                    x = jnp.where(bottom if cz == 1 else top, post_ref[OPPOSITE[i], :, lanes], x)
+                f_ref[i, :, lanes] = x
+        return carry
+
+    lax.fori_loop(0, SUBSTEPS, step, 0)
+
+    for t in range(plan.tiles):
+        for q in range(quads):
+            lanes = slice(q * LANES, (q + 1) * LANES)
+            parts = []
+            for field in range(t * per, (t + 1) * per):
+                if field < 19:
+                    part = f_ref[field, halo : halo + own, lanes]
+                elif field in FIELD_V:
+                    part = v_ref[FIELD_V.index(field), halo : halo + own, lanes]
+                else:
+                    part = jnp.zeros((own, LANES), jnp.float32)
+                parts.append(part)
+            for s, part in enumerate(swap_groups(parts, group)):
+                out_ref[q * per + s, :, t * LANES : (t + 1) * LANES] = part
+
+
+def finish_kernel(plan, in_ref, pop_ref, vel_ref):
+    bins = plan.bins
+    whole = 19 * plan.group // LANES
+    rest = 19 * plan.group - whole * LANES
+    holders = [plan.holder(q) for q in range(plan.sources)]
+    for t in range(plan.tiles):
+        at = slice(t * LANES, (t + 1) * LANES)
+        block = jnp.concatenate([in_ref[holders[q], :, at] for q in range(plan.sources)], axis=0).T
+        if t < whole:
+            pop_ref[t * LANES : (t + 1) * LANES, :] = block
+        elif t == whole:
+            pop_ref[whole * LANES :, :] = block[:rest, :]
+            vel_ref[:bins, :] = block[rest:, :]
+        else:
+            vel_ref[bins:, :] = block[bins : 3 * bins, :]
+
+
+def windows_body(plan, populations, grain_velocity, grain_volume, slots, contacts, bin_cell):
+    group, bins, sources = plan.group, plan.bins, plan.sources
+    rows, columns, own = plan.rows, plan.columns, plan.own
+    f32 = jnp.float32
+
+    def call(kernel, shapes, inputs, scratch=()):
+        shapes = [jax.ShapeDtypeStruct(shape, f32) for shape in shapes]
+        return pl.pallas_call(
+            lambda *refs: kernel(plan, *refs),
+            out_shape=shapes,
+            in_specs=[VMEM] * len(inputs),
+            out_specs=[VMEM] * len(shapes),
+            scratch_shapes=list(scratch),
+            compiler_params=pltpu.CompilerParams(vmem_limit_bytes=VMEM_LIMIT),
+        )(*inputs)
+
+    (outgoing,) = call(
+        prepare_kernel,
+        [(sources, own, plan.wide)],
+        (
+            populations.reshape(19 * group, LANES),
+            grain_velocity.reshape(3 * bins, LANES),
+            grain_volume,
+            slots,
+            contacts,
+            bin_cell.reshape(1, bins),
+        ),
+    )
+    layer_axes, every_axis = ("gx", "gy"), ("gx", "gy", "gz")
+    incoming = lax.all_to_all(outgoing, layer_axes, split_axis=0, concat_axis=0, tiled=True)
+    half = sources // 2
+    inner, outer = call(
+        edges_kernel,
+        [(half, SUBLANES, plan.width), (half, SUBLANES, plan.width + 2 * LANES)],
+        (incoming,),
+    )
+    inner = lax.ppermute(inner, every_axis, plan.swaps(0))
+    outer = lax.ppermute(outer, every_axis, plan.swaps(1))
+    (back,) = call(
+        substeps_kernel,
+        [(sources, own, plan.width)],
+        (incoming, inner, outer),
+        (
+            pltpu.VMEM((19, rows, columns), f32),
+            pltpu.VMEM((19, rows, columns), f32),
+            pltpu.VMEM((4, rows, columns), f32),
+            pltpu.VMEM((4, rows, columns), f32),
+            pltpu.VMEM((3, rows, columns), f32),
+            pltpu.VMEM((2, rows, columns), f32),
+            pltpu.VMEM((2, columns, columns), jnp.bfloat16),
+            pltpu.VMEM((2, columns, LANES), jnp.bfloat16),
+        ),
+    )
+    result = lax.all_to_all(back, layer_axes, split_axis=0, concat_axis=0, tiled=True)
+    fluid, velocity = call(
+        finish_kernel,
+        [(19 * group, LANES), (3 * bins, LANES)],
+        (result,),
+    )
+    return (fluid.reshape(populations.shape), velocity.reshape(grain_velocity.shape))
+
+
+def body(populations, grain_velocity, grain_volume, slots, contacts, bin_cell):
+    plan = Plan(
+        lax.axis_size("gx"),
+        lax.axis_size("gy"),
+        lax.axis_size("gz"),
+        populations,
+        contacts,
+        grain_velocity.shape[2],
+    )
+    arrays = (populations, grain_velocity, grain_volume, slots, contacts, bin_cell)
+    if plan.fits() and contacts.shape[0] == contacts.shape[1]:
+        return windows_body(plan, *arrays)
+    return columns_body(*arrays)
+
+
 def solution(mesh):
     placed = (
         P(None, "gx", "gy", "gz"),

time: 287 us -> 59.6 us (0.21)
  local copies, waits for them, and re-layouts: 67 us -> 4.56 us
  waiting for transfers between devices: 51.2 us -> 1.07 us
  starting transfers between devices: 49 us -> 2.36 us
  blocking collectives: 82.4 us -> 42.4 us
  other arithmetic: 30.8 us -> 0 us
  Pallas kernels: 0 us -> 8.04 us
  between operations: 4.16 us -> 0.67 us
    ppermute x24 -> x2, starting transfers between devices: 36.3 us -> 2.36 us  [the longest x1 1.68 us: windows_body(): inner = lax.ppermute(inner, every_axis, plan.swaps(0))]
    gather x56 -> x0, local copies, waits for them, and re-layouts: 32 us -> none  [the longest x24 13.3 us: moments(): momentum = jnp.sum(popul[rising], axis=0) - jnp.sum(popul[falling], axis=0)]
    all_to_all x3 -> x0, waiting for transfers between devices: 28.7 us -> none  [the longest x2 18.8 us: carry_flow(): lax.all_to_all(outgoing, ('gx', 'gy'), split_axis=1, concat_axis=1, tiled...]
    all_to_all x5 -> x2, blocking collectives: 68.7 us -> 42.4 us  [the longest x1 22 us: windows_body(): lax.all_to_all(back, layer_axes, split_axis=0, concat_axis=0, tiled=True)]
    scatter x28 -> x0, local copies, waits for them, and re-layouts: 25.2 us -> none  [the longest x4 8.21 us: body(): jnp.zeros((4, sources * capacity, grains), jnp.float32).at[:, own_row]]
    ppermute x24 -> x2, waiting for transfers between devices: 22.5 us -> 1.07 us  [the longest x1 1.07 us: windows_body(): inner = lax.ppermute(inner, every_axis, plan.swaps(0))]
    scatter-add x4 -> x0, other arithmetic: 20.8 us -> none  [body(): jnp.zeros_like(flow).at[:, send_column]]
    unnamed x1 -> x0, blocking collectives: 13.8 us -> none
  transfers between devices with their start and end apart: 27 -> 2, of which waited for: 21 -> 1; matrix products, arithmetic and copies ran while one was open for 6% -> 0% of each run, Pallas kernels for 0% -> 0%
where the time goes in v2:
time: 59.6 us; the launch traced here: 59.1 us
  blocking collectives  42.4 us (71%)
  Pallas kernels  8.04 us (13%)
  local copies, waits for them, and re-layouts  4.56 us (8%)
  starting transfers between devices  2.36 us (4%)
  waiting for transfers between devices  1.07 us (2%)
  between operations  0.67 us (1%)
    all_to_all x1, blocking collectives, windows_body(): lax.all_to_all(back, layer_axes, split_axis=0, concat_axis=0, tiled=True)  22 us
    all_to_all x1, blocking collectives, windows_body(): lax.all_to_all(outgoing, layer_axes, split_axis=0, concat_axis=0, tiled=T...  20.4 us
    pallas_call x4, Pallas kernels, call(): pl.pallas_call(lambda *refs: kernel(plan, *refs), out_shape=shapes, in_sp...  8.04 us
    unnamed x12, local copies, waits for them, and re-layouts  4.56 us
    ppermute x1, starting transfers between devices, windows_body(): inner = lax.ppermute(inner, every_axis, plan.swaps(0))  1.68 us
  transfers between devices with their start and end apart: 2, of which 1 were waited for; matrix products, arithmetic and copies ran while one was open for 0% of the time, Pallas kernels for 0%

profile of v2, /device:TPU:0, one launch (start us, length us, event | category | flops | bytes accessed | tf_op | source)
XLA Modules:
  0.0 59.1 jit_solution(10330342292935085987)
XLA Ops:
  0.6 0.0 copy-start.5
  0.6 0.6 %copy-done.5 = s32[32]{0:T(128)S(1)} copy-done((s32[32]{0:T(128)S(1)}, s32[32]{0:T(128)}, u32[]{:S(2)}) %copy-start.5) | copy-done | bytes 152
  1.3 0.0 copy-start
  1.3 1.0 %copy-done = f32[19,4,8,128]{3,2,1,0:T(8,128)S(1)} copy-done((f32[19,4,8,128]{3,2,1,0:T(8,128)S(1)}, f32[19,4,8,128]{3,2,1,0:T(8,128)}, u32[]{:S(2)}) %copy-start) | copy-done | bytes 311320
  2.3 0.0 copy-start.1
  2.3 0.8 %copy-done.1 = f32[3,32,128]{2,1,0:T(8,128)S(1)} copy-done((f32[3,32,128]{2,1,0:T(8,128)S(1)}, f32[3,32,128]{2,1,0:T(8,128)}, u32[]{:S(2)}) %copy-start.1) | copy-done | bytes 49176
  3.1 0.0 copy-start.2
  3.1 0.7 %copy-done.2 = f32[32,128]{1,0:T(8,128)S(1)} copy-done((f32[32,128]{1,0:T(8,128)S(1)}, f32[32,128]{1,0:T(8,128)}, u32[]{:S(2)}) %copy-start.2) | copy-done | bytes 16408
  3.8 0.0 copy-start.3
  3.8 0.7 %copy-done.3 = s32[32,128]{1,0:T(8,128)S(1)} copy-done((s32[32,128]{1,0:T(8,128)S(1)}, s32[32,128]{1,0:T(8,128)}, u32[]{:S(2)}) %copy-start.3) | copy-done | bytes 16408
  4.5 0.0 copy-start.4
  4.5 0.7 %copy-done.4 = s32[32,32]{1,0:T(8,128)S(1)} copy-done((s32[32,32]{1,0:T(8,128)S(1)}, s32[32,32]{1,0:T(8,128)}, u32[]{:S(2)}) %copy-start.4) | copy-done | bytes 4120
  5.2 0.2 shard_map.77
  5.4 20.4 %all_to_all.10.refs_0_ = f32[16,8,896]{2,1,0:T(8,128)S(1)} all-to-all(f32[16,8,896]{2,1,0:T(8,128)S(1)} %shard_map.77), channel_id=1, replica_groups=mesh['gx'=4,'gy'=4,'gz'=2] {'gx','gy'}, dimensions={0} | all-to-all | bytes 917504 | tf_op jit(solution)/shard_map/all_to_all | solution.py:605
  25.8 0.1 shard_map.78
  25.9 0.7 %collective-permute-start.1 = (f32[8,8,1024]{2,1,0:T(8,128)S(1)}, f32[8,8,1024]{2,1,0:T(8,128)S(1)}, u32[]{:S(2)}, u32[]{:S(2)}) collective-permute-start(f32[8,8,1024]{2,1,0:T(8,128)S(1)} %get-tuple-element.7), channel_id=1, source_target_pairs={{2,4},{4,2},{6,8},{8,6},{10,12},{12,10},{14,16},{16,14},{18,20},{2... | collective-permute-start | bytes 786440 | tf_op jit(solution)/shard_map/ppermute | solution.py:613
  26.6 1.7 %collective-permute-start = (f32[8,8,768]{2,1,0:T(8,128)S(1)}, f32[8,8,768]{2,1,0:T(8,128)S(1)}, u32[]{:S(2)}, u32[]{:S(2)}) collective-permute-start(f32[8,8,768]{2,1,0:T(8,128)S(1)} %get-tuple-element.6), channel_id=1, source_target_pairs={{0,2},{2,0},{4,6},{6,4},{8,10},{10,8},{12,14},{14,12},{16,18},{18,... | collective-permute-start | bytes 589832 | tf_op jit(solution)/shard_map/ppermute | solution.py:612
  28.3 1.1 %collective-permute-done.refs_1_ = f32[8,8,768]{2,1,0:T(8,128)S(1)} collective-permute-done((f32[8,8,768]{2,1,0:T(8,128)S(1)}, f32[8,8,768]{2,1,0:T(8,128)S(1)}, u32[]{:S(2)}, u32[]{:S(2)}) %collective-permute-start) | collective-permute-done | bytes 196640 | tf_op jit(solution)/shard_map/ppermute | solution.py:612
  29.3 0.0 collective-permute-done.1.refs_2_
  29.3 6.9 %shard_map.79 = f32[16,8,768]{2,1,0:T(8,128)S(1)} custom-call(f32[16,8,896]{2,1,0:T(8,128)S(1)} %all_to_all.10.refs_0_, f32[8,8,768]{2,1,0:T(8,128)S(1)} %collective-permute-done.refs_1_, f32[8,8,1024]{2,1,0:T(8,128)S(1)} %collective-permute-done.1.refs_2_), custom_call_target="tpu_custom_call" | custom-call | tf_op jit(solution)/shard_map/pallas_call | solution.py:583
  36.3 22.0 %all_to_all.11.refs_0_ = f32[16,8,768]{2,1,0:T(8,128)S(1)} all-to-all(f32[16,8,768]{2,1,0:T(8,128)S(1)} %shard_map.79), channel_id=1, replica_groups=mesh['gx'=4,'gy'=4,'gz'=2] {'gx','gy'}, dimensions={0} | all-to-all | bytes 786432 | tf_op jit(solution)/shard_map/all_to_all | solution.py:629
  58.2 0.9 %shard_map.80 = (f32[608,128]{1,0:T(8,128)}, f32[96,128]{1,0:T(8,128)}) custom-call(f32[16,8,768]{2,1,0:T(8,128)S(1)} %all_to_all.11.refs_0_), custom_call_target="tpu_custom_call" | custom-call | tf_op jit(solution)/shard_map/pallas_call | solution.py:583
Async XLA Ops:
  0.6 0.7 %copy-start.5 = (s32[32]{0:T(128)S(1)}, s32[32]{0:T(128)}, u32[]{:S(2)}) copy-start(s32[32]{0:T(128)} %param.11) | copy-start | bytes 388
  1.3 1.0 %copy-start = (f32[19,4,8,128]{3,2,1,0:T(8,128)S(1)}, f32[19,4,8,128]{3,2,1,0:T(8,128)}, u32[]{:S(2)}) copy-start(f32[19,4,8,128]{3,2,1,0:T(8,128)} %param.6) | copy-start | bytes 933892
  2.3 0.8 %copy-start.1 = (f32[3,32,128]{2,1,0:T(8,128)S(1)}, f32[3,32,128]{2,1,0:T(8,128)}, u32[]{:S(2)}) copy-start(f32[3,32,128]{2,1,0:T(8,128)} %param.7) | copy-start | bytes 147460
  3.1 0.7 %copy-start.2 = (f32[32,128]{1,0:T(8,128)S(1)}, f32[32,128]{1,0:T(8,128)}, u32[]{:S(2)}) copy-start(f32[32,128]{1,0:T(8,128)} %refs_2_.1) | copy-start | bytes 49156
  3.8 0.7 %copy-start.3 = (s32[32,128]{1,0:T(8,128)S(1)}, s32[32,128]{1,0:T(8,128)}, u32[]{:S(2)}) copy-start(s32[32,128]{1,0:T(8,128)} %refs_3_.1) | copy-start | bytes 49156
  4.5 0.7 %copy-start.4 = (s32[32,32]{1,0:T(8,128)S(1)}, s32[32,32]{1,0:T(8,128)}, u32[]{:S(2)}) copy-start(s32[32,32]{1,0:T(8,128)} %refs_4_.1) | copy-start | bytes 12292
  25.9 3.4 %collective-permute-start.1 = (f32[8,8,1024]{2,1,0:T(8,128)S(1)}, f32[8,8,1024]{2,1,0:T(8,128)S(1)}, u32[]{:S(2)}, u32[]{:S(2)}) collective-permute-start(f32[8,8,1024]{2,1,0:T(8,128)S(1)} %get-tuple-element.7), channel_id=1, source_target_pairs={{2,4},{4,2},{6,8},{8,6},{10,12},{12,10},{14,16},{16,14},{18,20},{2... | collective-permute-start | bytes 786440 | tf_op jit(solution)/shard_map/ppermute | solution.py:613
  26.6 2.7 %collective-permute-start = (f32[8,8,768]{2,1,0:T(8,128)S(1)}, f32[8,8,768]{2,1,0:T(8,128)S(1)}, u32[]{:S(2)}, u32[]{:S(2)}) collective-permute-start(f32[8,8,768]{2,1,0:T(8,128)S(1)} %get-tuple-element.6), channel_id=1, source_target_pairs={{0,2},{2,0},{4,6},{6,4},{8,10},{10,8},{12,14},{14,12},{16,18},{18,... | collective-permute-start | bytes 589832 | tf_op jit(solution)/shard_map/ppermute | solution.py:612

commit v3 on v2

--- a/solution.py
+++ b/solution.py
@@ -220,6 +220,7 @@
 SUBLANES = 8
 VMEM_LIMIT = 24 * 1024 * 1024
 VMEM = pl.BlockSpec(memory_space=pltpu.VMEM)
+HBM = pl.BlockSpec(memory_space=pltpu.HBM)
 FIELD_V = (19, 21, 22)
 FIELD_CELL = 20
 FIELD_RATE = 23
@@ -257,11 +258,15 @@
             and self.per_tile == self.n_gy
         )
 
+    def along(self, window):
+        gx, r = divmod(window, self.n_gy)
+        return gx * self.n_gy + (self.n_gy - 1 - r if gx % 2 else r)
+
     def device(self, window):
-        layer, place = divmod(window, self.sources)
+        layer, local = divmod(window, self.sources)
         if layer % 2:
-            place = self.sources - 1 - place
-        return place * self.n_gz + layer
+            local = self.sources - 1 - local
+        return self.along(local) * self.n_gz + layer
 
     def swaps(self, start):
         count = self.n_gz * self.sources
@@ -273,35 +278,56 @@
         return [(self.device(a), self.device(b)) for a, b in paired]
 
     def place(self):
-        layer = lax.axis_index("gz")
-        here = lax.axis_index("gx") * self.n_gy + lax.axis_index("gy")
-        return jnp.where(lax.rem(layer, 2) == 1, self.sources - 1 - here, here), layer
+        gx, gy, layer = (lax.axis_index(name) for name in ("gx", "gy", "gz"))
+        local = gx * self.n_gy + jnp.where(lax.rem(gx, 2) == 1, self.n_gy - 1 - gy, gy)
+        return jnp.where(lax.rem(layer, 2) == 1, self.sources - 1 - local, local), layer
 
     def holder(self, window):
-        layer = lax.axis_index("gz")
-        return jnp.where(lax.rem(layer, 2) == 1, self.sources - 1 - window, window)
-
-
-def swap_groups(parts, group):
-    parts = list(parts)
-    lane = lax.broadcasted_iota(jnp.int32, parts[0].shape, 1)
-    step = len(parts) // 2
+        odd = lax.rem(lax.axis_index("gz"), 2) == 1
+        return jnp.where(odd, self.along(self.sources - 1 - window), self.along(window))
+
+
+def swap_groups(sets, group):
+    sets = [list(parts) for parts in sets]
+    count = len(sets[0])
+    lane = lax.broadcasted_iota(jnp.int32, sets[0][0].shape, 1)
+    step = count // 2
     while step:
         low = lane // (group * step) % 2 == 0
-        for a in range(len(parts)):
+        shift = group * step
+        for a in range(count):
             if a // step % 2 == 0:
-                first, second = parts[a], parts[a + step]
-                shift = group * step
-                parts[a] = jnp.where(low, first, pltpu.roll(second, shift, 1))
-                parts[a + step] = jnp.where(low, pltpu.roll(first, LANES - shift, 1), second)
+                for parts in sets:
+                    first, second = parts[a], parts[a + step]
+                    parts[a] = jnp.where(low, first, pltpu.roll(second, shift, 1))
+                    parts[a + step] = jnp.where(low, pltpu.roll(first, LANES - shift, 1), second)
         step //= 2
-    return parts
-
-
-def prepare_kernel(plan, pop_ref, vel_ref, vol_ref, slot_ref, link_ref, cell_ref, out_ref):
+    return sets
+
+
+def prepare_kernel(plan, pop_ref, vel_ref, vol_ref, slot_ref, link_ref, cell_ref, out_ref,
+                   pops, slots, links, cells, sems):
     group, bins, own = plan.group, plan.bins, plan.own
     whole = 19 * group // LANES
-    cell = cell_ref[...]
+    rest = 19 * group - whole * LANES
+    end = whole * LANES + 2 * LANES
+    moves = [
+        (cell_ref, cells),
+        (link_ref, links),
+        (slot_ref, slots),
+        (vol_ref, pops.at[end - bins : end]),
+        (vel_ref.at[bins:], pops.at[end - 3 * bins : end - bins]),
+        (vel_ref.at[:bins], pops.at[whole * LANES + rest : (whole + 1) * LANES]),
+        (pop_ref.at[whole * LANES :], pops.at[whole * LANES : whole * LANES + rest]),
+    ]
+    moves += [(pop_ref.at[t * LANES : (t + 1) * LANES], pops.at[t * LANES : (t + 1) * LANES]) for t in range(whole)]
+    copies = [pltpu.make_async_copy(a, b, sems.at[i]) for i, (a, b) in enumerate(moves)]
+    for copy in copies:
+        copy.start()
+    for copy in copies[:7]:
+        copy.wait()
+
+    cell = cells[...]
     width_y = plan.dy * plan.n_gy
     xcell = lax.div(cell, width_y * plan.n_gz)
     ycell = lax.rem(lax.div(cell, plan.n_gz), width_y)
@@ -309,26 +335,27 @@
     cell = source * group + lax.rem(xcell, plan.dx) * plan.dy + lax.rem(ycell, plan.dy)
     cell = jnp.concatenate([cell.astype(jnp.float32), jnp.zeros((1, LANES - bins), jnp.float32)], axis=1)
     packed = jnp.concatenate(
-        [link_ref[g * SUBLANES : (g + 1) * SUBLANES, :].astype(jnp.float32) for g in range(bins // SUBLANES)],
+        [links[g * SUBLANES : (g + 1) * SUBLANES, :].astype(jnp.float32) for g in range(bins // SUBLANES)],
         axis=1,
     )
     holders = [plan.holder(q) for q in range(plan.sources)]
-    for t in range(plan.tiles):
+    for q in range(plan.sources):
+        out_ref[q, :, plan.width :] = packed
+    for t in (whole, whole + 1, *range(whole)):
         if t < whole:
-            block = pop_ref[t * LANES : (t + 1) * LANES, :]
+            copies[7 + t].wait()
+            block = pops[t * LANES : (t + 1) * LANES, :]
         elif t == whole:
-            block = jnp.concatenate([pop_ref[whole * LANES :, :], vel_ref[:bins, :]], axis=0)
+            block = pops[whole * LANES : (whole + 1) * LANES, :]
         else:
-            rate = vol_ref[...] * slot_ref[...].astype(jnp.float32)
-            block = jnp.concatenate([rate, vel_ref[bins:, :], rate], axis=0)
+            rate = pops[end - bins : end, :] * slots[...].astype(jnp.float32)
+            block = jnp.concatenate([rate, pops[end - 3 * bins : end - bins, :], rate], axis=0)
         block = block.T
         if t == plan.tiles - 1:
             lane = lax.broadcasted_iota(jnp.int32, block.shape, 1)
             block = jnp.where(lane < bins, cell, block)
         for q in range(plan.sources):
             out_ref[holders[q], :, t * LANES : (t + 1) * LANES] = block[q * own : (q + 1) * own, :]
-    for q in range(plan.sources):
-        out_ref[q, :, plan.width :] = packed
 
 
 def edges_kernel(plan, in_ref, inner_ref, outer_ref):
@@ -364,8 +391,41 @@
     ]
 
 
-def substeps_kernel(plan, in_ref, inner_ref, outer_ref, out_ref, f_ref, post_ref, u_ref, force_ref, v_ref,
-                    aux_ref, column_ref, link_ref):
+def bins_on_columns(columns, cells):
+    which = lax.broadcasted_iota(jnp.int32, (columns, columns), 0).astype(jnp.float32)
+    return (which == cells).astype(jnp.float32).astype(jnp.bfloat16)
+
+
+def contact_blocks(plan, packed, link_ref):
+    group, per = plan.group, plan.per_tile
+    lane = lax.broadcasted_iota(jnp.int32, (SUBLANES, LANES), 1)
+    for s in range(plan.sources):
+        place = s % per
+        tile = packed(s)
+        pieces = []
+        for g in range(per):
+            moved = tile if g == place else pltpu.roll(tile, (place - g) * group % LANES, 1)
+            pieces.append(jnp.where(lane // group == place, moved, 0.0))
+        link_ref[s * group : (s + 1) * group, :] = jnp.concatenate(pieces, axis=0).astype(jnp.bfloat16)
+
+
+def unpack(plan, tile_of, state_ref, rows):
+    per = plan.per_tile
+    for t in range(plan.tiles):
+        sets = [[tile_of(s, t) for s in range(q, q + per)] for q in range(0, plan.sources, per)]
+        for q, parts in enumerate(swap_groups(sets, plan.group)):
+            for j, part in enumerate(parts):
+                state_ref[t * per + j, rows, q * LANES : (q + 1) * LANES] = part
+
+
+def settle_kernel(plan, in_ref, state_ref, column_ref, link_ref):
+    unpack(plan, lambda s, t: in_ref[s, :, t * LANES : (t + 1) * LANES], state_ref, slice(0, plan.own))
+    column_ref[...] = bins_on_columns(plan.columns, state_ref[FIELD_CELL, 0:1, :])
+    contact_blocks(plan, lambda s: in_ref[s, :, plan.width :], link_ref)
+
+
+def substeps_kernel(plan, settled_ref, column_ref, link_ref, inner_ref, outer_ref, out_ref, state_ref,
+                    post_ref, u_ref, force_ref, count_ref, other_column_ref, other_link_ref):
     rows, columns, group, per = plan.rows, plan.columns, plan.group, plan.per_tile
     halo, own, dx, dy = plan.halo, plan.own, plan.dx, plan.dy
     quads = plan.sources // per
@@ -375,95 +435,64 @@
     ground, ceiling = first & (layer == 0), last & (layer == plan.n_gz - 1)
     tile_row = lax.broadcasted_iota(jnp.int32, (SUBLANES, LANES), 0)
 
-    def store(field, lanes, part):
-        if field < 19:
-            f_ref[field, :, lanes] = part
-        elif field in FIELD_V:
-            v_ref[FIELD_V.index(field), :, lanes] = part
+    def halo_tile(s, t):
+        at = slice(t * LANES, (t + 1) * LANES)
+        inner, outer = inner_ref[s // 2, :, at], outer_ref[s // 2, :, at]
+        below = jnp.where(even, outer, inner)
+        above = jnp.where(even, inner, outer)
+        if s % 2:
+            above = pltpu.roll(above, halo, 0)
         else:
-            aux_ref[0 if field == FIELD_RATE else 1, :, lanes] = part
-
-    for t in range(plan.tiles):
-        at = slice(t * LANES, (t + 1) * LANES)
-        for q in range(quads):
-            parts = []
-            for s in range(q * per, (q + 1) * per):
-                inner, outer = inner_ref[s // 2, :, at], outer_ref[s // 2, :, at]
-                below = jnp.where(even, outer, inner)
-                above = jnp.where(even, inner, outer)
-                if s % 2:
-                    below = pltpu.roll(below, halo, 0)
-                else:
-                    above = pltpu.roll(above, halo, 0)
-                turned = pltpu.roll(in_ref[s, :, at], halo, 0)
-                parts.append(
-                    jnp.concatenate(
-                        [jnp.where(tile_row < halo, below, turned), jnp.where(tile_row < halo, turned, above)],
-                        axis=0,
-                    )
-                )
-            lanes = slice(q * LANES, (q + 1) * LANES)
-            for j, part in enumerate(swap_groups(parts, group)):
-                store(t * per + j, lanes, part)
-
-    rate = aux_ref[0]
-    live = (rate > 0.0).astype(jnp.float32)
-    cells = aux_ref[1]
-    other_cells = jnp.where(first, cells[0:1, :], cells[rows - 1 : rows, :])
-    which = lax.broadcasted_iota(jnp.int32, (columns, columns), 0).astype(jnp.float32)
-    for k, chosen in enumerate((cells[halo : halo + 1, :], other_cells)):
-        column_ref[k] = (which == chosen).astype(jnp.float32).astype(jnp.bfloat16)
-    lane = lax.broadcasted_iota(jnp.int32, (SUBLANES, LANES), 1)
-    for k in range(2):
-        for s in range(plan.sources):
-            if k == 0:
-                packed = in_ref[s, :, plan.width :]
-            else:
-                start = plan.width + s % 2 * LANES
-                packed = outer_ref[s // 2, :, start : start + LANES]
-            place = s % per
-            pieces = []
-            for g in range(per):
-                moved = packed if g == place else pltpu.roll(packed, (place - g) * group % LANES, 1)
-                pieces.append(jnp.where(lane // group == place, moved, 0.0))
-            link_ref[k, s * group : (s + 1) * group, :] = jnp.concatenate(pieces, axis=0).astype(jnp.bfloat16)
-
-    row = lax.broadcasted_iota(jnp.int32, (rows, columns), 0)
-    tile_rows = lax.broadcasted_iota(jnp.int32, (SUBLANES, columns), 0)
-    below_foreign = first & (tile_rows < halo)
-    above_foreign = last & (tile_rows >= halo)
-
-    def both_layers(parts, product):
-        mine = product(parts, 0)
-        others = product([jnp.where(first, x[:SUBLANES], x[SUBLANES:]) for x in parts], 1)
+            below = pltpu.roll(below, halo, 0)
+        return jnp.where(tile_row < halo, above, below)
+
+    unpack(plan, halo_tile, state_ref, slice(own, rows))
+    other_cells = jnp.where(first, state_ref[FIELD_CELL, rows - 1 : rows, :], state_ref[FIELD_CELL, own : own + 1, :])
+    other_column_ref[...] = bins_on_columns(columns, other_cells)
+
+    def other_contacts(s):
+        start = plan.width + s % 2 * LANES
+        return outer_ref[s // 2, :, start : start + LANES]
+
+    contact_blocks(plan, other_contacts, other_link_ref)
+
+    halo_row = lax.broadcasted_iota(jnp.int32, (SUBLANES, columns), 0)
+    foreign = (last & (halo_row < halo)) | (first & (halo_row >= halo))
+
+    def both_layers(parts, product, own_matrix, other_matrix):
+        mine = product(parts, own_matrix)
+        others = product([x[own:] for x in parts], other_matrix)
         return [
-            jnp.concatenate(
-                [jnp.where(below_foreign, b, a[:SUBLANES]), jnp.where(above_foreign, b, a[SUBLANES:])], axis=0
-            )
-            for a, b in zip(mine, others)
+            jnp.concatenate([a[:own], jnp.where(foreign, b, a[own:])], axis=0) for a, b in zip(mine, others)
         ]
 
-    def to_bins(parts, k):
-        return two_part_dot(parts, column_ref[k], 0)
-
-    def to_columns(parts, k):
-        return two_part_dot(parts, column_ref[k], 1)
-
-    def near(parts, k):
+    def to_bins(parts):
+        return both_layers(parts, lambda x, m: two_part_dot(x, m[...], 0), column_ref, other_column_ref)
+
+    def to_columns(parts):
+        return both_layers(parts, lambda x, m: two_part_dot(x, m[...], 1), column_ref, other_column_ref)
+
+    def touching(parts, matrix):
         blocks = [
             two_part_dot(
-                [x[:, q * LANES : (q + 1) * LANES] for x in parts], link_ref[k, q * LANES : (q + 1) * LANES, :], 1
+                [x[:, q * LANES : (q + 1) * LANES] for x in parts], matrix[q * LANES : (q + 1) * LANES, :], 1
             )
             for q in range(quads)
         ]
         return [jnp.concatenate([b[i] for b in blocks], axis=1) for i in range(len(parts))]
 
-    force_ref[3] = both_layers([rate], to_columns)[0]
-    aux_ref[1] = both_layers([live], near)[0]
-
-    wide_lane = lax.broadcasted_iota(jnp.int32, (rows, LANES), 1)
-    lane_y = lax.div(wide_lane, group) * dy + lax.rem(wide_lane, dy)
-    lane_x = lax.rem(lax.div(wide_lane, dy), dx)
+    def near(parts):
+        return both_layers(parts, touching, link_ref, other_link_ref)
+
+    rate = state_ref[FIELD_RATE]
+    force_ref[3] = 1.0 / (1.0 + to_columns([rate])[0])
+    count_ref[...] = near([(rate > 0.0).astype(jnp.float32)])[0]
+
+    lane = lax.broadcasted_iota(jnp.int32, (rows, LANES), 1)
+    row = lax.broadcasted_iota(jnp.int32, (rows, LANES), 0)
+    lane_y = lax.div(lane, group) * dy + lax.rem(lane, dy)
+    lane_x = lax.rem(lax.div(lane, dy), dx)
+    bottom, top = ground & (row == 0), ceiling & (row == own - 1)
 
     def source_lanes(cx, cy):
         y = lax.rem(lane_y - cy + plan.n_gy * dy, plan.n_gy * dy)
@@ -473,53 +502,56 @@
     def step(_, carry):
         for q in range(quads):
             lanes = slice(q * LANES, (q + 1) * LANES)
-            popul = [f_ref[i, :, lanes] for i in range(19)]
+            popul = [state_ref[i, :, lanes] for i in range(19)]
             density = popul[0]
             for i in range(1, 19):
                 density = density + popul[i]
+            inverse = 1.0 / density
             u_ref[3, :, lanes] = density
+            u_ref[4, :, lanes] = inverse
             for a in range(3):
                 rising = [popul[i] for i in range(19) if VELOCITIES[i, a] == 1]
                 falling = [popul[i] for i in range(19) if VELOCITIES[i, a] == -1]
-                u_ref[a, :, lanes] = (sum(rising[1:], rising[0]) - sum(falling[1:], falling[0])) / density
-        rate = aux_ref[0]
-        count = aux_ref[1]
+                u_ref[a, :, lanes] = (sum(rising[1:], rising[0]) - sum(falling[1:], falling[0])) * inverse
+        rate = state_ref[FIELD_RATE]
         live = (rate > 0.0).astype(jnp.float32)
-        velocity = [v_ref[a] for a in range(3)]
-        speed = both_layers([u_ref[a] for a in range(3)], to_bins)
+        velocity = [state_ref[field] for field in FIELD_V]
+        speed = to_bins([u_ref[a] for a in range(3)])
         drags = [drag_factor * rate * (speed[a] - velocity[a]) for a in range(3)]
-        for a, force in enumerate(both_layers([-d for d in drags], to_columns)):
+        for a, force in enumerate(to_columns(drags)):
             force_ref[a] = force
-        touching = both_layers([velocity[a] * live for a in range(3)], near)
+        moving = near([velocity[a] * live for a in range(3)])
+        count = count_ref[...]
         for a in range(3):
-            push = contact_stiffness * live * (touching[a] - count * velocity[a])
+            push = contact_stiffness * live * (moving[a] - count * velocity[a])
             updated = velocity[a] + drags[a] + push
             if a == 2:
                 updated = updated - gravity * live
-            v_ref[a] = updated
+            state_ref[FIELD_V[a]] = updated
+        keep, take = 1.0 - 1.0 / relax_time, 1.0 / relax_time
         for q in range(quads):
             lanes = slice(q * LANES, (q + 1) * LANES)
-            density = u_ref[3, :, lanes]
-            scale = 1.0 / (1.0 + force_ref[3, :, lanes])
-            target = [
-                scale * (u_ref[a, :, lanes] + relax_time * force_ref[a, :, lanes] / density)
-                for a in range(3)
-            ]
+            density, inverse = u_ref[3, :, lanes], u_ref[4, :, lanes]
+            scale = force_ref[3, :, lanes]
+            share = relax_time * inverse
+            target = [scale * (u_ref[a, :, lanes] - share * force_ref[a, :, lanes]) for a in range(3)]
             square = target[0] * target[0] + target[1] * target[1] + target[2] * target[2]
             base = 1.0 - 1.5 * square
-            for i in range(19):
+            triple = [3.0 * x for x in target]
+            shares = {w: (take * float(w)) * density for w in sorted(set(WEIGHTS))}
+            post_ref[0, :, lanes] = keep * state_ref[0, :, lanes] + shares[WEIGHTS[0]] * base
+            for i in range(1, 19, 2):
                 along = None
                 for a in range(3):
                     if VELOCITIES[i, a] != 0:
-                        term = target[a] if VELOCITIES[i, a] == 1 else -target[a]
-                        along = term if along is None else along + term
-                shape = base if along is None else base + along * (3.0 + 4.5 * along)
-                equil = (float(WEIGHTS[i]) * density) * shape
-                popul = f_ref[i, :, lanes]
-                post_ref[i, :, lanes] = popul - (popul - equil) * (1.0 / relax_time)
-        small_row = lax.broadcasted_iota(jnp.int32, (rows, LANES), 0)
-        bottom = ground & (small_row == halo)
-        top = ceiling & (small_row == halo + own - 1)
+                        if along is None:
+                            along = triple[a] if VELOCITIES[i, a] == 1 else -triple[a]
+                        else:
+                            along = along + triple[a] if VELOCITIES[i, a] == 1 else along - triple[a]
+                level = base + 0.5 * (along * along)
+                share_i = shares[WEIGHTS[i]]
+                post_ref[i, :, lanes] = keep * state_ref[i, :, lanes] + share_i * (level + along)
+                post_ref[i + 1, :, lanes] = keep * state_ref[i + 1, :, lanes] + share_i * (level - along)
         for i in range(19):
             cx, cy, cz = (int(c) for c in VELOCITIES[i])
             moved = [post_ref[i, :, q * LANES : (q + 1) * LANES] for q in range(quads)]
@@ -535,63 +567,69 @@
                 if cz:
                     x = pltpu.roll(x, cz % rows, 0)
                     x = jnp.where(bottom if cz == 1 else top, post_ref[OPPOSITE[i], :, lanes], x)
-                f_ref[i, :, lanes] = x
+                state_ref[i, :, lanes] = x
         return carry
 
     lax.fori_loop(0, SUBSTEPS, step, 0)
 
     for t in range(plan.tiles):
-        for q in range(quads):
-            lanes = slice(q * LANES, (q + 1) * LANES)
-            parts = []
-            for field in range(t * per, (t + 1) * per):
-                if field < 19:
-                    part = f_ref[field, halo : halo + own, lanes]
-                elif field in FIELD_V:
-                    part = v_ref[FIELD_V.index(field), halo : halo + own, lanes]
-                else:
-                    part = jnp.zeros((own, LANES), jnp.float32)
-                parts.append(part)
-            for s, part in enumerate(swap_groups(parts, group)):
+        sets = [
+            [state_ref[t * per + j, 0:own, q * LANES : (q + 1) * LANES] for j in range(per)] for q in range(quads)
+        ]
+        for q, parts in enumerate(swap_groups(sets, group)):
+            for s, part in enumerate(parts):
                 out_ref[q * per + s, :, t * LANES : (t + 1) * LANES] = part
 
 
-def finish_kernel(plan, in_ref, pop_ref, vel_ref):
+def finish_kernel(plan, in_ref, pop_ref, vel_ref, stage, sems):
     bins = plan.bins
     whole = 19 * plan.group // LANES
     rest = 19 * plan.group - whole * LANES
     holders = [plan.holder(q) for q in range(plan.sources)]
+    copies = []
+
+    def send(start, size, target):
+        copies.append(pltpu.make_async_copy(stage.at[start : start + size], target, sems.at[len(copies)]))
+        copies[-1].start()
+
     for t in range(plan.tiles):
         at = slice(t * LANES, (t + 1) * LANES)
-        block = jnp.concatenate([in_ref[holders[q], :, at] for q in range(plan.sources)], axis=0).T
+        start = t * LANES
+        stage[at, :] = jnp.concatenate([in_ref[holders[q], :, at] for q in range(plan.sources)], axis=0).T
         if t < whole:
-            pop_ref[t * LANES : (t + 1) * LANES, :] = block
+            send(start, LANES, pop_ref.at[at])
         elif t == whole:
-            pop_ref[whole * LANES :, :] = block[:rest, :]
-            vel_ref[:bins, :] = block[rest:, :]
+            send(start, rest, pop_ref.at[start:])
+            send(start + rest, bins, vel_ref.at[:bins])
         else:
-            vel_ref[bins:, :] = block[bins : 3 * bins, :]
+            send(start + bins, 2 * bins, vel_ref.at[bins:])
+    for copy in copies:
+        copy.wait()
 
 
 def windows_body(plan, populations, grain_velocity, grain_volume, slots, contacts, bin_cell):
     group, bins, sources = plan.group, plan.bins, plan.sources
     rows, columns, own = plan.rows, plan.columns, plan.own
-    f32 = jnp.float32
-
-    def call(kernel, shapes, inputs, scratch=()):
-        shapes = [jax.ShapeDtypeStruct(shape, f32) for shape in shapes]
+    f32, bf16, i32 = jnp.float32, jnp.bfloat16, jnp.int32
+    half = sources // 2
+
+    def call(kernel, shapes, inputs, scratch=(), where=(VMEM, VMEM), aliases=None):
+        if where[0] is HBM:
+            inputs = [pltpu.with_memory_space_constraint(x, pltpu.HBM) for x in inputs]
+        shapes = [jax.ShapeDtypeStruct(shape, kind) for shape, kind in shapes]
         return pl.pallas_call(
             lambda *refs: kernel(plan, *refs),
             out_shape=shapes,
-            in_specs=[VMEM] * len(inputs),
-            out_specs=[VMEM] * len(shapes),
+            in_specs=[where[0]] * len(inputs),
+            out_specs=[where[1]] * len(shapes),
             scratch_shapes=list(scratch),
+            input_output_aliases=aliases or {},
             compiler_params=pltpu.CompilerParams(vmem_limit_bytes=VMEM_LIMIT),
         )(*inputs)
 
     (outgoing,) = call(
         prepare_kernel,
-        [(sources, own, plan.wide)],
+        [((sources, own, plan.wide), f32)],
         (
             populations.reshape(19 * group, LANES),
             grain_velocity.reshape(3 * bins, LANES),
@@ -600,37 +638,50 @@
             contacts,
             bin_cell.reshape(1, bins),
         ),
+        (
+            pltpu.VMEM((plan.width, LANES), f32),
+            pltpu.VMEM((bins, LANES), i32),
+            pltpu.VMEM((bins, bins), i32),
+            pltpu.VMEM((1, bins), i32),
+            pltpu.SemaphoreType.DMA((16,)),
+        ),
+        (HBM, VMEM),
     )
     layer_axes, every_axis = ("gx", "gy"), ("gx", "gy", "gz")
     incoming = lax.all_to_all(outgoing, layer_axes, split_axis=0, concat_axis=0, tiled=True)
-    half = sources // 2
     inner, outer = call(
         edges_kernel,
-        [(half, SUBLANES, plan.width), (half, SUBLANES, plan.width + 2 * LANES)],
+        [((half, SUBLANES, plan.width), f32), ((half, SUBLANES, plan.width + 2 * LANES), f32)],
         (incoming,),
     )
     inner = lax.ppermute(inner, every_axis, plan.swaps(0))
     outer = lax.ppermute(outer, every_axis, plan.swaps(1))
-    (back,) = call(
+    state, column, link = call(
+        settle_kernel,
+        [((plan.fields, rows, columns), f32), ((columns, columns), bf16), ((columns, LANES), bf16)],
+        (incoming,),
+    )
+    back, _ = call(
         substeps_kernel,
-        [(sources, own, plan.width)],
-        (incoming, inner, outer),
+        [((sources, own, plan.width), f32), ((plan.fields, rows, columns), f32)],
+        (state, column, link, inner, outer),
         (
             pltpu.VMEM((19, rows, columns), f32),
-            pltpu.VMEM((19, rows, columns), f32),
+            pltpu.VMEM((5, rows, columns), f32),
             pltpu.VMEM((4, rows, columns), f32),
-            pltpu.VMEM((4, rows, columns), f32),
-            pltpu.VMEM((3, rows, columns), f32),
-            pltpu.VMEM((2, rows, columns), f32),
-            pltpu.VMEM((2, columns, columns), jnp.bfloat16),
-            pltpu.VMEM((2, columns, LANES), jnp.bfloat16),
+            pltpu.VMEM((rows, columns), f32),
+            pltpu.VMEM((columns, columns), bf16),
+            pltpu.VMEM((columns, LANES), bf16),
         ),
+        aliases={0: 1},
     )
     result = lax.all_to_all(back, layer_axes, split_axis=0, concat_axis=0, tiled=True)
     fluid, velocity = call(
         finish_kernel,
-        [(19 * group, LANES), (3 * bins, LANES)],
+        [((19 * group, LANES), f32), ((3 * bins, LANES), f32)],
         (result,),
+        (pltpu.VMEM((plan.width, LANES), f32), pltpu.SemaphoreType.DMA((16,))),
+        (VMEM, HBM),
     )
     return (fluid.reshape(populations.shape), velocity.reshape(grain_velocity.shape))
 

time: 59.6 us -> 52.6 us (0.88)
  local copies, waits for them, and re-layouts: 4.56 us -> 0 us
  blocking collectives: 42.4 us -> 40.7 us
  waiting for transfers between devices: 1.07 us -> 0.38 us
    unnamed x12 -> x0, local copies, waits for them, and re-layouts: 4.56 us -> none
    all_to_all x1, blocking collectives: 22 us -> 20.2 us  [windows_body(): lax.all_to_all(back, layer_axes, split_axis=0, concat_axis=0, tiled=True)]
    ppermute x1, waiting for transfers between devices: 1.07 us -> 0.38 us  [windows_body(): inner = lax.ppermute(inner, every_axis, plan.swaps(0))]
    pallas_call x4 -> x5, Pallas kernels: 8.04 us -> 8.28 us  [call(): pl.pallas_call(lambda *refs: kernel(plan, *refs), out_shape=shapes, in_sp...]
  transfers between devices with their start and end apart: 2 -> 2, of which waited for: 1 -> 1; matrix products, arithmetic and copies ran while one was open for 0% -> 0% of each run, Pallas kernels for 0% -> 1%
where the time goes in v3:
time: 52.6 us; the launch traced here: 52.4 us
  blocking collectives  40.7 us (77%)
  Pallas kernels  8.28 us (16%)
  starting transfers between devices  2.36 us (4%)
  between operations  0.67 us (1%)
    all_to_all x1, blocking collectives, windows_body(): lax.all_to_all(outgoing, layer_axes, split_axis=0, concat_axis=0, tiled=T...  20.4 us
    all_to_all x1, blocking collectives, windows_body(): lax.all_to_all(back, layer_axes, split_axis=0, concat_axis=0, tiled=True)  20.2 us
    pallas_call x5, Pallas kernels, call(): pl.pallas_call(lambda *refs: kernel(plan, *refs), out_shape=shapes, in_sp...  8.28 us
    ppermute x1, starting transfers between devices, windows_body(): inner = lax.ppermute(inner, every_axis, plan.swaps(0))  1.68 us
  transfers between devices with their start and end apart: 2, of which 1 were waited for; matrix products, arithmetic and copies ran while one was open for 0% of the time, Pallas kernels for 1%

profile of v3, /device:TPU:0, one launch (start us, length us, event | category | flops | bytes accessed | tf_op | source)
XLA Modules:
  0.0 52.4 jit_solution(3429964733525573181)
XLA Ops:
  0.6 1.6 %shard_map.77 = f32[16,8,896]{2,1,0:T(8,128)S(1)} custom-call(f32[608,128]{1,0:T(8,128)} %bitcast.5, f32[96,128]{1,0:T(8,128)} %bitcast.6, f32[32,128]{1,0:T(8,128)} %refs_2_.1, s32[32,128]{1,0:T(8,128)} %refs_3_.1, s32[32,32]{1,0:T(8,128)} %refs_4_.1, s32[1,32]{1,0:T(1,128)} %bitcast.7), custom_call_target="tpu_custom_call" | custom-call | tf_op jit(solution)/shard_map/pallas_call | solution.py:620
  2.2 20.4 %all_to_all.10.refs_0_ = f32[16,8,896]{2,1,0:T(8,128)S(1)} all-to-all(f32[16,8,896]{2,1,0:T(8,128)S(1)} %shard_map.77), channel_id=1, replica_groups=mesh['gx'=4,'gy'=4,'gz'=2] {'gx','gy'}, dimensions={0} | all-to-all | bytes 917504 | tf_op jit(solution)/shard_map/all_to_all | solution.py:651
  22.6 0.1 shard_map.79
  22.7 0.7 %collective-permute-start.1 = (f32[8,8,1024]{2,1,0:T(8,128)S(1)}, f32[8,8,1024]{2,1,0:T(8,128)S(1)}, u32[]{:S(2)}, u32[]{:S(2)}) collective-permute-start(f32[8,8,1024]{2,1,0:T(8,128)S(1)} %get-tuple-element.14), channel_id=1, source_target_pairs={{2,4},{4,2},{6,14},{14,6},{12,10},{10,12},{8,16},{16,8},{18,20},{2... | collective-permute-start | bytes 786440 | tf_op jit(solution)/shard_map/ppermute | solution.py:658
  23.4 1.7 %collective-permute-start = (f32[8,8,768]{2,1,0:T(8,128)S(1)}, f32[8,8,768]{2,1,0:T(8,128)S(1)}, u32[]{:S(2)}, u32[]{:S(2)}) collective-permute-start(f32[8,8,768]{2,1,0:T(8,128)S(1)} %get-tuple-element.13), channel_id=1, source_target_pairs={{0,2},{2,0},{4,6},{6,4},{14,12},{12,14},{10,8},{8,10},{16,18},{18,... | collective-permute-start | bytes 589832 | tf_op jit(solution)/shard_map/ppermute | solution.py:657
  25.1 0.7 %shard_map.78 = (f32[24,16,512]{2,1,0:T(8,128)S(1)}, bf16[512,512]{1,0:T(8,128)(2,1)S(1)}, bf16[512,128]{1,0:T(8,128)(2,1)S(1)}) custom-call(f32[16,8,896]{2,1,0:T(8,128)S(1)} %all_to_all.10.refs_0_), custom_call_target="tpu_custom_call" | custom-call | tf_op jit(solution)/shard_map/pallas_call | solution.py:620
  25.8 0.4 collective-permute-done.refs_3_
  26.1 0.0 collective-permute-done.1.refs_4_
  26.1 5.0 %shard_map.80 = (f32[16,8,768]{2,1,0:T(8,128)S(1)}, f32[24,16,512]{2,1,0:T(8,128)S(1)}) custom-call(f32[24,16,512]{2,1,0:T(8,128)S(1)} %get-tuple-element.10.refs_0_, bf16[512,512]{1,0:T(8,128)(2,1)S(1)} %get-tuple-element.11.refs_1_, bf16[512,128]{1,0:T(8,128)(2,1)S(1)} %get-tuple-element.12.refs_2_, ...), custom_call_target="tpu_custom_call", output_to_operand_aliasing={{1}: (0, {})} | custom-call | tf_op jit(solution)/shard_map/pallas_call | solution.py:620
  31.1 20.2 %all_to_all.11.refs_0_ = f32[16,8,768]{2,1,0:T(8,128)S(1)} all-to-all(f32[16,8,768]{2,1,0:T(8,128)S(1)} %get-tuple-element.15), channel_id=1, replica_groups=mesh['gx'=4,'gy'=4,'gz'=2] {'gx','gy'}, dimensions={0} | all-to-all | bytes 786432 | tf_op jit(solution)/shard_map/all_to_all | solution.py:678
  51.4 1.0 %shard_map.81 = (f32[608,128]{1,0:T(8,128)}, f32[96,128]{1,0:T(8,128)}) custom-call(f32[16,8,768]{2,1,0:T(8,128)S(1)} %all_to_all.11.refs_0_), custom_call_target="tpu_custom_call" | custom-call | tf_op jit(solution)/shard_map/pallas_call | solution.py:620
Async XLA Ops:
  22.7 3.4 %collective-permute-start.1 = (f32[8,8,1024]{2,1,0:T(8,128)S(1)}, f32[8,8,1024]{2,1,0:T(8,128)S(1)}, u32[]{:S(2)}, u32[]{:S(2)}) collective-permute-start(f32[8,8,1024]{2,1,0:T(8,128)S(1)} %get-tuple-element.14), channel_id=1, source_target_pairs={{2,4},{4,2},{6,14},{14,6},{12,10},{10,12},{8,16},{16,8},{18,20},{2... | collective-permute-start | bytes 786440 | tf_op jit(solution)/shard_map/ppermute | solution.py:658
  23.4 2.7 %collective-permute-start = (f32[8,8,768]{2,1,0:T(8,128)S(1)}, f32[8,8,768]{2,1,0:T(8,128)S(1)}, u32[]{:S(2)}, u32[]{:S(2)}) collective-permute-start(f32[8,8,768]{2,1,0:T(8,128)S(1)} %get-tuple-element.13), channel_id=1, source_target_pairs={{0,2},{2,0},{4,6},{6,4},{14,12},{12,14},{10,8},{8,10},{16,18},{18,... | collective-permute-start | bytes 589832 | tf_op jit(solution)/shard_map/ppermute | solution.py:657

commit v4 on v3

--- a/solution.py
+++ b/solution.py
@@ -221,8 +221,8 @@
 VMEM_LIMIT = 24 * 1024 * 1024
 VMEM = pl.BlockSpec(memory_space=pltpu.VMEM)
 HBM = pl.BlockSpec(memory_space=pltpu.HBM)
-FIELD_V = (19, 21, 22)
-FIELD_CELL = 20
+FIELD_V = (19, 20, 21)
+FIELD_CELL = 22
 FIELD_RATE = 23
 
 
@@ -274,7 +274,7 @@
         for a in range(start, count - 1, 2):
             paired += [(a, a + 1), (a + 1, a)]
         if start:
-            paired += [(0, 0), (count - 1, count - 1)]
+            paired += [(0, count - 1), (count - 1, 0)]
         return [(self.device(a), self.device(b)) for a, b in paired]
 
     def place(self):
@@ -287,44 +287,51 @@
         return jnp.where(odd, self.along(self.sources - 1 - window), self.along(window))
 
 
+def pick(group, parts):
+    lane = lax.broadcasted_iota(jnp.int32, parts[0].shape, 1) // group
+    step = 1
+    while len(parts) > 1:
+        odd = lane // step % 2 == 1
+        parts = [jnp.where(odd, b, a) for a, b in zip(parts[::2], parts[1::2])]
+        step *= 2
+    return parts[0]
+
+
+def turned_groups(parts, group):
+    count = len(parts)
+    turned = []
+    for r in range(count):
+        chosen = pick(group, [parts[(g + r) % count] for g in range(count)])
+        turned.append(pltpu.roll(chosen, r * group, 1) if r else chosen)
+    return turned
+
+
 def swap_groups(sets, group):
-    sets = [list(parts) for parts in sets]
+    turned = [turned_groups(parts, group) for parts in sets]
     count = len(sets[0])
-    lane = lax.broadcasted_iota(jnp.int32, sets[0][0].shape, 1)
-    step = count // 2
-    while step:
-        low = lane // (group * step) % 2 == 0
-        shift = group * step
-        for a in range(count):
-            if a // step % 2 == 0:
-                for parts in sets:
-                    first, second = parts[a], parts[a + step]
-                    parts[a] = jnp.where(low, first, pltpu.roll(second, shift, 1))
-                    parts[a + step] = jnp.where(low, pltpu.roll(first, LANES - shift, 1), second)
-        step //= 2
-    return sets
+    return [[pick(group, [t[(g - j) % count] for g in range(count)]) for j in range(count)] for t in turned]
 
 
 def prepare_kernel(plan, pop_ref, vel_ref, vol_ref, slot_ref, link_ref, cell_ref, out_ref,
                    pops, slots, links, cells, sems):
     group, bins, own = plan.group, plan.bins, plan.own
     whole = 19 * group // LANES
-    rest = 19 * group - whole * LANES
-    end = whole * LANES + 2 * LANES
+    end = plan.width
+    vel_start = 19 * group
+    split = whole * LANES // 2
     moves = [
         (cell_ref, cells),
         (link_ref, links),
         (slot_ref, slots),
         (vol_ref, pops.at[end - bins : end]),
-        (vel_ref.at[bins:], pops.at[end - 3 * bins : end - bins]),
-        (vel_ref.at[:bins], pops.at[whole * LANES + rest : (whole + 1) * LANES]),
-        (pop_ref.at[whole * LANES :], pops.at[whole * LANES : whole * LANES + rest]),
+        (vel_ref, pops.at[vel_start : vel_start + 3 * bins]),
+        (pop_ref.at[split:], pops.at[split:vel_start]),
+        (pop_ref.at[:split], pops.at[:split]),
     ]
-    moves += [(pop_ref.at[t * LANES : (t + 1) * LANES], pops.at[t * LANES : (t + 1) * LANES]) for t in range(whole)]
     copies = [pltpu.make_async_copy(a, b, sems.at[i]) for i, (a, b) in enumerate(moves)]
     for copy in copies:
         copy.start()
-    for copy in copies[:7]:
+    for copy in copies:
         copy.wait()
 
     cell = cells[...]
@@ -333,7 +340,8 @@
     ycell = lax.rem(lax.div(cell, plan.n_gz), width_y)
     source = lax.div(xcell, plan.dx) * plan.n_gy + lax.div(ycell, plan.dy)
     cell = source * group + lax.rem(xcell, plan.dx) * plan.dy + lax.rem(ycell, plan.dy)
-    cell = jnp.concatenate([cell.astype(jnp.float32), jnp.zeros((1, LANES - bins), jnp.float32)], axis=1)
+    blank = jnp.zeros((1, bins), jnp.float32)
+    cell = jnp.concatenate([blank, blank, cell.astype(jnp.float32), blank], axis=1)
     packed = jnp.concatenate(
         [links[g * SUBLANES : (g + 1) * SUBLANES, :].astype(jnp.float32) for g in range(bins // SUBLANES)],
         axis=1,
@@ -341,19 +349,15 @@
     holders = [plan.holder(q) for q in range(plan.sources)]
     for q in range(plan.sources):
         out_ref[q, :, plan.width :] = packed
-    for t in (whole, whole + 1, *range(whole)):
-        if t < whole:
-            copies[7 + t].wait()
-            block = pops[t * LANES : (t + 1) * LANES, :]
-        elif t == whole:
-            block = pops[whole * LANES : (whole + 1) * LANES, :]
-        else:
+    for t in range(plan.tiles):
+        block = pops[t * LANES : (t + 1) * LANES, :]
+        if t == plan.tiles - 1:
             rate = pops[end - bins : end, :] * slots[...].astype(jnp.float32)
-            block = jnp.concatenate([rate, pops[end - 3 * bins : end - bins, :], rate], axis=0)
+            block = jnp.concatenate([block[: 2 * bins], rate, rate], axis=0)
         block = block.T
         if t == plan.tiles - 1:
-            lane = lax.broadcasted_iota(jnp.int32, block.shape, 1)
-            block = jnp.where(lane < bins, cell, block)
+            lane = lax.broadcasted_iota(jnp.int32, block.shape, 1) // bins
+            block = jnp.where(lane == FIELD_CELL % plan.per_tile, cell, block)
         for q in range(plan.sources):
             out_ref[holders[q], :, t * LANES : (t + 1) * LANES] = block[q * own : (q + 1) * own, :]
 
@@ -376,12 +380,12 @@
             outer_ref[h, :, start : start + LANES] = in_ref[2 * h + k, :, plan.width :]
 
 
-def two_part_dot(parts, matrix, contract):
+def two_part_dot(parts, matrix):
     whole = jnp.concatenate(parts, axis=0)
     rest = whole - whole.astype(jnp.bfloat16).astype(jnp.float32)
     stacked = jnp.concatenate([whole, rest], axis=0).astype(jnp.bfloat16)
     out = lax.dot_general(
-        stacked, matrix, (((1,), (contract,)), ((), ())), preferred_element_type=jnp.float32
+        stacked, matrix, (((1,), (1,)), ((), ())), preferred_element_type=jnp.float32
     )
     rows = parts[0].shape[0]
     half = rows * len(parts)
@@ -398,15 +402,13 @@
 
 def contact_blocks(plan, packed, link_ref):
     group, per = plan.group, plan.per_tile
-    lane = lax.broadcasted_iota(jnp.int32, (SUBLANES, LANES), 1)
-    for s in range(plan.sources):
-        place = s % per
-        tile = packed(s)
-        pieces = []
-        for g in range(per):
-            moved = tile if g == place else pltpu.roll(tile, (place - g) * group % LANES, 1)
-            pieces.append(jnp.where(lane // group == place, moved, 0.0))
-        link_ref[s * group : (s + 1) * group, :] = jnp.concatenate(pieces, axis=0).astype(jnp.bfloat16)
+    lane = lax.broadcasted_iota(jnp.int32, (SUBLANES, LANES), 1) // group
+    for q in range(0, plan.sources, per):
+        turned = turned_groups([packed(s) for s in range(q, q + per)], group)
+        for s in range(per):
+            pieces = [jnp.where(lane == s, turned[(s - g) % per], 0.0) for g in range(per)]
+            start = (q + s) * group
+            link_ref[start : start + group, :] = jnp.concatenate(pieces, axis=0).astype(jnp.bfloat16)
 
 
 def unpack(plan, tile_of, state_ref, rows):
@@ -418,22 +420,146 @@
                 state_ref[t * per + j, rows, q * LANES : (q + 1) * LANES] = part
 
 
-def settle_kernel(plan, in_ref, state_ref, column_ref, link_ref):
-    unpack(plan, lambda s, t: in_ref[s, :, t * LANES : (t + 1) * LANES], state_ref, slice(0, plan.own))
+def touching(plan, parts, matrix):
+    quads = plan.sources // plan.per_tile
+    blocks = []
+    for q in range(quads):
+        at = slice(q * LANES, (q + 1) * LANES)
+        blocks.append(two_part_dot([x[:, at] for x in parts], matrix[at, :]))
+    return [jnp.concatenate([b[i] for b in blocks], axis=1) for i in range(len(parts))]
+
+
+def tile_lanes(plan):
+    return [slice(q * LANES, (q + 1) * LANES) for q in range(plan.sources // plan.per_tile)]
+
+
+def on_bins(plan, fields, cells):
+    tiles = tile_lanes(plan)
+    cells = cells.astype(jnp.int32)
+    lane, tile = lax.rem(cells, LANES), lax.div(cells, LANES)
+    out = []
+    for x in fields:
+        pieces = []
+        for to in tiles:
+            found = None
+            for q, at in enumerate(tiles):
+                moved = jnp.take_along_axis(x[:, at], lane[:, to], axis=1, mode="promise_in_bounds")
+                found = moved if found is None else jnp.where(tile[:, to] == q, moved, found)
+            pieces.append(found)
+        out.append(jnp.concatenate(pieces, axis=1))
+    return out
+
+
+def fixed_fields(products, state_ref, aux_ref, rows):
+    to_columns, near = products
+    rate = state_ref[FIELD_RATE, rows]
+    aux_ref[0, rows] = 1.0 / (1.0 + to_columns([rate])[0])
+    aux_ref[1, rows] = near([(rate > 0.0).astype(jnp.float32)])[0]
+
+
+def collide_rows(plan, products, state_ref, post_ref, aux_ref, u_ref, force_ref, rows):
+    to_columns, near = products
+    for lanes in tile_lanes(plan):
+        popul = [state_ref[i, rows, lanes] for i in range(19)]
+        density = popul[0]
+        for i in range(1, 19):
+            density = density + popul[i]
+        inverse = 1.0 / density
+        u_ref[3, rows, lanes] = density
+        u_ref[4, rows, lanes] = inverse
+        for a in range(3):
+            rising = [popul[i] for i in range(19) if VELOCITIES[i, a] == 1]
+            falling = [popul[i] for i in range(19) if VELOCITIES[i, a] == -1]
+            u_ref[a, rows, lanes] = (sum(rising[1:], rising[0]) - sum(falling[1:], falling[0])) * inverse
+    rate = state_ref[FIELD_RATE, rows]
+    live = (rate > 0.0).astype(jnp.float32)
+    velocity = [state_ref[field, rows] for field in FIELD_V]
+    speed = on_bins(plan, [u_ref[a, rows] for a in range(3)], state_ref[FIELD_CELL, rows])
+    drags = [drag_factor * rate * (speed[a] - velocity[a]) for a in range(3)]
+    for a, force in enumerate(to_columns(drags)):
+        force_ref[a, rows] = force
+    moving = near([velocity[a] * live for a in range(3)])
+    count = aux_ref[1, rows]
+    for a in range(3):
+        push = contact_stiffness * live * (moving[a] - count * velocity[a])
+        updated = velocity[a] + drags[a] + push
+        if a == 2:
+            updated = updated - gravity * live
+        state_ref[FIELD_V[a], rows] = updated
+    keep, take = 1.0 - 1.0 / relax_time, 1.0 / relax_time
+    for lanes in tile_lanes(plan):
+        density, inverse = u_ref[3, rows, lanes], u_ref[4, rows, lanes]
+        scale = aux_ref[0, rows, lanes]
+        share = relax_time * inverse
+        target = [scale * (u_ref[a, rows, lanes] - share * force_ref[a, rows, lanes]) for a in range(3)]
+        square = target[0] * target[0] + target[1] * target[1] + target[2] * target[2]
+        base = 1.0 - 1.5 * square
+        triple = [3.0 * x for x in target]
+        shares = {w: (take * float(w)) * density for w in sorted(set(WEIGHTS))}
+        post_ref[0, rows, lanes] = keep * state_ref[0, rows, lanes] + shares[WEIGHTS[0]] * base
+        for i in range(1, 19, 2):
+            along = None
+            for a in range(3):
+                if VELOCITIES[i, a] != 0:
+                    if along is None:
+                        along = triple[a] if VELOCITIES[i, a] == 1 else -triple[a]
+                    else:
+                        along = along + triple[a] if VELOCITIES[i, a] == 1 else along - triple[a]
+            level = base + 0.5 * (along * along)
+            share_i = shares[WEIGHTS[i]]
+            post_ref[i, rows, lanes] = keep * state_ref[i, rows, lanes] + share_i * (level + along)
+            post_ref[i + 1, rows, lanes] = keep * state_ref[i + 1, rows, lanes] + share_i * (level - along)
+
+
+def stream_rows(plan, state_ref, post_ref, ground, ceiling):
+    rows, group, dx, dy = plan.rows, plan.group, plan.dx, plan.dy
+    lane = lax.broadcasted_iota(jnp.int32, (rows, LANES), 1)
+    row = lax.broadcasted_iota(jnp.int32, (rows, LANES), 0)
+    lane_y = lax.div(lane, group) * dy + lax.rem(lane, dy)
+    lane_x = lax.rem(lax.div(lane, dy), dx)
+    bottom, top = ground & (row == 0), ceiling & (row == plan.own - 1)
+    tiles = tile_lanes(plan)
+    for i in range(19):
+        cx, cy, cz = (int(c) for c in VELOCITIES[i])
+        moved = [post_ref[i, :, lanes] for lanes in tiles]
+        if cx or cy:
+            y = lax.rem(lane_y - cy + plan.n_gy * dy, plan.n_gy * dy)
+            x = lax.rem(lane_x - cx + dx, dx)
+            from_lane = lax.div(y, dy) * group + x * dy + lax.rem(y, dy)
+            moved = [jnp.take_along_axis(x, from_lane, axis=1, mode="promise_in_bounds") for x in moved]
+        if cx:
+            edge = lane_x == (0 if cx == 1 else dx - 1)
+            moved = [jnp.where(edge, moved[(q - cx) % len(tiles)], moved[q]) for q in range(len(tiles))]
+        for x, lanes in zip(moved, tiles):
+            if cz:
+                x = pltpu.roll(x, cz % rows, 0)
+                x = jnp.where(bottom if cz == 1 else top, post_ref[OPPOSITE[i], :, lanes], x)
+            state_ref[i, :, lanes] = x
+
+
+def settle_kernel(plan, in_ref, state_ref, post_ref, aux_ref, column_ref, link_ref, u_ref, force_ref):
+    own = slice(0, plan.own)
+    unpack(plan, lambda s, t: in_ref[s, :, t * LANES : (t + 1) * LANES], state_ref, own)
     column_ref[...] = bins_on_columns(plan.columns, state_ref[FIELD_CELL, 0:1, :])
     contact_blocks(plan, lambda s: in_ref[s, :, plan.width :], link_ref)
-
-
-def substeps_kernel(plan, settled_ref, column_ref, link_ref, inner_ref, outer_ref, out_ref, state_ref,
-                    post_ref, u_ref, force_ref, count_ref, other_column_ref, other_link_ref):
+    products = (
+        lambda parts: two_part_dot(parts, column_ref[...]),
+        lambda parts: touching(plan, parts, link_ref),
+    )
+    fixed_fields(products, state_ref, aux_ref, own)
+    collide_rows(plan, products, state_ref, post_ref, aux_ref, u_ref, force_ref, own)
+
+
+def substeps_kernel(plan, settled_ref, collided_ref, fixed_ref, column_ref, link_ref, inner_ref, outer_ref,
+                    out_ref, state_ref, post_ref, aux_ref, u_ref, force_ref, other_column_ref, other_link_ref):
     rows, columns, group, per = plan.rows, plan.columns, plan.group, plan.per_tile
-    halo, own, dx, dy = plan.halo, plan.own, plan.dx, plan.dy
-    quads = plan.sources // per
+    halo, own = plan.halo, plan.own
     window, layer = plan.place()
     even = lax.rem(window, 2) == 0
     first, last = window == 0, window == plan.sources - 1
     ground, ceiling = first & (layer == 0), last & (layer == plan.n_gz - 1)
     tile_row = lax.broadcasted_iota(jnp.int32, (SUBLANES, LANES), 0)
+    beyond = slice(own, rows)
 
     def halo_tile(s, t):
         at = slice(t * LANES, (t + 1) * LANES)
@@ -446,7 +572,7 @@
             below = pltpu.roll(below, halo, 0)
         return jnp.where(tile_row < halo, above, below)
 
-    unpack(plan, halo_tile, state_ref, slice(own, rows))
+    unpack(plan, halo_tile, state_ref, beyond)
     other_cells = jnp.where(first, state_ref[FIELD_CELL, rows - 1 : rows, :], state_ref[FIELD_CELL, own : own + 1, :])
     other_column_ref[...] = bins_on_columns(columns, other_cells)
 
@@ -459,150 +585,57 @@
     halo_row = lax.broadcasted_iota(jnp.int32, (SUBLANES, columns), 0)
     foreign = (last & (halo_row < halo)) | (first & (halo_row >= halo))
 
-    def both_layers(parts, product, own_matrix, other_matrix):
-        mine = product(parts, own_matrix)
-        others = product([x[own:] for x in parts], other_matrix)
-        return [
-            jnp.concatenate([a[:own], jnp.where(foreign, b, a[own:])], axis=0) for a, b in zip(mine, others)
-        ]
-
-    def to_bins(parts):
-        return both_layers(parts, lambda x, m: two_part_dot(x, m[...], 0), column_ref, other_column_ref)
-
-    def to_columns(parts):
-        return both_layers(parts, lambda x, m: two_part_dot(x, m[...], 1), column_ref, other_column_ref)
-
-    def touching(parts, matrix):
-        blocks = [
-            two_part_dot(
-                [x[:, q * LANES : (q + 1) * LANES] for x in parts], matrix[q * LANES : (q + 1) * LANES, :], 1
-            )
-            for q in range(quads)
-        ]
-        return [jnp.concatenate([b[i] for b in blocks], axis=1) for i in range(len(parts))]
-
-    def near(parts):
-        return both_layers(parts, touching, link_ref, other_link_ref)
-
-    rate = state_ref[FIELD_RATE]
-    force_ref[3] = 1.0 / (1.0 + to_columns([rate])[0])
-    count_ref[...] = near([(rate > 0.0).astype(jnp.float32)])[0]
-
-    lane = lax.broadcasted_iota(jnp.int32, (rows, LANES), 1)
-    row = lax.broadcasted_iota(jnp.int32, (rows, LANES), 0)
-    lane_y = lax.div(lane, group) * dy + lax.rem(lane, dy)
-    lane_x = lax.rem(lax.div(lane, dy), dx)
-    bottom, top = ground & (row == 0), ceiling & (row == own - 1)
-
-    def source_lanes(cx, cy):
-        y = lax.rem(lane_y - cy + plan.n_gy * dy, plan.n_gy * dy)
-        x = lax.rem(lane_x - cx + dx, dx)
-        return lax.div(y, dy) * group + x * dy + lax.rem(y, dy)
+    def both_layers(product, own_matrix, other_matrix):
+        def call(parts):
+            mine = product(parts, own_matrix)
+            others = product([x[-SUBLANES:] for x in parts], other_matrix)
+            if parts[0].shape[0] == SUBLANES:
+                return [jnp.where(foreign, b, a) for a, b in zip(mine, others)]
+            return [
+                jnp.concatenate([a[:own], jnp.where(foreign, b, a[own:])], axis=0) for a, b in zip(mine, others)
+            ]
+
+        return call
+
+    products = (
+        both_layers(lambda x, m: two_part_dot(x, m[...]), column_ref, other_column_ref),
+        both_layers(lambda x, m: touching(plan, x, m), link_ref, other_link_ref),
+    )
+    fixed_fields(products, state_ref, aux_ref, beyond)
+    collide_rows(plan, products, state_ref, post_ref, aux_ref, u_ref, force_ref, beyond)
+    stream_rows(plan, state_ref, post_ref, ground, ceiling)
 
     def step(_, carry):
-        for q in range(quads):
-            lanes = slice(q * LANES, (q + 1) * LANES)
-            popul = [state_ref[i, :, lanes] for i in range(19)]
-            density = popul[0]
-            for i in range(1, 19):
-                density = density + popul[i]
-            inverse = 1.0 / density
-            u_ref[3, :, lanes] = density
-            u_ref[4, :, lanes] = inverse
-            for a in range(3):
-                rising = [popul[i] for i in range(19) if VELOCITIES[i, a] == 1]
-                falling = [popul[i] for i in range(19) if VELOCITIES[i, a] == -1]
-                u_ref[a, :, lanes] = (sum(rising[1:], rising[0]) - sum(falling[1:], falling[0])) * inverse
-        rate = state_ref[FIELD_RATE]
-        live = (rate > 0.0).astype(jnp.float32)
-        velocity = [state_ref[field] for field in FIELD_V]
-        speed = to_bins([u_ref[a] for a in range(3)])
-        drags = [drag_factor * rate * (speed[a] - velocity[a]) for a in range(3)]
-        for a, force in enumerate(to_columns(drags)):
-            force_ref[a] = force
-        moving = near([velocity[a] * live for a in range(3)])
-        count = count_ref[...]
-        for a in range(3):
-            push = contact_stiffness * live * (moving[a] - count * velocity[a])
-            updated = velocity[a] + drags[a] + push
-            if a == 2:
-                updated = updated - gravity * live
-            state_ref[FIELD_V[a]] = updated
-        keep, take = 1.0 - 1.0 / relax_time, 1.0 / relax_time
-        for q in range(quads):
-            lanes = slice(q * LANES, (q + 1) * LANES)
-            density, inverse = u_ref[3, :, lanes], u_ref[4, :, lanes]
-            scale = force_ref[3, :, lanes]
-            share = relax_time * inverse
-            target = [scale * (u_ref[a, :, lanes] - share * force_ref[a, :, lanes]) for a in range(3)]
-            square = target[0] * target[0] + target[1] * target[1] + target[2] * target[2]
-            base = 1.0 - 1.5 * square
-            triple = [3.0 * x for x in target]
-            shares = {w: (take * float(w)) * density for w in sorted(set(WEIGHTS))}
-            post_ref[0, :, lanes] = keep * state_ref[0, :, lanes] + shares[WEIGHTS[0]] * base
-            for i in range(1, 19, 2):
-                along = None
-                for a in range(3):
-                    if VELOCITIES[i, a] != 0:
-                        if along is None:
-                            along = triple[a] if VELOCITIES[i, a] == 1 else -triple[a]
-                        else:
-                            along = along + triple[a] if VELOCITIES[i, a] == 1 else along - triple[a]
-                level = base + 0.5 * (along * along)
-                share_i = shares[WEIGHTS[i]]
-                post_ref[i, :, lanes] = keep * state_ref[i, :, lanes] + share_i * (level + along)
-                post_ref[i + 1, :, lanes] = keep * state_ref[i + 1, :, lanes] + share_i * (level - along)
-        for i in range(19):
-            cx, cy, cz = (int(c) for c in VELOCITIES[i])
-            moved = [post_ref[i, :, q * LANES : (q + 1) * LANES] for q in range(quads)]
-            if cx or cy:
-                from_lane = source_lanes(cx, cy)
-                moved = [jnp.take_along_axis(x, from_lane, axis=1, mode="promise_in_bounds") for x in moved]
-            if cx:
-                edge = lane_x == (0 if cx == 1 else dx - 1)
-                moved = [jnp.where(edge, moved[(q - cx) % quads], moved[q]) for q in range(quads)]
-            for q in range(quads):
-                lanes = slice(q * LANES, (q + 1) * LANES)
-                x = moved[q]
-                if cz:
-                    x = pltpu.roll(x, cz % rows, 0)
-                    x = jnp.where(bottom if cz == 1 else top, post_ref[OPPOSITE[i], :, lanes], x)
-                state_ref[i, :, lanes] = x
+        collide_rows(plan, products, state_ref, post_ref, aux_ref, u_ref, force_ref, slice(0, rows))
+        stream_rows(plan, state_ref, post_ref, ground, ceiling)
         return carry
 
-    lax.fori_loop(0, SUBSTEPS, step, 0)
+    lax.fori_loop(1, SUBSTEPS, step, 0)
 
     for t in range(plan.tiles):
-        sets = [
-            [state_ref[t * per + j, 0:own, q * LANES : (q + 1) * LANES] for j in range(per)] for q in range(quads)
-        ]
+        sets = [[state_ref[t * per + j, 0:own, lanes] for j in range(per)] for lanes in tile_lanes(plan)]
         for q, parts in enumerate(swap_groups(sets, group)):
             for s, part in enumerate(parts):
                 out_ref[q * per + s, :, t * LANES : (t + 1) * LANES] = part
 
 
 def finish_kernel(plan, in_ref, pop_ref, vel_ref, stage, sems):
-    bins = plan.bins
     whole = 19 * plan.group // LANES
-    rest = 19 * plan.group - whole * LANES
+    end = 19 * plan.group
+    split = whole * LANES // 2
     holders = [plan.holder(q) for q in range(plan.sources)]
+    moves = {
+        plan.tiles - 1: (stage.at[end : end + 3 * plan.bins], vel_ref),
+        whole // 2 - 1: (stage.at[:split], pop_ref.at[:split]),
+        whole - 1: (stage.at[split:end], pop_ref.at[split:]),
+    }
     copies = []
-
-    def send(start, size, target):
-        copies.append(pltpu.make_async_copy(stage.at[start : start + size], target, sems.at[len(copies)]))
-        copies[-1].start()
-
-    for t in range(plan.tiles):
+    for t in (whole, whole + 1, *range(whole)):
         at = slice(t * LANES, (t + 1) * LANES)
-        start = t * LANES
         stage[at, :] = jnp.concatenate([in_ref[holders[q], :, at] for q in range(plan.sources)], axis=0).T
-        if t < whole:
-            send(start, LANES, pop_ref.at[at])
-        elif t == whole:
-            send(start, rest, pop_ref.at[start:])
-            send(start + rest, bins, vel_ref.at[:bins])
-        else:
-            send(start + bins, 2 * bins, vel_ref.at[bins:])
+        if t in moves:
+            copies.append(pltpu.make_async_copy(*moves[t], sems.at[len(copies)]))
+            copies[-1].start()
     for copy in copies:
         copy.wait()
 
@@ -656,24 +689,28 @@
     )
     inner = lax.ppermute(inner, every_axis, plan.swaps(0))
     outer = lax.ppermute(outer, every_axis, plan.swaps(1))
-    state, column, link = call(
+    carried = [
+        ((plan.fields, rows, columns), f32),
+        ((19, rows, columns), f32),
+        ((2, rows, columns), f32),
+    ]
+    moments_and_forces = (pltpu.VMEM((5, rows, columns), f32), pltpu.VMEM((3, rows, columns), f32))
+    *settled, column, link = call(
         settle_kernel,
-        [((plan.fields, rows, columns), f32), ((columns, columns), bf16), ((columns, LANES), bf16)],
+        carried + [((columns, columns), bf16), ((columns, LANES), bf16)],
         (incoming,),
-    )
-    back, _ = call(
+        moments_and_forces,
+    )
+    back, *_ = call(
         substeps_kernel,
-        [((sources, own, plan.width), f32), ((plan.fields, rows, columns), f32)],
-        (state, column, link, inner, outer),
+        [((sources, own, plan.width), f32)] + carried,
+        (*settled, column, link, inner, outer),
         (
-            pltpu.VMEM((19, rows, columns), f32),
-            pltpu.VMEM((5, rows, columns), f32),
-            pltpu.VMEM((4, rows, columns), f32),
-            pltpu.VMEM((rows, columns), f32),
+            *moments_and_forces,
             pltpu.VMEM((columns, columns), bf16),
             pltpu.VMEM((columns, LANES), bf16),
         ),
-        aliases={0: 1},
+        aliases={0: 1, 1: 2, 2: 3},
     )
     result = lax.all_to_all(back, layer_axes, split_axis=0, concat_axis=0, tiled=True)
     fluid, velocity = call(

time: 52.6 us -> 49.8 us (0.947)
  blocking collectives: 40.7 us -> 35.8 us
  waiting for transfers between devices: 0.38 us -> 4.15 us
  Pallas kernels: 8.28 us -> 7.36 us
  starting transfers between devices: 2.36 us -> 1.56 us
    all_to_all x1, blocking collectives: 20.2 us -> 15.4 us  [windows_body(): lax.all_to_all(back, layer_axes, split_axis=0, concat_axis=0, tiled=True)]
    ppermute x1, waiting for transfers between devices: 0.01 us -> 3.44 us  [windows_body(): outer = lax.ppermute(outer, every_axis, plan.swaps(1))]
    ppermute x1, starting transfers between devices: 1.68 us -> 0.01 us  [windows_body(): inner = lax.ppermute(inner, every_axis, plan.swaps(0))]
    pallas_call x5, Pallas kernels: 8.28 us -> 7.36 us  [call(): pl.pallas_call(lambda *refs: kernel(plan, *refs), out_shape=shapes, in_sp...]
    ppermute x1, starting transfers between devices: 0.68 us -> 1.56 us  [windows_body(): outer = lax.ppermute(outer, every_axis, plan.swaps(1))]
  transfers between devices with their start and end apart: 2 -> 2, of which waited for: 1 -> 2; matrix products, arithmetic and copies ran while one was open for 0% -> 0% of each run, Pallas kernels for 1% -> 1%
where the time goes in v4:
time: 49.8 us; the launch traced here: 49.6 us
  blocking collectives  35.8 us (72%)
  Pallas kernels  7.36 us (15%)
  waiting for transfers between devices  4.15 us (8%)
  starting transfers between devices  1.56 us (3%)
  between operations  0.66 us (1%)
    all_to_all x1, blocking collectives, windows_body(): lax.all_to_all(outgoing, layer_axes, split_axis=0, concat_axis=0, tiled=T...  20.4 us
    all_to_all x1, blocking collectives, windows_body(): lax.all_to_all(back, layer_axes, split_axis=0, concat_axis=0, tiled=True)  15.4 us
    pallas_call x5, Pallas kernels, call(): pl.pallas_call(lambda *refs: kernel(plan, *refs), out_shape=shapes, in_sp...  7.36 us
    ppermute x1, waiting for transfers between devices, windows_body(): outer = lax.ppermute(outer, every_axis, plan.swaps(1))  3.44 us
    ppermute x1, starting transfers between devices, windows_body(): outer = lax.ppermute(outer, every_axis, plan.swaps(1))  1.56 us
  transfers between devices with their start and end apart: 2, of which 2 were waited for; matrix products, arithmetic and copies ran while one was open for 0% of the time, Pallas kernels for 1%

profile of v4, /device:TPU:0, one launch (start us, length us, event | category | flops | bytes accessed | tf_op | source)
XLA Modules:
  0.0 49.6 jit_solution(3952091103251163416)
XLA Ops:
  0.6 1.4 %shard_map.77 = f32[16,8,896]{2,1,0:T(8,128)S(1)} custom-call(f32[608,128]{1,0:T(8,128)} %bitcast.5, f32[96,128]{1,0:T(8,128)} %bitcast.6, f32[32,128]{1,0:T(8,128)} %refs_2_.1, s32[32,128]{1,0:T(8,128)} %refs_3_.1, s32[32,32]{1,0:T(8,128)} %refs_4_.1, s32[1,32]{1,0:T(1,128)} %bitcast.7), custom_call_target="tpu_custom_call" | custom-call | tf_op jit(solution)/shard_map/pallas_call | solution.py:653
  2.1 20.4 %all_to_all.10.refs_0_ = f32[16,8,896]{2,1,0:T(8,128)S(1)} all-to-all(f32[16,8,896]{2,1,0:T(8,128)S(1)} %shard_map.77), channel_id=1, replica_groups=mesh['gx'=4,'gy'=4,'gz'=2] {'gx','gy'}, dimensions={0} | all-to-all | bytes 917504 | tf_op jit(solution)/shard_map/all_to_all | solution.py:684
  22.5 0.1 shard_map.79
  22.6 1.6 %collective-permute-start.1 = (f32[8,8,1024]{2,1,0:T(8,128)S(1)}, f32[8,8,1024]{2,1,0:T(8,128)S(1)}, u32[]{:S(2)}, u32[]{:S(2)}) collective-permute-start(f32[8,8,1024]{2,1,0:T(8,128)S(1)} %get-tuple-element.18), channel_id=1, source_target_pairs={{2,4},{4,2},{6,14},{14,6},{12,10},{10,12},{8,16},{16,8},{18,20},{2... | collective-permute-start | bytes 786440 | tf_op jit(solution)/shard_map/ppermute | solution.py:691
  24.1 0.0 collective-permute-start
  24.1 0.7 %shard_map.78 = (f32[24,16,512]{2,1,0:T(8,128)S(1)}, f32[19,16,512]{2,1,0:T(8,128)S(1)}, f32[2,16,512]{2,1,0:T(8,128)S(1)}, bf16[512,512]{1,0:T(8,128)(2,1)S(1)}, bf16[512,128]{1,0:T(8,128)(2,1)S(1)}) custom-call(f32[16,8,896]{2,1,0:T(8,128)S(1)} %all_to_all.10.refs_0_), custom_call_target="tpu_custom_call" | custom-call | tf_op jit(solution)/shard_map/pallas_call | solution.py:653
  24.8 0.7 %collective-permute-done.refs_5_ = f32[8,8,768]{2,1,0:T(8,128)S(1)} collective-permute-done((f32[8,8,768]{2,1,0:T(8,128)S(1)}, f32[8,8,768]{2,1,0:T(8,128)S(1)}, u32[]{:S(2)}, u32[]{:S(2)}) %collective-permute-start) | collective-permute-done | bytes 196640 | tf_op jit(solution)/shard_map/ppermute | solution.py:690
  25.6 3.4 %collective-permute-done.1.refs_6_ = f32[8,8,1024]{2,1,0:T(8,128)S(1)} collective-permute-done((f32[8,8,1024]{2,1,0:T(8,128)S(1)}, f32[8,8,1024]{2,1,0:T(8,128)S(1)}, u32[]{:S(2)}, u32[]{:S(2)}) %collective-permute-start.1) | collective-permute-done | bytes 262176 | tf_op jit(solution)/shard_map/ppermute | solution.py:691
  29.0 4.2 %shard_map.80 = (f32[16,8,768]{2,1,0:T(8,128)S(1)}, f32[24,16,512]{2,1,0:T(8,128)S(1)}, f32[19,16,512]{2,1,0:T(8,128)S(1)}, f32[2,16,512]{2,1,0:T(8,128)S(1)}) custom-call(f32[24,16,512]{2,1,0:T(8,128)S(1)} %get-tuple-element.12.refs_0_, f32[19,16,512]{2,1,0:T(8,128)S(1)} %get-tuple-element.13.refs_1_, ...), custom_call_target="tpu_custom_call", output_to_operand_aliasing={{1}: (0, {}), {2}: (1, {}), {3}: (2, {})} | custom-call | tf_op jit(solution)/shard_map/pallas_call | solution.py:653
  33.2 15.4 %all_to_all.11.refs_0_ = f32[16,8,768]{2,1,0:T(8,128)S(1)} all-to-all(f32[16,8,768]{2,1,0:T(8,128)S(1)} %get-tuple-element.19), channel_id=1, replica_groups=mesh['gx'=4,'gy'=4,'gz'=2] {'gx','gy'}, dimensions={0} | all-to-all | bytes 786432 | tf_op jit(solution)/shard_map/all_to_all | solution.py:715
  48.6 1.0 %shard_map.81 = (f32[608,128]{1,0:T(8,128)}, f32[96,128]{1,0:T(8,128)}) custom-call(f32[16,8,768]{2,1,0:T(8,128)S(1)} %all_to_all.11.refs_0_), custom_call_target="tpu_custom_call" | custom-call | tf_op jit(solution)/shard_map/pallas_call | solution.py:653
Async XLA Ops:
  22.6 6.4 %collective-permute-start.1 = (f32[8,8,1024]{2,1,0:T(8,128)S(1)}, f32[8,8,1024]{2,1,0:T(8,128)S(1)}, u32[]{:S(2)}, u32[]{:S(2)}) collective-permute-start(f32[8,8,1024]{2,1,0:T(8,128)S(1)} %get-tuple-element.18), channel_id=1, source_target_pairs={{2,4},{4,2},{6,14},{14,6},{12,10},{10,12},{8,16},{16,8},{18,20},{2... | collective-permute-start | bytes 786440 | tf_op jit(solution)/shard_map/ppermute | solution.py:691
  24.1 1.4 %collective-permute-start = (f32[8,8,768]{2,1,0:T(8,128)S(1)}, f32[8,8,768]{2,1,0:T(8,128)S(1)}, u32[]{:S(2)}, u32[]{:S(2)}) collective-permute-start(f32[8,8,768]{2,1,0:T(8,128)S(1)} %get-tuple-element.17), channel_id=1, source_target_pairs={{0,2},{2,0},{4,6},{6,4},{14,12},{12,14},{10,8},{8,10},{16,18},{18,... | collective-permute-start | bytes 589832 | tf_op jit(solution)/shard_map/ppermute | solution.py:690

commit v5 on v4

--- a/solution.py
+++ b/solution.py
@@ -243,6 +243,7 @@
         self.tiles = self.fields // self.per_tile
         self.width = self.fields * self.group
         self.wide = self.width + LANES
+        self.returned = (2 * self.tiles - 1) * LANES
 
     def fits(self):
         group = self.group
@@ -251,7 +252,7 @@
             and self.depth == LANES
             and self.grains == LANES
             and self.own * self.sources == LANES
-            and self.own == SUBLANES
+            and self.own == SUBLANES == 2 * self.halo
             and self.rows == 2 * SUBLANES
             and group == self.bins
             and group * group == SUBLANES * LANES
@@ -450,14 +451,7 @@
     return out
 
 
-def fixed_fields(products, state_ref, aux_ref, rows):
-    to_columns, near = products
-    rate = state_ref[FIELD_RATE, rows]
-    aux_ref[0, rows] = 1.0 / (1.0 + to_columns([rate])[0])
-    aux_ref[1, rows] = near([(rate > 0.0).astype(jnp.float32)])[0]
-
-
-def collide_rows(plan, products, state_ref, post_ref, aux_ref, u_ref, force_ref, rows):
+def collide_rows(plan, products, state_ref, post_ref, aux_ref, u_ref, force_ref, rows, begin=False):
     to_columns, near = products
     for lanes in tile_lanes(plan):
         popul = [state_ref[i, rows, lanes] for i in range(19)]
@@ -476,10 +470,18 @@
     velocity = [state_ref[field, rows] for field in FIELD_V]
     speed = on_bins(plan, [u_ref[a, rows] for a in range(3)], state_ref[FIELD_CELL, rows])
     drags = [drag_factor * rate * (speed[a] - velocity[a]) for a in range(3)]
-    for a, force in enumerate(to_columns(drags)):
+    moving = [velocity[a] * live for a in range(3)]
+    if begin:
+        *forces, solid = to_columns(drags + [rate])
+        *moving, count = near(moving + [live])
+        aux_ref[0, rows] = 1.0 / (1.0 + solid)
+        aux_ref[1, rows] = count
+    else:
+        forces = to_columns(drags)
+        moving = near(moving)
+        count = aux_ref[1, rows]
+    for a, force in enumerate(forces):
         force_ref[a, rows] = force
-    moving = near([velocity[a] * live for a in range(3)])
-    count = aux_ref[1, rows]
     for a in range(3):
         push = contact_stiffness * live * (moving[a] - count * velocity[a])
         updated = velocity[a] + drags[a] + push
@@ -546,8 +548,7 @@
         lambda parts: two_part_dot(parts, column_ref[...]),
         lambda parts: touching(plan, parts, link_ref),
     )
-    fixed_fields(products, state_ref, aux_ref, own)
-    collide_rows(plan, products, state_ref, post_ref, aux_ref, u_ref, force_ref, own)
+    collide_rows(plan, products, state_ref, post_ref, aux_ref, u_ref, force_ref, own, True)
 
 
 def substeps_kernel(plan, settled_ref, collided_ref, fixed_ref, column_ref, link_ref, inner_ref, outer_ref,
@@ -601,8 +602,7 @@
         both_layers(lambda x, m: two_part_dot(x, m[...]), column_ref, other_column_ref),
         both_layers(lambda x, m: touching(plan, x, m), link_ref, other_link_ref),
     )
-    fixed_fields(products, state_ref, aux_ref, beyond)
-    collide_rows(plan, products, state_ref, post_ref, aux_ref, u_ref, force_ref, beyond)
+    collide_rows(plan, products, state_ref, post_ref, aux_ref, u_ref, force_ref, beyond, True)
     stream_rows(plan, state_ref, post_ref, ground, ceiling)
 
     def step(_, carry):
@@ -612,11 +612,19 @@
 
     lax.fori_loop(1, SUBSTEPS, step, 0)
 
+    first_half = lax.broadcasted_iota(jnp.int32, (halo, LANES), 1) < LANES // 2
     for t in range(plan.tiles):
         sets = [[state_ref[t * per + j, 0:own, lanes] for j in range(per)] for lanes in tile_lanes(plan)]
         for q, parts in enumerate(swap_groups(sets, group)):
             for s, part in enumerate(parts):
-                out_ref[q * per + s, :, t * LANES : (t + 1) * LANES] = part
+                low, high = part[:halo], part[halo:]
+                if t == plan.tiles - 1:
+                    pieces = [jnp.where(first_half, low, pltpu.roll(high, LANES // 2, 1))]
+                else:
+                    pieces = [low, high]
+                for k, piece in enumerate(pieces):
+                    start = (2 * t + k) * LANES
+                    out_ref[q * per + s, :, start : start + LANES] = piece
 
 
 def finish_kernel(plan, in_ref, pop_ref, vel_ref, stage, sems):
@@ -631,8 +639,16 @@
     }
     copies = []
     for t in (whole, whole + 1, *range(whole)):
-        at = slice(t * LANES, (t + 1) * LANES)
-        stage[at, :] = jnp.concatenate([in_ref[holders[q], :, at] for q in range(plan.sources)], axis=0).T
+        pieces = []
+        for holder in holders:
+            start = 2 * t * LANES
+            low = in_ref[holder, :, start : start + LANES]
+            if t == plan.tiles - 1:
+                high = pltpu.roll(low, LANES // 2, 1)
+            else:
+                high = in_ref[holder, :, start + LANES : start + 2 * LANES]
+            pieces += [low, high]
+        stage[t * LANES : (t + 1) * LANES, :] = jnp.concatenate(pieces, axis=0).T
         if t in moves:
             copies.append(pltpu.make_async_copy(*moves[t], sems.at[len(copies)]))
             copies[-1].start()
@@ -703,7 +719,7 @@
     )
     back, *_ = call(
         substeps_kernel,
-        [((sources, own, plan.width), f32)] + carried,
+        [((sources, plan.halo, plan.returned), f32)] + carried,
         (*settled, column, link, inner, outer),
         (
             *moments_and_forces,

time: 49.8 us -> 49.1 us (0.986)
  blocking collectives: 35.8 us -> 35.3 us
    all_to_all x1, blocking collectives: 15.4 us -> 14.8 us  [windows_body(): lax.all_to_all(back, layer_axes, split_axis=0, concat_axis=0, tiled=True)]
where the time goes in v5:
time: 49.1 us; the launch traced here: 48.9 us
  blocking collectives  35.3 us (72%)
  Pallas kernels  7.13 us (15%)
  waiting for transfers between devices  4.24 us (9%)
  starting transfers between devices  1.56 us (3%)
  between operations  0.66 us (1%)
    all_to_all x1, blocking collectives, windows_body(): lax.all_to_all(outgoing, layer_axes, split_axis=0, concat_axis=0, tiled=T...  20.4 us
    all_to_all x1, blocking collectives, windows_body(): lax.all_to_all(back, layer_axes, split_axis=0, concat_axis=0, tiled=True)  14.8 us
    pallas_call x5, Pallas kernels, call(): pl.pallas_call(lambda *refs: kernel(plan, *refs), out_shape=shapes, in_sp...  7.13 us
    ppermute x1, waiting for transfers between devices, windows_body(): outer = lax.ppermute(outer, every_axis, plan.swaps(1))  3.44 us
    ppermute x1, starting transfers between devices, windows_body(): outer = lax.ppermute(outer, every_axis, plan.swaps(1))  1.56 us
  transfers between devices with their start and end apart: 2, of which 2 were waited for; matrix products, arithmetic and copies ran while one was open for 0% of the time, Pallas kernels for 1%

profile of v5, /device:TPU:0, one launch (start us, length us, event | category | flops | bytes accessed | tf_op | source)
XLA Modules:
  0.0 48.9 jit_solution(12117093326117282853)
XLA Ops:
  0.6 1.4 %shard_map.77 = f32[16,8,896]{2,1,0:T(8,128)S(1)} custom-call(f32[608,128]{1,0:T(8,128)} %bitcast.5, f32[96,128]{1,0:T(8,128)} %bitcast.6, f32[32,128]{1,0:T(8,128)} %refs_2_.1, s32[32,128]{1,0:T(8,128)} %refs_3_.1, s32[32,32]{1,0:T(8,128)} %refs_4_.1, s32[1,32]{1,0:T(1,128)} %bitcast.7), custom_call_target="tpu_custom_call" | custom-call | tf_op jit(solution)/shard_map/pallas_call | solution.py:669
  2.1 20.4 %all_to_all.10.refs_0_ = f32[16,8,896]{2,1,0:T(8,128)S(1)} all-to-all(f32[16,8,896]{2,1,0:T(8,128)S(1)} %shard_map.77), channel_id=1, replica_groups=mesh['gx'=4,'gy'=4,'gz'=2] {'gx','gy'}, dimensions={0} | all-to-all | bytes 917504 | tf_op jit(solution)/shard_map/all_to_all | solution.py:700
  22.5 0.1 shard_map.79
  22.6 1.6 %collective-permute-start.1 = (f32[8,8,1024]{2,1,0:T(8,128)S(1)}, f32[8,8,1024]{2,1,0:T(8,128)S(1)}, u32[]{:S(2)}, u32[]{:S(2)}) collective-permute-start(f32[8,8,1024]{2,1,0:T(8,128)S(1)} %get-tuple-element.18), channel_id=1, source_target_pairs={{2,4},{4,2},{6,14},{14,6},{12,10},{10,12},{8,16},{16,8},{18,20},{2... | collective-permute-start | bytes 786440 | tf_op jit(solution)/shard_map/ppermute | solution.py:707
  24.1 0.0 collective-permute-start
  24.1 0.6 %shard_map.78 = (f32[24,16,512]{2,1,0:T(8,128)S(1)}, f32[19,16,512]{2,1,0:T(8,128)S(1)}, f32[2,16,512]{2,1,0:T(8,128)S(1)}, bf16[512,512]{1,0:T(8,128)(2,1)S(1)}, bf16[512,128]{1,0:T(8,128)(2,1)S(1)}) custom-call(f32[16,8,896]{2,1,0:T(8,128)S(1)} %all_to_all.10.refs_0_), custom_call_target="tpu_custom_call" | custom-call | tf_op jit(solution)/shard_map/pallas_call | solution.py:669
  24.8 0.8 %collective-permute-done.refs_5_ = f32[8,8,768]{2,1,0:T(8,128)S(1)} collective-permute-done((f32[8,8,768]{2,1,0:T(8,128)S(1)}, f32[8,8,768]{2,1,0:T(8,128)S(1)}, u32[]{:S(2)}, u32[]{:S(2)}) %collective-permute-start) | collective-permute-done | bytes 196640 | tf_op jit(solution)/shard_map/ppermute | solution.py:706
  25.6 3.4 %collective-permute-done.1.refs_6_ = f32[8,8,1024]{2,1,0:T(8,128)S(1)} collective-permute-done((f32[8,8,1024]{2,1,0:T(8,128)S(1)}, f32[8,8,1024]{2,1,0:T(8,128)S(1)}, u32[]{:S(2)}, u32[]{:S(2)}) %collective-permute-start.1) | collective-permute-done | bytes 262176 | tf_op jit(solution)/shard_map/ppermute | solution.py:707
  29.0 4.0 %shard_map.80 = (f32[16,4,1408]{2,1,0:T(4,128)S(1)}, f32[24,16,512]{2,1,0:T(8,128)S(1)}, f32[19,16,512]{2,1,0:T(8,128)S(1)}, f32[2,16,512]{2,1,0:T(8,128)S(1)}) custom-call(f32[24,16,512]{2,1,0:T(8,128)S(1)} %get-tuple-element.12.refs_0_, f32[19,16,512]{2,1,0:T(8,128)S(1)} %get-tuple-element.13.refs_1_, ...), custom_call_target="tpu_custom_call", output_to_operand_aliasing={{1}: (0, {}), {2}: (1, {}), {3}: (2, {})} | custom-call | tf_op jit(solution)/shard_map/pallas_call | solution.py:669
  33.0 14.8 %all_to_all.11.refs_0_ = f32[16,4,1408]{2,1,0:T(4,128)S(1)} all-to-all(f32[16,4,1408]{2,1,0:T(4,128)S(1)} %get-tuple-element.19), channel_id=1, replica_groups=mesh['gx'=4,'gy'=4,'gz'=2] {'gx','gy'}, dimensions={0} | all-to-all | bytes 720896 | tf_op jit(solution)/shard_map/all_to_all | solution.py:731
  47.8 1.0 %shard_map.81 = (f32[608,128]{1,0:T(8,128)}, f32[96,128]{1,0:T(8,128)}) custom-call(f32[16,4,1408]{2,1,0:T(4,128)S(1)} %all_to_all.11.refs_0_), custom_call_target="tpu_custom_call" | custom-call | tf_op jit(solution)/shard_map/pallas_call | solution.py:669
Async XLA Ops:
  22.6 6.4 %collective-permute-start.1 = (f32[8,8,1024]{2,1,0:T(8,128)S(1)}, f32[8,8,1024]{2,1,0:T(8,128)S(1)}, u32[]{:S(2)}, u32[]{:S(2)}) collective-permute-start(f32[8,8,1024]{2,1,0:T(8,128)S(1)} %get-tuple-element.18), channel_id=1, source_target_pairs={{2,4},{4,2},{6,14},{14,6},{12,10},{10,12},{8,16},{16,8},{18,20},{2... | collective-permute-start | bytes 786440 | tf_op jit(solution)/shard_map/ppermute | solution.py:707
  24.1 1.4 %collective-permute-start = (f32[8,8,768]{2,1,0:T(8,128)S(1)}, f32[8,8,768]{2,1,0:T(8,128)S(1)}, u32[]{:S(2)}, u32[]{:S(2)}) collective-permute-start(f32[8,8,768]{2,1,0:T(8,128)S(1)} %get-tuple-element.17), channel_id=1, source_target_pairs={{0,2},{2,0},{4,6},{6,4},{14,12},{12,14},{10,8},{8,10},{16,18},{18,... | collective-permute-start | bytes 589832 | tf_op jit(solution)/shard_map/ppermute | solution.py:706

commit v6 on v5

--- a/solution.py
+++ b/solution.py
@@ -242,7 +242,7 @@
         self.fields = 24
         self.tiles = self.fields // self.per_tile
         self.width = self.fields * self.group
-        self.wide = self.width + LANES
+        self.wide = (2 * self.tiles + 1) * LANES
         self.returned = (2 * self.tiles - 1) * LANES
 
     def fits(self):
@@ -315,7 +315,7 @@
 
 def prepare_kernel(plan, pop_ref, vel_ref, vol_ref, slot_ref, link_ref, cell_ref, out_ref,
                    pops, slots, links, cells, sems):
-    group, bins, own = plan.group, plan.bins, plan.own
+    group, bins, own, halo = plan.group, plan.bins, plan.own, plan.halo
     whole = 19 * group // LANES
     end = plan.width
     vel_start = 19 * group
@@ -349,7 +349,8 @@
     )
     holders = [plan.holder(q) for q in range(plan.sources)]
     for q in range(plan.sources):
-        out_ref[q, :, plan.width :] = packed
+        part = q % 2 * halo
+        out_ref[holders[q], :, 2 * plan.width :] = packed[part : part + halo, :]
     for t in range(plan.tiles):
         block = pops[t * LANES : (t + 1) * LANES, :]
         if t == plan.tiles - 1:
@@ -360,25 +361,26 @@
             lane = lax.broadcasted_iota(jnp.int32, block.shape, 1) // bins
             block = jnp.where(lane == FIELD_CELL % plan.per_tile, cell, block)
         for q in range(plan.sources):
-            out_ref[holders[q], :, t * LANES : (t + 1) * LANES] = block[q * own : (q + 1) * own, :]
+            for k in range(2):
+                start, row = (2 * t + k) * LANES, q * own + k * halo
+                out_ref[holders[q], :, start : start + LANES] = block[row : row + halo, :]
+
+
+def half_tile(ref, s, t, k):
+    start = (2 * t + k) * LANES
+    return ref[s, :, start : start + LANES]
 
 
 def edges_kernel(plan, in_ref, inner_ref, outer_ref):
     window, _ = plan.place()
     even = lax.rem(window, 2) == 0
-    halo = plan.halo
-    low_rows = lax.broadcasted_iota(jnp.int32, (SUBLANES, LANES), 0) < halo
-    for h in range(plan.sources // 2):
+    for s in range(plan.sources):
         for t in range(plan.tiles):
             lanes = slice(t * LANES, (t + 1) * LANES)
-            a, b = in_ref[2 * h, :, lanes], in_ref[2 * h + 1, :, lanes]
-            low = jnp.where(low_rows, a, pltpu.roll(b, halo, 0))
-            high = jnp.where(low_rows, pltpu.roll(a, halo, 0), b)
-            inner_ref[h, :, lanes] = jnp.where(even, high, low)
-            outer_ref[h, :, lanes] = jnp.where(even, low, high)
-        for k in range(2):
-            start = plan.width + k * LANES
-            outer_ref[h, :, start : start + LANES] = in_ref[2 * h + k, :, plan.width :]
+            low, high = half_tile(in_ref, s, t, 0), half_tile(in_ref, s, t, 1)
+            inner_ref[s, :, lanes] = jnp.where(even, high, low)
+            outer_ref[s, :, lanes] = jnp.where(even, low, high)
+        inner_ref[s, :, plan.width :] = half_tile(in_ref, s, plan.tiles, 0)
 
 
 def two_part_dot(parts, matrix):
@@ -451,8 +453,7 @@
     return out
 
 
-def collide_rows(plan, products, state_ref, post_ref, aux_ref, u_ref, force_ref, rows, begin=False):
-    to_columns, near = products
+def collide_rows(plan, to_columns, state_ref, post_ref, aux_ref, u_ref, force_ref, rows, begin=False):
     for lanes in tile_lanes(plan):
         popul = [state_ref[i, rows, lanes] for i in range(19)]
         density = popul[0]
@@ -466,28 +467,16 @@
             falling = [popul[i] for i in range(19) if VELOCITIES[i, a] == -1]
             u_ref[a, rows, lanes] = (sum(rising[1:], rising[0]) - sum(falling[1:], falling[0])) * inverse
     rate = state_ref[FIELD_RATE, rows]
-    live = (rate > 0.0).astype(jnp.float32)
     velocity = [state_ref[field, rows] for field in FIELD_V]
     speed = on_bins(plan, [u_ref[a, rows] for a in range(3)], state_ref[FIELD_CELL, rows])
     drags = [drag_factor * rate * (speed[a] - velocity[a]) for a in range(3)]
-    moving = [velocity[a] * live for a in range(3)]
     if begin:
         *forces, solid = to_columns(drags + [rate])
-        *moving, count = near(moving + [live])
         aux_ref[0, rows] = 1.0 / (1.0 + solid)
-        aux_ref[1, rows] = count
     else:
         forces = to_columns(drags)
-        moving = near(moving)
-        count = aux_ref[1, rows]
     for a, force in enumerate(forces):
         force_ref[a, rows] = force
-    for a in range(3):
-        push = contact_stiffness * live * (moving[a] - count * velocity[a])
-        updated = velocity[a] + drags[a] + push
-        if a == 2:
-            updated = updated - gravity * live
-        state_ref[FIELD_V[a], rows] = updated
     keep, take = 1.0 - 1.0 / relax_time, 1.0 / relax_time
     for lanes in tile_lanes(plan):
         density, inverse = u_ref[3, rows, lanes], u_ref[4, rows, lanes]
@@ -511,9 +500,31 @@
             share_i = shares[WEIGHTS[i]]
             post_ref[i, rows, lanes] = keep * state_ref[i, rows, lanes] + share_i * (level + along)
             post_ref[i + 1, rows, lanes] = keep * state_ref[i + 1, rows, lanes] + share_i * (level - along)
-
-
-def stream_rows(plan, state_ref, post_ref, ground, ceiling):
+    return drags
+
+
+def move_grains(near, state_ref, aux_ref, rows, drags, begin=False):
+    live = (state_ref[FIELD_RATE, rows] > 0.0).astype(jnp.float32)
+    velocity = [state_ref[field, rows] for field in FIELD_V]
+    moving = [velocity[a] * live for a in range(3)]
+    if begin:
+        *moving, count = near(moving + [live])
+        aux_ref[1, rows] = count
+    else:
+        moving = near(moving)
+        count = aux_ref[1, rows]
+    for a in range(3):
+        push = contact_stiffness * live * (moving[a] - count * velocity[a])
+        updated = velocity[a] + drags[a] + push
+        if a == 2:
+            updated = updated - gravity * live
+        state_ref[FIELD_V[a], rows] = updated
+
+
+def stream_rows(plan, state_ref, post_ref):
+    window, layer = plan.place()
+    ground = (window == 0) & (layer == 0)
+    ceiling = (window == plan.sources - 1) & (layer == plan.n_gz - 1)
     rows, group, dx, dy = plan.rows, plan.group, plan.dx, plan.dy
     lane = lax.broadcasted_iota(jnp.int32, (rows, LANES), 1)
     row = lax.broadcasted_iota(jnp.int32, (rows, LANES), 0)
@@ -539,75 +550,96 @@
             state_ref[i, :, lanes] = x
 
 
-def settle_kernel(plan, in_ref, state_ref, post_ref, aux_ref, column_ref, link_ref, u_ref, force_ref):
+def settle_kernel(plan, in_ref, state_ref, post_ref, aux_ref, column_ref, u_ref, force_ref):
     own = slice(0, plan.own)
-    unpack(plan, lambda s, t: in_ref[s, :, t * LANES : (t + 1) * LANES], state_ref, own)
+
+    def own_tile(s, t):
+        return jnp.concatenate([half_tile(in_ref, s, t, 0), half_tile(in_ref, s, t, 1)], axis=0)
+
+    unpack(plan, own_tile, state_ref, own)
     column_ref[...] = bins_on_columns(plan.columns, state_ref[FIELD_CELL, 0:1, :])
-    contact_blocks(plan, lambda s: in_ref[s, :, plan.width :], link_ref)
-    products = (
+    drags = collide_rows(
+        plan,
         lambda parts: two_part_dot(parts, column_ref[...]),
-        lambda parts: touching(plan, parts, link_ref),
-    )
-    collide_rows(plan, products, state_ref, post_ref, aux_ref, u_ref, force_ref, own, True)
-
-
-def substeps_kernel(plan, settled_ref, collided_ref, fixed_ref, column_ref, link_ref, inner_ref, outer_ref,
-                    out_ref, state_ref, post_ref, aux_ref, u_ref, force_ref, other_column_ref, other_link_ref):
-    rows, columns, group, per = plan.rows, plan.columns, plan.group, plan.per_tile
-    halo, own = plan.halo, plan.own
-    window, layer = plan.place()
+        state_ref, post_ref, aux_ref, u_ref, force_ref, own, True,
+    )
+    for a in range(3):
+        aux_ref[2 + a, own] = drags[a]
+
+
+def contact_kernel(plan, in_ref, inner_ref, settled_ref, fixed_ref, state_ref, aux_ref, link_ref, packed_ref):
+    window, _ = plan.place()
     even = lax.rem(window, 2) == 0
-    first, last = window == 0, window == plan.sources - 1
-    ground, ceiling = first & (layer == 0), last & (layer == plan.n_gz - 1)
-    tile_row = lax.broadcasted_iota(jnp.int32, (SUBLANES, LANES), 0)
+    own = slice(0, plan.own)
+
+    def packed(s):
+        mine, sibling = half_tile(in_ref, s, plan.tiles, 0), inner_ref[s, :, plan.width :]
+        return jnp.concatenate([jnp.where(even, mine, sibling), jnp.where(even, sibling, mine)], axis=0)
+
+    for s in range(plan.sources):
+        packed_ref[s] = packed(s)
+    contact_blocks(plan, lambda s: packed_ref[s], link_ref)
+    drags = [aux_ref[2 + a, own] for a in range(3)]
+    move_grains(lambda parts: touching(plan, parts, link_ref), state_ref, aux_ref, own, drags, True)
+
+
+def both_layers(plan, product, own_matrix, other_matrix):
+    window, _ = plan.place()
+    halo_row = lax.broadcasted_iota(jnp.int32, (SUBLANES, plan.columns), 0)
+    last, first = window == plan.sources - 1, window == 0
+    foreign = (last & (halo_row < plan.halo)) | (first & (halo_row >= plan.halo))
+    own = plan.own
+
+    def call(parts):
+        mine = product(parts, own_matrix)
+        others = product([x[-SUBLANES:] for x in parts], other_matrix)
+        if parts[0].shape[0] == SUBLANES:
+            return [jnp.where(foreign, b, a) for a, b in zip(mine, others)]
+        return [jnp.concatenate([a[:own], jnp.where(foreign, b, a[own:])], axis=0) for a, b in zip(mine, others)]
+
+    return call
+
+
+def columns_of(plan, column_ref, other_column_ref):
+    return both_layers(plan, lambda x, m: two_part_dot(x, m[...]), column_ref, other_column_ref)
+
+
+def halo_kernel(plan, settled_ref, collided_ref, fixed_ref, column_ref, inner_ref, outer_ref,
+                state_ref, post_ref, aux_ref, other_column_ref, u_ref, force_ref):
+    rows, own = plan.rows, plan.own
+    window, _ = plan.place()
+    even = lax.rem(window, 2) == 0
     beyond = slice(own, rows)
 
     def halo_tile(s, t):
         at = slice(t * LANES, (t + 1) * LANES)
-        inner, outer = inner_ref[s // 2, :, at], outer_ref[s // 2, :, at]
-        below = jnp.where(even, outer, inner)
-        above = jnp.where(even, inner, outer)
-        if s % 2:
-            above = pltpu.roll(above, halo, 0)
-        else:
-            below = pltpu.roll(below, halo, 0)
-        return jnp.where(tile_row < halo, above, below)
+        inner, outer = inner_ref[s, :, at], outer_ref[s, :, at]
+        return jnp.concatenate([jnp.where(even, inner, outer), jnp.where(even, outer, inner)], axis=0)
 
     unpack(plan, halo_tile, state_ref, beyond)
-    other_cells = jnp.where(first, state_ref[FIELD_CELL, rows - 1 : rows, :], state_ref[FIELD_CELL, own : own + 1, :])
-    other_column_ref[...] = bins_on_columns(columns, other_cells)
-
-    def other_contacts(s):
-        start = plan.width + s % 2 * LANES
-        return outer_ref[s // 2, :, start : start + LANES]
-
-    contact_blocks(plan, other_contacts, other_link_ref)
-
-    halo_row = lax.broadcasted_iota(jnp.int32, (SUBLANES, columns), 0)
-    foreign = (last & (halo_row < halo)) | (first & (halo_row >= halo))
-
-    def both_layers(product, own_matrix, other_matrix):
-        def call(parts):
-            mine = product(parts, own_matrix)
-            others = product([x[-SUBLANES:] for x in parts], other_matrix)
-            if parts[0].shape[0] == SUBLANES:
-                return [jnp.where(foreign, b, a) for a, b in zip(mine, others)]
-            return [
-                jnp.concatenate([a[:own], jnp.where(foreign, b, a[own:])], axis=0) for a, b in zip(mine, others)
-            ]
-
-        return call
-
-    products = (
-        both_layers(lambda x, m: two_part_dot(x, m[...]), column_ref, other_column_ref),
-        both_layers(lambda x, m: touching(plan, x, m), link_ref, other_link_ref),
-    )
-    collide_rows(plan, products, state_ref, post_ref, aux_ref, u_ref, force_ref, beyond, True)
-    stream_rows(plan, state_ref, post_ref, ground, ceiling)
+    other_cells = jnp.where(window == 0, state_ref[FIELD_CELL, rows - 1 : rows, :], state_ref[FIELD_CELL, own : own + 1, :])
+    other_column_ref[...] = bins_on_columns(plan.columns, other_cells)
+    to_columns = columns_of(plan, column_ref, other_column_ref)
+    drags = collide_rows(plan, to_columns, state_ref, post_ref, aux_ref, u_ref, force_ref, beyond, True)
+    for a in range(3):
+        aux_ref[2 + a, beyond] = drags[a]
+    stream_rows(plan, state_ref, post_ref)
+
+
+def substeps_kernel(plan, settled_ref, fixed_ref, column_ref, other_column_ref, link_ref, packed_ref,
+                    out_ref, state_ref, aux_ref, post_ref, u_ref, force_ref, other_link_ref):
+    rows, own, halo, group, per = plan.rows, plan.own, plan.halo, plan.group, plan.per_tile
+    beyond = slice(own, rows)
+    contact_blocks(plan, lambda s: packed_ref[s], other_link_ref)
+    to_columns = columns_of(plan, column_ref, other_column_ref)
+    near = both_layers(plan, lambda x, m: touching(plan, x, m), link_ref, other_link_ref)
+    move_grains(near, state_ref, aux_ref, beyond, [aux_ref[2 + a, beyond] for a in range(3)], True)
+    refs = (state_ref, post_ref, aux_ref, u_ref, force_ref)
 
     def step(_, carry):
-        collide_rows(plan, products, state_ref, post_ref, aux_ref, u_ref, force_ref, slice(0, rows))
-        stream_rows(plan, state_ref, post_ref, ground, ceiling)
+        drags = collide_rows(plan, to_columns, *refs, slice(0, rows))
+        move_grains(near, state_ref, aux_ref, slice(0, rows), drags)
+        stream_rows(plan, state_ref, post_ref)
         return carry
 
     lax.fori_loop(1, SUBSTEPS, step, 0)
@@ -660,7 +692,7 @@
     group, bins, sources = plan.group, plan.bins, plan.sources
     rows, columns, own = plan.rows, plan.columns, plan.own
     f32, bf16, i32 = jnp.float32, jnp.bfloat16, jnp.int32
-    half = sources // 2
+    halo = plan.halo
 
     def call(kernel, shapes, inputs, scratch=(), where=(VMEM, VMEM), aliases=None):
         if where[0] is HBM:
@@ -678,7 +710,7 @@
 
     (outgoing,) = call(
         prepare_kernel,
-        [((sources, own, plan.wide), f32)],
+        [((sources, halo, plan.wide), f32)],
         (
             populations.reshape(19 * group, LANES),
             grain_velocity.reshape(3 * bins, LANES),
@@ -700,7 +732,7 @@
     incoming = lax.all_to_all(outgoing, layer_axes, split_axis=0, concat_axis=0, tiled=True)
     inner, outer = call(
         edges_kernel,
-        [((half, SUBLANES, plan.width), f32), ((half, SUBLANES, plan.width + 2 * LANES), f32)],
+        [((sources, halo, plan.width + LANES), f32), ((sources, halo, plan.width), f32)],
         (incoming,),
     )
     inner = lax.ppermute(inner, every_axis, plan.swaps(0))
@@ -708,25 +740,39 @@
     carried = [
         ((plan.fields, rows, columns), f32),
         ((19, rows, columns), f32),
-        ((2, rows, columns), f32),
+        ((5, rows, columns), f32),
     ]
     moments_and_forces = (pltpu.VMEM((5, rows, columns), f32), pltpu.VMEM((3, rows, columns), f32))
-    *settled, column, link = call(
+    state, post, aux, column = call(
         settle_kernel,
-        carried + [((columns, columns), bf16), ((columns, LANES), bf16)],
+        carried + [((columns, columns), bf16)],
         (incoming,),
         moments_and_forces,
     )
+    state, aux, link, packed = call(
+        contact_kernel,
+        [carried[0], carried[2], ((columns, LANES), bf16), ((sources, SUBLANES, LANES), f32)],
+        (incoming, inner, state, aux),
+        aliases={2: 0, 3: 1},
+    )
+    packed = lax.ppermute(packed, every_axis, plan.swaps(1))
+    state, _, aux, other_column = call(
+        halo_kernel,
+        carried + [((columns, columns), bf16)],
+        (state, post, aux, column, inner, outer),
+        moments_and_forces,
+        aliases={0: 0, 1: 1, 2: 2},
+    )
     back, *_ = call(
         substeps_kernel,
-        [((sources, plan.halo, plan.returned), f32)] + carried,
-        (*settled, column, link, inner, outer),
+        [((sources, halo, plan.returned), f32), carried[0], carried[2]],
+        (state, aux, column, other_column, link, packed),
         (
+            pltpu.VMEM((19, rows, columns), f32),
             *moments_and_forces,
-            pltpu.VMEM((columns, columns), bf16),
             pltpu.VMEM((columns, LANES), bf16),
         ),
-        aliases={0: 1, 1: 2, 2: 3},
+        aliases={0: 1, 1: 2},
     )
     result = lax.all_to_all(back, layer_axes, split_axis=0, concat_axis=0, tiled=True)
     fluid, velocity = call(

time: 49.1 us -> 48.1 us (0.980)
  waiting for transfers between devices: 4.24 us -> 2.6 us
  starting transfers between devices: 1.56 us -> 2.49 us
  blocking collectives: 35.3 us -> 34.5 us
  Pallas kernels: 7.13 us -> 7.65 us
    ppermute x1, waiting for transfers between devices: 3.44 us -> 2.45 us  [windows_body(): outer = lax.ppermute(outer, every_axis, plan.swaps(1))]
    ppermute x0 -> x1, starting transfers between devices: none -> 0.82 us  [windows_body(): packed = lax.ppermute(packed, every_axis, plan.swaps(1))]
    ppermute x1, waiting for transfers between devices: 0.81 us -> 0.01 us  [windows_body(): inner = lax.ppermute(inner, every_axis, plan.swaps(0))]
    all_to_all x1, blocking collectives: 20.4 us -> 19.9 us  [windows_body(): lax.all_to_all(outgoing, layer_axes, split_axis=0, concat_axis=0, tiled=T...]
    pallas_call x5 -> x7, Pallas kernels: 7.13 us -> 7.65 us  [call(): pl.pallas_call(lambda *refs: kernel(plan, *refs), out_shape=shapes, in_sp...]
  transfers between devices with their start and end apart: 2 -> 3, of which waited for: 2 -> 2; matrix products, arithmetic and copies ran while one was open for 0% -> 0% of each run, Pallas kernels for 1% -> 4%
where the time goes in v6:
time: 48.1 us; the launch traced here: 47.9 us
  blocking collectives  34.5 us (72%)
  Pallas kernels  7.65 us (16%)
  waiting for transfers between devices  2.6 us (5%)
  starting transfers between devices  2.49 us (5%)
  between operations  0.69 us (1%)
    all_to_all x1, blocking collectives, windows_body(): lax.all_to_all(outgoing, layer_axes, split_axis=0, concat_axis=0, tiled=T...  19.9 us
    all_to_all x1, blocking collectives, windows_body(): lax.all_to_all(back, layer_axes, split_axis=0, concat_axis=0, tiled=True)  14.6 us
    pallas_call x7, Pallas kernels, call(): pl.pallas_call(lambda *refs: kernel(plan, *refs), out_shape=shapes, in_sp...  7.65 us
    ppermute x1, waiting for transfers between devices, windows_body(): outer = lax.ppermute(outer, every_axis, plan.swaps(1))  2.45 us
    ppermute x1, starting transfers between devices, windows_body(): outer = lax.ppermute(outer, every_axis, plan.swaps(1))  1.49 us
  transfers between devices with their start and end apart: 3, of which 2 were waited for; matrix products, arithmetic and copies ran while one was open for 0% of the time, Pallas kernels for 4%

profile of v6, /device:TPU:0, one launch (start us, length us, event | category | flops | bytes accessed | tf_op | source)
XLA Modules:
  0.0 47.9 jit_solution(10349885289420112937)
XLA Ops:
  0.6 1.4 %shard_map.77 = f32[16,4,1664]{2,1,0:T(4,128)S(1)} custom-call(f32[608,128]{1,0:T(8,128)} %bitcast.5, f32[96,128]{1,0:T(8,128)} %bitcast.6, f32[32,128]{1,0:T(8,128)} %refs_2_.1, s32[32,128]{1,0:T(8,128)} %refs_3_.1, s32[32,32]{1,0:T(8,128)} %refs_4_.1, s32[1,32]{1,0:T(1,128)} %bitcast.7), custom_call_target="tpu_custom_call" | custom-call | tf_op jit(solution)/shard_map/pallas_call | solution.py:701
  2.1 19.9 %all_to_all.10.refs_0_ = f32[16,4,1664]{2,1,0:T(4,128)S(1)} all-to-all(f32[16,4,1664]{2,1,0:T(4,128)S(1)} %shard_map.77), channel_id=1, replica_groups=mesh['gx'=4,'gy'=4,'gz'=2] {'gx','gy'}, dimensions={0} | all-to-all | bytes 851968 | tf_op jit(solution)/shard_map/all_to_all | solution.py:732
  22.0 0.1 shard_map.78
  22.1 0.2 collective-permute-start
  22.2 1.5 %collective-permute-start.1 = (f32[16,4,768]{2,1,0:T(4,128)S(1)}, f32[16,4,768]{2,1,0:T(4,128)S(1)}, u32[]{:S(2)}, u32[]{:S(2)}) collective-permute-start(f32[16,4,768]{2,1,0:T(4,128)S(1)} %get-tuple-element.25), channel_id=1, source_target_pairs={{2,4},{4,2},{6,14},{14,6},{12,10},{10,12},{8,16},{16,8},{18,20},{2... | collective-permute-start | bytes 589832 | tf_op jit(solution)/shard_map/ppermute | solution.py:739
  23.7 0.6 %shard_map.79 = (f32[24,16,512]{2,1,0:T(8,128)S(1)}, f32[19,16,512]{2,1,0:T(8,128)S(1)}, f32[5,16,512]{2,1,0:T(8,128)S(1)}, bf16[512,512]{1,0:T(8,128)(2,1)S(1)}) custom-call(f32[16,4,1664]{2,1,0:T(4,128)S(1)} %all_to_all.10.refs_0_), custom_call_target="tpu_custom_call" | custom-call | tf_op jit(solution)/shard_map/pallas_call | solution.py:701
  24.4 0.0 collective-permute-done.refs_1_.refs_4_
  24.4 0.3 shard_map.80
  24.6 0.8 %collective-permute-start.2 = (f32[16,8,128]{2,1,0:T(8,128)S(1)}, f32[16,8,128]{2,1,0:T(8,128)S(1)}, u32[]{:S(2)}, u32[]{:S(2)}) collective-permute-start(f32[16,8,128]{2,1,0:T(8,128)S(1)} %get-tuple-element.30), channel_id=1, source_target_pairs={{2,4},{4,2},{6,14},{14,6},{12,10},{10,12},{8,16},{16,8},{18,20},{2... | collective-permute-start | bytes 196616 | tf_op jit(solution)/shard_map/ppermute | solution.py:758
  25.5 2.5 %collective-permute-done.1.refs_5_ = f32[16,4,768]{2,1,0:T(4,128)S(1)} collective-permute-done((f32[16,4,768]{2,1,0:T(4,128)S(1)}, f32[16,4,768]{2,1,0:T(4,128)S(1)}, u32[]{:S(2)}, u32[]{:S(2)}) %collective-permute-start.1) | collective-permute-done | bytes 196640 | tf_op jit(solution)/shard_map/ppermute | solution.py:739
  27.9 0.9 %shard_map.81 = (f32[24,16,512]{2,1,0:T(8,128)S(1)}, f32[19,16,512]{2,1,0:T(8,128)S(1)}, f32[5,16,512]{2,1,0:T(8,128)S(1)}, bf16[512,512]{1,0:T(8,128)(2,1)S(1)}) custom-call(f32[24,16,512]{2,1,0:T(8,128)S(1)} %get-tuple-element.21.refs_0_, f32[19,16,512]{2,1,0:T(8,128)S(1)} %get-tuple-element.22.refs_1_, ...), custom_call_target="tpu_custom_call", output_to_operand_aliasing={{0}: (0, {}), {1}: (1, {}), {2}: (2, {})} | custom-call | tf_op jit(solution)/shard_map/pallas_call | solution.py:701
  28.8 0.1 collective-permute-done.2.refs_5_
  29.0 3.3 %shard_map.82 = (f32[16,4,1408]{2,1,0:T(4,128)S(1)}, f32[24,16,512]{2,1,0:T(8,128)S(1)}, f32[5,16,512]{2,1,0:T(8,128)S(1)}) custom-call(f32[24,16,512]{2,1,0:T(8,128)S(1)} %get-tuple-element.26.refs_0_, f32[5,16,512]{2,1,0:T(8,128)S(1)} %get-tuple-element.27.refs_1_, ...), custom_call_target="tpu_custom_call", output_to_operand_aliasing={{1}: (0, {}), {2}: (1, {})} | custom-call | tf_op jit(solution)/shard_map/pallas_call | solution.py:701
  32.3 14.6 %all_to_all.11.refs_0_ = f32[16,4,1408]{2,1,0:T(4,128)S(1)} all-to-all(f32[16,4,1408]{2,1,0:T(4,128)S(1)} %get-tuple-element.31), channel_id=1, replica_groups=mesh['gx'=4,'gy'=4,'gz'=2] {'gx','gy'}, dimensions={0} | all-to-all | bytes 720896 | tf_op jit(solution)/shard_map/all_to_all | solution.py:777
  46.9 1.0 %shard_map.83 = (f32[608,128]{1,0:T(8,128)}, f32[96,128]{1,0:T(8,128)}) custom-call(f32[16,4,1408]{2,1,0:T(4,128)S(1)} %all_to_all.11.refs_0_), custom_call_target="tpu_custom_call" | custom-call | tf_op jit(solution)/shard_map/pallas_call | solution.py:701
Async XLA Ops:
  22.1 2.3 %collective-permute-start = (f32[16,4,896]{2,1,0:T(4,128)S(1)}, f32[16,4,896]{2,1,0:T(4,128)S(1)}, u32[]{:S(2)}, u32[]{:S(2)}) collective-permute-start(f32[16,4,896]{2,1,0:T(4,128)S(1)} %get-tuple-element.18), channel_id=1, source_target_pairs={{0,2},{2,0},{4,6},{6,4},{14,12},{12,14},{10,8},{8,10},{16,18},{18,... | collective-permute-start | bytes 688136 | tf_op jit(solution)/shard_map/ppermute | solution.py:738
  22.2 5.7 %collective-permute-start.1 = (f32[16,4,768]{2,1,0:T(4,128)S(1)}, f32[16,4,768]{2,1,0:T(4,128)S(1)}, u32[]{:S(2)}, u32[]{:S(2)}) collective-permute-start(f32[16,4,768]{2,1,0:T(4,128)S(1)} %get-tuple-element.25), channel_id=1, source_target_pairs={{2,4},{4,2},{6,14},{14,6},{12,10},{10,12},{8,16},{16,8},{18,20},{2... | collective-permute-start | bytes 589832 | tf_op jit(solution)/shard_map/ppermute | solution.py:739
  24.6 4.3 %collective-permute-start.2 = (f32[16,8,128]{2,1,0:T(8,128)S(1)}, f32[16,8,128]{2,1,0:T(8,128)S(1)}, u32[]{:S(2)}, u32[]{:S(2)}) collective-permute-start(f32[16,8,128]{2,1,0:T(8,128)S(1)} %get-tuple-element.30), channel_id=1, source_target_pairs={{2,4},{4,2},{6,14},{14,6},{12,10},{10,12},{8,16},{16,8},{18,20},{2... | collective-permute-start | bytes 196616 | tf_op jit(solution)/shard_map/ppermute | solution.py:758

commit v7 on v6

--- a/solution.py
+++ b/solution.py
@@ -1,3 +1,4 @@
+import functools
 import jax
 import jax.numpy as jnp
 import numpy as np
@@ -521,7 +522,7 @@
         state_ref[FIELD_V[a], rows] = updated
 
 
-def stream_rows(plan, state_ref, post_ref):
+def stream_rows(plan, state_ref, post_ref, keep=None):
     window, layer = plan.place()
     ground = (window == 0) & (layer == 0)
     ceiling = (window == plan.sources - 1) & (layer == plan.n_gz - 1)
@@ -534,20 +535,22 @@
     tiles = tile_lanes(plan)
     for i in range(19):
         cx, cy, cz = (int(c) for c in VELOCITIES[i])
-        moved = [post_ref[i, :, lanes] for lanes in tiles]
+        take = rows if cz or keep is None else keep
+        moved = [post_ref[i, :take, lanes] for lanes in tiles]
         if cx or cy:
             y = lax.rem(lane_y - cy + plan.n_gy * dy, plan.n_gy * dy)
             x = lax.rem(lane_x - cx + dx, dx)
             from_lane = lax.div(y, dy) * group + x * dy + lax.rem(y, dy)
+            from_lane = from_lane[:take]
             moved = [jnp.take_along_axis(x, from_lane, axis=1, mode="promise_in_bounds") for x in moved]
         if cx:
-            edge = lane_x == (0 if cx == 1 else dx - 1)
+            edge = lane_x[:take] == (0 if cx == 1 else dx - 1)
             moved = [jnp.where(edge, moved[(q - cx) % len(tiles)], moved[q]) for q in range(len(tiles))]
         for x, lanes in zip(moved, tiles):
             if cz:
                 x = pltpu.roll(x, cz % rows, 0)
                 x = jnp.where(bottom if cz == 1 else top, post_ref[OPPOSITE[i], :, lanes], x)
-            state_ref[i, :, lanes] = x
+            state_ref[i, :keep, lanes] = x[:keep]
 
 
 def settle_kernel(plan, in_ref, state_ref, post_ref, aux_ref, column_ref, u_ref, force_ref):
@@ -636,13 +639,16 @@
     move_grains(near, state_ref, aux_ref, beyond, [aux_ref[2 + a, beyond] for a in range(3)], True)
     refs = (state_ref, post_ref, aux_ref, u_ref, force_ref)
 
-    def step(_, carry):
-        drags = collide_rows(plan, to_columns, *refs, slice(0, rows))
-        move_grains(near, state_ref, aux_ref, slice(0, rows), drags)
-        stream_rows(plan, state_ref, post_ref)
-        return carry
-
-    lax.fori_loop(1, SUBSTEPS, step, 0)
+    everywhere, mine = slice(0, rows), slice(0, own)
+    for step in range(1, SUBSTEPS):
+        drags = collide_rows(plan, to_columns, *refs, everywhere)
+        if step < SUBSTEPS - 1:
+            move_grains(near, state_ref, aux_ref, everywhere, drags)
+            stream_rows(plan, state_ref, post_ref)
+        else:
+            own_near = functools.partial(touching, plan, matrix=link_ref)
+            move_grains(own_near, state_ref, aux_ref, mine, [d[mine] for d in drags])
+            stream_rows(plan, state_ref, post_ref, own)
 
     first_half = lax.broadcasted_iota(jnp.int32, (halo, LANES), 1) < LANES // 2
     for t in range(plan.tiles):

time: 48.1 us -> 47.6 us (0.990)
  Pallas kernels: 7.65 us -> 7.16 us
    pallas_call x7, Pallas kernels: 7.65 us -> 7.16 us  [call(): pl.pallas_call(lambda *refs: kernel(plan, *refs), out_shape=shapes, in_sp...]
where the time goes in v7:
time: 47.6 us; the launch traced here: 47.4 us
  blocking collectives  34.5 us (72%)
  Pallas kernels  7.16 us (15%)
  waiting for transfers between devices  2.6 us (5%)
  starting transfers between devices  2.49 us (5%)
  between operations  0.69 us (1%)
    all_to_all x1, blocking collectives, windows_body(): lax.all_to_all(outgoing, layer_axes, split_axis=0, concat_axis=0, tiled=T...  19.9 us
    all_to_all x1, blocking collectives, windows_body(): lax.all_to_all(back, layer_axes, split_axis=0, concat_axis=0, tiled=True)  14.6 us
    pallas_call x7, Pallas kernels, call(): pl.pallas_call(lambda *refs: kernel(plan, *refs), out_shape=shapes, in_sp...  7.16 us
    ppermute x1, waiting for transfers between devices, windows_body(): outer = lax.ppermute(outer, every_axis, plan.swaps(1))  2.45 us
    ppermute x1, starting transfers between devices, windows_body(): outer = lax.ppermute(outer, every_axis, plan.swaps(1))  1.49 us
  transfers between devices with their start and end apart: 3, of which 2 were waited for; matrix products, arithmetic and copies ran while one was open for 0% of the time, Pallas kernels for 4%

profile of v7, /device:TPU:0, one launch (start us, length us, event | category | flops | bytes accessed | tf_op | source)
XLA Modules:
  0.0 47.4 jit_solution(12146938990778609998)
XLA Ops:
  0.6 1.4 %shard_map.77 = f32[16,4,1664]{2,1,0:T(4,128)S(1)} custom-call(f32[608,128]{1,0:T(8,128)} %bitcast.5, f32[96,128]{1,0:T(8,128)} %bitcast.6, f32[32,128]{1,0:T(8,128)} %refs_2_.1, s32[32,128]{1,0:T(8,128)} %refs_3_.1, s32[32,32]{1,0:T(8,128)} %refs_4_.1, s32[1,32]{1,0:T(1,128)} %bitcast.7), custom_call_target="tpu_custom_call" | custom-call | tf_op jit(solution)/shard_map/pallas_call | solution.py:707
  2.1 19.9 %all_to_all.10.refs_0_ = f32[16,4,1664]{2,1,0:T(4,128)S(1)} all-to-all(f32[16,4,1664]{2,1,0:T(4,128)S(1)} %shard_map.77), channel_id=1, replica_groups=mesh['gx'=4,'gy'=4,'gz'=2] {'gx','gy'}, dimensions={0} | all-to-all | bytes 851968 | tf_op jit(solution)/shard_map/all_to_all | solution.py:738
  22.0 0.1 shard_map.78
  22.1 0.2 collective-permute-start
  22.2 1.5 %collective-permute-start.1 = (f32[16,4,768]{2,1,0:T(4,128)S(1)}, f32[16,4,768]{2,1,0:T(4,128)S(1)}, u32[]{:S(2)}, u32[]{:S(2)}) collective-permute-start(f32[16,4,768]{2,1,0:T(4,128)S(1)} %get-tuple-element.25), channel_id=1, source_target_pairs={{2,4},{4,2},{6,14},{14,6},{12,10},{10,12},{8,16},{16,8},{18,20},{2... | collective-permute-start | bytes 589832 | tf_op jit(solution)/shard_map/ppermute | solution.py:745
  23.7 0.6 %shard_map.79 = (f32[24,16,512]{2,1,0:T(8,128)S(1)}, f32[19,16,512]{2,1,0:T(8,128)S(1)}, f32[5,16,512]{2,1,0:T(8,128)S(1)}, bf16[512,512]{1,0:T(8,128)(2,1)S(1)}) custom-call(f32[16,4,1664]{2,1,0:T(4,128)S(1)} %all_to_all.10.refs_0_), custom_call_target="tpu_custom_call" | custom-call | tf_op jit(solution)/shard_map/pallas_call | solution.py:707
  24.4 0.0 collective-permute-done.refs_1_.refs_4_
  24.4 0.3 shard_map.80
  24.6 0.8 %collective-permute-start.2 = (f32[16,8,128]{2,1,0:T(8,128)S(1)}, f32[16,8,128]{2,1,0:T(8,128)S(1)}, u32[]{:S(2)}, u32[]{:S(2)}) collective-permute-start(f32[16,8,128]{2,1,0:T(8,128)S(1)} %get-tuple-element.30), channel_id=1, source_target_pairs={{2,4},{4,2},{6,14},{14,6},{12,10},{10,12},{8,16},{16,8},{18,20},{2... | collective-permute-start | bytes 196616 | tf_op jit(solution)/shard_map/ppermute | solution.py:764
  25.5 2.5 %collective-permute-done.1.refs_5_ = f32[16,4,768]{2,1,0:T(4,128)S(1)} collective-permute-done((f32[16,4,768]{2,1,0:T(4,128)S(1)}, f32[16,4,768]{2,1,0:T(4,128)S(1)}, u32[]{:S(2)}, u32[]{:S(2)}) %collective-permute-start.1) | collective-permute-done | bytes 196640 | tf_op jit(solution)/shard_map/ppermute | solution.py:745
  27.9 0.9 %shard_map.81 = (f32[24,16,512]{2,1,0:T(8,128)S(1)}, f32[19,16,512]{2,1,0:T(8,128)S(1)}, f32[5,16,512]{2,1,0:T(8,128)S(1)}, bf16[512,512]{1,0:T(8,128)(2,1)S(1)}) custom-call(f32[24,16,512]{2,1,0:T(8,128)S(1)} %get-tuple-element.21.refs_0_, f32[19,16,512]{2,1,0:T(8,128)S(1)} %get-tuple-element.22.refs_1_, ...), custom_call_target="tpu_custom_call", output_to_operand_aliasing={{0}: (0, {}), {1}: (1, {}), {2}: (2, {})} | custom-call | tf_op jit(solution)/shard_map/pallas_call | solution.py:707
  28.8 0.1 collective-permute-done.2.refs_5_
  29.0 2.8 %shard_map.82 = (f32[16,4,1408]{2,1,0:T(4,128)S(1)}, f32[24,16,512]{2,1,0:T(8,128)S(1)}, f32[5,16,512]{2,1,0:T(8,128)S(1)}) custom-call(f32[24,16,512]{2,1,0:T(8,128)S(1)} %get-tuple-element.26.refs_0_, f32[5,16,512]{2,1,0:T(8,128)S(1)} %get-tuple-element.27.refs_1_, ...), custom_call_target="tpu_custom_call", output_to_operand_aliasing={{1}: (0, {}), {2}: (1, {})} | custom-call | tf_op jit(solution)/shard_map/pallas_call | solution.py:707
  31.8 14.6 %all_to_all.11.refs_0_ = f32[16,4,1408]{2,1,0:T(4,128)S(1)} all-to-all(f32[16,4,1408]{2,1,0:T(4,128)S(1)} %get-tuple-element.31), channel_id=1, replica_groups=mesh['gx'=4,'gy'=4,'gz'=2] {'gx','gy'}, dimensions={0} | all-to-all | bytes 720896 | tf_op jit(solution)/shard_map/all_to_all | solution.py:783
  46.4 1.0 %shard_map.83 = (f32[608,128]{1,0:T(8,128)}, f32[96,128]{1,0:T(8,128)}) custom-call(f32[16,4,1408]{2,1,0:T(4,128)S(1)} %all_to_all.11.refs_0_), custom_call_target="tpu_custom_call" | custom-call | tf_op jit(solution)/shard_map/pallas_call | solution.py:707
Async XLA Ops:
  22.1 2.3 %collective-permute-start = (f32[16,4,896]{2,1,0:T(4,128)S(1)}, f32[16,4,896]{2,1,0:T(4,128)S(1)}, u32[]{:S(2)}, u32[]{:S(2)}) collective-permute-start(f32[16,4,896]{2,1,0:T(4,128)S(1)} %get-tuple-element.18), channel_id=1, source_target_pairs={{0,2},{2,0},{4,6},{6,4},{14,12},{12,14},{10,8},{8,10},{16,18},{18,... | collective-permute-start | bytes 688136 | tf_op jit(solution)/shard_map/ppermute | solution.py:744
  22.2 5.7 %collective-permute-start.1 = (f32[16,4,768]{2,1,0:T(4,128)S(1)}, f32[16,4,768]{2,1,0:T(4,128)S(1)}, u32[]{:S(2)}, u32[]{:S(2)}) collective-permute-start(f32[16,4,768]{2,1,0:T(4,128)S(1)} %get-tuple-element.25), channel_id=1, source_target_pairs={{2,4},{4,2},{6,14},{14,6},{12,10},{10,12},{8,16},{16,8},{18,20},{2... | collective-permute-start | bytes 589832 | tf_op jit(solution)/shard_map/ppermute | solution.py:745
  24.6 4.3 %collective-permute-start.2 = (f32[16,8,128]{2,1,0:T(8,128)S(1)}, f32[16,8,128]{2,1,0:T(8,128)S(1)}, u32[]{:S(2)}, u32[]{:S(2)}) collective-permute-start(f32[16,8,128]{2,1,0:T(8,128)S(1)} %get-tuple-element.30), channel_id=1, source_target_pairs={{2,4},{4,2},{6,14},{14,6},{12,10},{10,12},{8,16},{16,8},{18,20},{2... | collective-permute-start | bytes 196616 | tf_op jit(solution)/shard_map/ppermute | solution.py:764

commit v8 on v7

--- a/solution.py
+++ b/solution.py
@@ -187,7 +187,7 @@
         local = (xcell % depth_x * depth_y + ycell % depth_y) * zblocks + zblock % zblocks
         return (source, local)
 
-    own_source, own_local = locate(bin_cell)
+    own_source, _ = locate(bin_cell)
     own_row = own_source * capacity + rank_within(own_source)
     every = lax.all_gather(bin_cell, ("gx", "gy"), axis=0, tiled=True).reshape(sources, bins)
     all_source, all_local = locate(every)
@@ -201,7 +201,7 @@
     links = contacts.astype(jnp.float32)
     fluid = populations
     velocity = grain_velocity
-    for step in range(SUBSTEPS):
+    for _ in range(SUBSTEPS):
         density, speed = moments(fluid)
         flow = jnp.stack(speed + [density]).reshape(4, -1, grains)
         outgoing = jnp.take(flow, send_column, axis=1) * send_mask[None, :, None]
@@ -570,17 +570,16 @@
         aux_ref[2 + a, own] = drags[a]
 
 
-def contact_kernel(plan, in_ref, inner_ref, settled_ref, fixed_ref, state_ref, aux_ref, link_ref, packed_ref):
+def pack_kernel(plan, in_ref, inner_ref, packed_ref):
     window, _ = plan.place()
     even = lax.rem(window, 2) == 0
+    for s in range(plan.sources):
+        mine, sibling = half_tile(in_ref, s, plan.tiles, 0), inner_ref[s, :, plan.width :]
+        packed_ref[s] = jnp.concatenate([jnp.where(even, mine, sibling), jnp.where(even, sibling, mine)], axis=0)
+
+
+def contact_kernel(plan, packed_ref, settled_ref, fixed_ref, state_ref, aux_ref, link_ref):
     own = slice(0, plan.own)
-
-    def packed(s):
-        mine, sibling = half_tile(in_ref, s, plan.tiles, 0), inner_ref[s, :, plan.width :]
-        return jnp.concatenate([jnp.where(even, mine, sibling), jnp.where(even, sibling, mine)], axis=0)
-
-    for s in range(plan.sources):
-        packed_ref[s] = packed(s)
     contact_blocks(plan, lambda s: packed_ref[s], link_ref)
     drags = [aux_ref[2 + a, own] for a in range(3)]
     move_grains(lambda parts: touching(plan, parts, link_ref), state_ref, aux_ref, own, drags, True)
@@ -696,7 +695,7 @@
 
 def windows_body(plan, populations, grain_velocity, grain_volume, slots, contacts, bin_cell):
     group, bins, sources = plan.group, plan.bins, plan.sources
-    rows, columns, own = plan.rows, plan.columns, plan.own
+    rows, columns = plan.rows, plan.columns
     f32, bf16, i32 = jnp.float32, jnp.bfloat16, jnp.int32
     halo = plan.halo
 
@@ -741,8 +740,8 @@
         [((sources, halo, plan.width + LANES), f32), ((sources, halo, plan.width), f32)],
         (incoming,),
     )
+    outer = lax.ppermute(outer, every_axis, plan.swaps(1))
     inner = lax.ppermute(inner, every_axis, plan.swaps(0))
-    outer = lax.ppermute(outer, every_axis, plan.swaps(1))
     carried = [
         ((plan.fields, rows, columns), f32),
         ((19, rows, columns), f32),
@@ -755,13 +754,14 @@
         (incoming,),
         moments_and_forces,
     )
-    state, aux, link, packed = call(
+    (contacts_here,) = call(pack_kernel, [((sources, SUBLANES, LANES), f32)], (incoming, inner))
+    packed = lax.ppermute(contacts_here, every_axis, plan.swaps(1))
+    state, aux, link = call(
         contact_kernel,
-        [carried[0], carried[2], ((columns, LANES), bf16), ((sources, SUBLANES, LANES), f32)],
-        (incoming, inner, state, aux),
-        aliases={2: 0, 3: 1},
-    )
-    packed = lax.ppermute(packed, every_axis, plan.swaps(1))
+        [carried[0], carried[2], ((columns, LANES), bf16)],
+        (contacts_here, state, aux),
+        aliases={1: 0, 2: 1},
+    )
     state, _, aux, other_column = call(
         halo_kernel,
         carried + [((columns, columns), bf16)],

time: 47.6 us -> 47.6 us (level)
  waiting for transfers between devices: 2.6 us -> 1.83 us
  starting transfers between devices: 2.49 us -> 3.09 us
    ppermute x1, waiting for transfers between devices: 2.45 us -> 1.83 us  [windows_body(): outer = lax.ppermute(outer, every_axis, plan.swaps(1))]
    ppermute x1, starting transfers between devices: 0.82 us -> 1.42 us  [windows_body(): packed = lax.ppermute(contacts_here, every_axis, plan.swaps(1))]
    pallas_call x7 -> x8, Pallas kernels: 7.16 us -> 7.17 us  [call(): pl.pallas_call(lambda *refs: kernel(plan, *refs), out_shape=shapes, in_sp...]
  transfers between devices with their start and end apart: 3 -> 3, of which waited for: 2 -> 1; matrix products, arithmetic and copies ran while one was open for 0% -> 0% of each run, Pallas kernels for 4% -> 4%
where the time goes in v8:
time: 47.6 us; the launch traced here: 47.4 us
  blocking collectives  34.6 us (73%)
  Pallas kernels  7.17 us (15%)
  starting transfers between devices  3.09 us (6%)
  waiting for transfers between devices  1.83 us (4%)
  between operations  0.7 us (1%)
    all_to_all x1, blocking collectives, windows_body(): lax.all_to_all(outgoing, layer_axes, split_axis=0, concat_axis=0, tiled=T...  19.9 us
    all_to_all x1, blocking collectives, windows_body(): lax.all_to_all(back, layer_axes, split_axis=0, concat_axis=0, tiled=True)  14.7 us
    pallas_call x8, Pallas kernels, call(): pl.pallas_call(lambda *refs: kernel(plan, *refs), out_shape=shapes, in_sp...  7.17 us
    ppermute x1, waiting for transfers between devices, windows_body(): outer = lax.ppermute(outer, every_axis, plan.swaps(1))  1.83 us
    ppermute x1, starting transfers between devices, windows_body(): outer = lax.ppermute(outer, every_axis, plan.swaps(1))  1.49 us
    ppermute x1, starting transfers between devices, windows_body(): packed = lax.ppermute(contacts_here, every_axis, plan.swaps(1))  1.42 us
  transfers between devices with their start and end apart: 3, of which 1 were waited for; matrix products, arithmetic and copies ran while one was open for 0% of the time, Pallas kernels for 4%

profile of v8, /device:TPU:0, one launch (start us, length us, event | category | flops | bytes accessed | tf_op | source)
XLA Modules:
  0.0 47.4 jit_solution(16219776468879794475)
XLA Ops:
  0.6 1.4 %shard_map.77 = f32[16,4,1664]{2,1,0:T(4,128)S(1)} custom-call(f32[608,128]{1,0:T(8,128)} %bitcast.5, f32[96,128]{1,0:T(8,128)} %bitcast.6, f32[32,128]{1,0:T(8,128)} %refs_2_.1, s32[32,128]{1,0:T(8,128)} %refs_3_.1, s32[32,32]{1,0:T(8,128)} %refs_4_.1, s32[1,32]{1,0:T(1,128)} %bitcast.7), custom_call_target="tpu_custom_call" | custom-call | tf_op jit(solution)/shard_map/pallas_call | solution.py:706
  2.1 19.9 %all_to_all.10.refs_0_ = f32[16,4,1664]{2,1,0:T(4,128)S(1)} all-to-all(f32[16,4,1664]{2,1,0:T(4,128)S(1)} %shard_map.77), channel_id=1, replica_groups=mesh['gx'=4,'gy'=4,'gz'=2] {'gx','gy'}, dimensions={0} | all-to-all | bytes 851968 | tf_op jit(solution)/shard_map/all_to_all | solution.py:737
  22.0 0.1 shard_map.78
  22.1 0.2 collective-permute-start
  22.2 1.5 %collective-permute-start.1 = (f32[16,4,768]{2,1,0:T(4,128)S(1)}, f32[16,4,768]{2,1,0:T(4,128)S(1)}, u32[]{:S(2)}, u32[]{:S(2)}) collective-permute-start(f32[16,4,768]{2,1,0:T(4,128)S(1)} %get-tuple-element.24), channel_id=1, source_target_pairs={{2,4},{4,2},{6,14},{14,6},{12,10},{10,12},{8,16},{16,8},{18,20},{2... | collective-permute-start | bytes 589832 | tf_op jit(solution)/shard_map/ppermute | solution.py:743
  23.7 0.0 collective-permute-done.refs_1_.refs_4_
  23.8 1.4 %collective-permute-start.2 = (f32[16,8,128]{2,1,0:T(8,128)S(1)}, f32[16,8,128]{2,1,0:T(8,128)S(1)}, u32[]{:S(2)}, u32[]{:S(2)}) collective-permute-start(f32[16,8,128]{2,1,0:T(8,128)S(1)} %shard_map.79.refs_0_), channel_id=1, source_target_pairs={{2,4},{4,2},{6,14},{14,6},{12,10},{10,12},{8,16},{16,8},{18,20},{2... | collective-permute-start | bytes 196616 | tf_op jit(solution)/shard_map/ppermute | solution.py:758
  25.2 0.6 %shard_map.80 = (f32[24,16,512]{2,1,0:T(8,128)S(1)}, f32[19,16,512]{2,1,0:T(8,128)S(1)}, f32[5,16,512]{2,1,0:T(8,128)S(1)}, bf16[512,512]{1,0:T(8,128)(2,1)S(1)}) custom-call(f32[16,4,1664]{2,1,0:T(4,128)S(1)} %all_to_all.10.refs_0_), custom_call_target="tpu_custom_call" | custom-call | tf_op jit(solution)/shard_map/pallas_call | solution.py:706
  25.8 0.3 shard_map.81
  26.1 1.8 %collective-permute-done.1.refs_5_ = f32[16,4,768]{2,1,0:T(4,128)S(1)} collective-permute-done((f32[16,4,768]{2,1,0:T(4,128)S(1)}, f32[16,4,768]{2,1,0:T(4,128)S(1)}, u32[]{:S(2)}, u32[]{:S(2)}) %collective-permute-start.1) | collective-permute-done | bytes 196640 | tf_op jit(solution)/shard_map/ppermute | solution.py:743
  27.9 0.9 %shard_map.82 = (f32[24,16,512]{2,1,0:T(8,128)S(1)}, f32[19,16,512]{2,1,0:T(8,128)S(1)}, f32[5,16,512]{2,1,0:T(8,128)S(1)}, bf16[512,512]{1,0:T(8,128)(2,1)S(1)}) custom-call(f32[24,16,512]{2,1,0:T(8,128)S(1)} %get-tuple-element.20.refs_0_, f32[19,16,512]{2,1,0:T(8,128)S(1)} %get-tuple-element.21.refs_1_, ...), custom_call_target="tpu_custom_call", output_to_operand_aliasing={{0}: (0, {}), {1}: (1, {}), {2}: (2, {})} | custom-call | tf_op jit(solution)/shard_map/pallas_call | solution.py:706
  28.8 0.0 collective-permute-done.2.refs_5_
  28.9 2.8 %shard_map.83 = (f32[16,4,1408]{2,1,0:T(4,128)S(1)}, f32[24,16,512]{2,1,0:T(8,128)S(1)}, f32[5,16,512]{2,1,0:T(8,128)S(1)}) custom-call(f32[24,16,512]{2,1,0:T(8,128)S(1)} %get-tuple-element.25.refs_0_, f32[5,16,512]{2,1,0:T(8,128)S(1)} %get-tuple-element.26.refs_1_, ...), custom_call_target="tpu_custom_call", output_to_operand_aliasing={{1}: (0, {}), {2}: (1, {})} | custom-call | tf_op jit(solution)/shard_map/pallas_call | solution.py:706
  31.7 14.7 %all_to_all.11.refs_0_ = f32[16,4,1408]{2,1,0:T(4,128)S(1)} all-to-all(f32[16,4,1408]{2,1,0:T(4,128)S(1)} %get-tuple-element.29), channel_id=1, replica_groups=mesh['gx'=4,'gy'=4,'gz'=2] {'gx','gy'}, dimensions={0} | all-to-all | bytes 720896 | tf_op jit(solution)/shard_map/all_to_all | solution.py:783
  46.4 1.0 %shard_map.84 = (f32[608,128]{1,0:T(8,128)}, f32[96,128]{1,0:T(8,128)}) custom-call(f32[16,4,1408]{2,1,0:T(4,128)S(1)} %all_to_all.11.refs_0_), custom_call_target="tpu_custom_call" | custom-call | tf_op jit(solution)/shard_map/pallas_call | solution.py:706
  (1 shorter events, 0.0 us)
Async XLA Ops:
  22.1 1.7 %collective-permute-start = (f32[16,4,896]{2,1,0:T(4,128)S(1)}, f32[16,4,896]{2,1,0:T(4,128)S(1)}, u32[]{:S(2)}, u32[]{:S(2)}) collective-permute-start(f32[16,4,896]{2,1,0:T(4,128)S(1)} %get-tuple-element.17), channel_id=1, source_target_pairs={{0,2},{2,0},{4,6},{6,4},{14,12},{12,14},{10,8},{8,10},{16,18},{18,... | collective-permute-start | bytes 688136 | tf_op jit(solution)/shard_map/ppermute | solution.py:744
  22.2 5.7 %collective-permute-start.1 = (f32[16,4,768]{2,1,0:T(4,128)S(1)}, f32[16,4,768]{2,1,0:T(4,128)S(1)}, u32[]{:S(2)}, u32[]{:S(2)}) collective-permute-start(f32[16,4,768]{2,1,0:T(4,128)S(1)} %get-tuple-element.24), channel_id=1, source_target_pairs={{2,4},{4,2},{6,14},{14,6},{12,10},{10,12},{8,16},{16,8},{18,20},{2... | collective-permute-start | bytes 589832 | tf_op jit(solution)/shard_map/ppermute | solution.py:743
  23.8 5.1 %collective-permute-start.2 = (f32[16,8,128]{2,1,0:T(8,128)S(1)}, f32[16,8,128]{2,1,0:T(8,128)S(1)}, u32[]{:S(2)}, u32[]{:S(2)}) collective-permute-start(f32[16,8,128]{2,1,0:T(8,128)S(1)} %shard_map.79.refs_0_), channel_id=1, source_target_pairs={{2,4},{4,2},{6,14},{14,6},{12,10},{10,12},{8,16},{16,8},{18,20},{2... | collective-permute-start | bytes 196616 | tf_op jit(solution)/shard_map/ppermute | solution.py:758
